TPU v7x, 32 devices: a whole 2x2x4 slice. The times are simulated.
32 devices in a mesh: gx: 2 (over core), yz: 16 (over z, y, x).
Axes of the slice: x: 2, y: 2, z: 4, core: 2. Of those that a mesh axis runs over, the one named last changes fastest.
Arguments:
- features_in: bfloat16 [16, 32, 24, 144], P('yz', None, 'gx'), may hold values from -6 to 6
- encode_fine_first: bfloat16 [32, 864], replicated, may hold values from -0.3125 to 0.3125
- encode_fine_second: bfloat16 [32, 864], replicated, may hold values from -0.3125 to 0.3125
- reduce_fine: bfloat16 [64, 256], replicated, may hold values from -0.5 to 0.5
- encode_middle_first: bfloat16 [64, 1728], replicated, may hold values from -0.21875 to 0.21875
- encode_middle_second: bfloat16 [64, 1728], replicated, may hold values from -0.21875 to 0.21875
- reduce_middle: bfloat16 [256, 512], replicated, may hold values from -0.375 to 0.375
- bottom_first: bfloat16 [1024, 1728], P('yz'), may hold values from -0.109375 to 0.109375
- bottom_second: bfloat16 [1024, 1728], P('yz'), may hold values from -0.109375 to 0.109375
- expand_middle: bfloat16 [256, 512], replicated, may hold values from -0.5 to 0.5
- decode_middle_first: bfloat16 [64, 1728], replicated, may hold values from -0.21875 to 0.21875
- decode_middle_second: bfloat16 [64, 1728], replicated, may hold values from -0.21875 to 0.21875
- expand_fine: bfloat16 [64, 256], replicated, may hold values from -1 to 1
- decode_fine_first: bfloat16 [32, 864], replicated, may hold values from -0.3125 to 0.3125
- decode_fine_second: bfloat16 [32, 864], replicated, may hold values from -0.3125 to 0.3125
Outputs:
- features_out: bfloat16 [16, 32, 24, 144], P('yz', None, 'gx')
All inputs are finite; a program needn't handle non-finite values.
Results may differ from a plain program's by a relative error of at most 0.023.
Values may be sent and summed in bfloat16 or wider, within the bound.
No kernel may reach another device: no remote copies, remote signals or barrier semaphores. Data moves between devices by JAX's collectives and lax.ppermute only.
A program may use at most 128 MiB of HBM per device.

v0:
```python
import math

import jax
import jax.numpy as jnp
from jax import lax
from jax.experimental import pallas as pl
from jax.experimental.pallas import tpu as pltpu
from jax.sharding import PartitionSpec as P

BF = jnp.bfloat16
F32 = jnp.float32
LANES = 128
DEPTH = 256


def dot(a, b):
    return lax.dot_general(a, b, (((1,), (0,)), ((), ())), preferred_element_type=F32)


def lane_group(rows, width):
    return lax.broadcasted_iota(jnp.int32, (rows, LANES), 1) // width


def transposed(flat, weight):
    columns = weight.shape[1]
    copies = jnp.concatenate([weight.astype(F32)] * (LANES // weight.shape[0]), axis=0)
    for start in range(0, columns, LANES):
        stop = min(start + LANES, columns)
        flat[start:stop, :] = copies[:, start:stop].T


def blocks(taps, cells, wide_in, wide_out, target):
    group = lane_group(wide_in, wide_out)
    for cell in range(cells):
        value = jnp.zeros((wide_in, LANES), F32)
        for k, tap in enumerate(taps):
            out = target(cell, k)
            if out is not None and 0 <= out < LANES // wide_out:
                value = jnp.where(group == out, tap, value)
        yield cell * wide_in, value.astype(BF)


def conv_table(table, flat, weight, channels):
    transposed(flat, weight)
    for dy in range(3):
        for dx in range(3):
            taps = [flat[pl.ds(9 * dx + 3 * dy + dz, channels, 27), :] for dz in range(3)]
            for row, block in blocks(
                taps, DEPTH // channels, channels, channels, lambda z, k: z - k
            ):
                table[3 * dy + dx, row : row + channels, :] = block


def shrink_table(table, flat, weight, channels, offset):
    transposed(flat, weight)

    def target(z, k):
        return (z - offset - k) // 2 if (z - offset - k) % 2 == 0 else None

    for dx in range(2):
        for dy in range(2):
            taps = [flat[pl.ds(4 * dx + 2 * dy + dz, channels, 8), :] for dz in range(2)]
            for row, block in blocks(
                taps, DEPTH // channels, channels, weight.shape[0], target
            ):
                row += DEPTH * dy
                table[row : row + channels, LANES * dx : LANES * (dx + 1)] = block


def picked(weight, dx, dy, channels):
    rows = weight.shape[1]
    lane = lax.broadcasted_iota(jnp.int32, (rows, LANES), 1) % (2 * channels)
    row = lax.broadcasted_iota(jnp.int32, (rows, LANES), 0)
    wanted = 8 * (lane % channels) + 4 * dx + 2 * dy + lane // channels
    return dot(weight, (row == wanted).astype(BF))


def stage(wide, shifted, layers, rows, first, width, base=0):
    for y in range(layers):
        for d in range(3):
            shifted[d, y * rows : (y + 1) * rows, :width] = wide[
                base + y, first + d : first + d + rows, :width
            ].astype(BF)


def convolve(shifted, table, layers, rows, tile, depth=DEPTH):
    height = layers * rows
    start = tile * LANES
    left = jnp.concatenate(
        [
            shifted[dx, dy * rows : dy * rows + height, start : start + depth]
            for dy in range(3)
            for dx in range(3)
        ],
        axis=1,
    )
    return dot(left, table[:, :depth, :].reshape(9 * depth, LANES))


def rounded_relu(value):
    return jnp.maximum(value, 0.0).astype(BF)


def span_of(tile):
    return slice(tile * LANES, (tile + 1) * LANES)


def fine_encoder(
    low, mid, high, first, second, reduce, skip, small, wide, s1, s2, table, flat, down, halves, flats
):
    layers, width = mid.shape[0], mid.shape[2]
    start = 0
    for piece in (low, mid, high):
        wide[:, start : start + piece.shape[1], :] = piece[...].astype(F32)
        start += piece.shape[1]
    stage(wide, s1, layers, 32, 0, width)
    conv_table(table, flat, first[...], 32)
    inner = layers - 2
    tiles = width // LANES
    for tile in range(tiles):
        depth = DEPTH if tile + 1 < tiles else LANES
        value = rounded_relu(convolve(s1, table, inner, 32, tile, depth))
        wide[:inner, :32, span_of(tile)] = value.astype(F32).reshape(inner, 32, LANES)
    stage(wide, s2, inner, 16, 0, width)
    conv_table(table, flat, second[...], 32)
    kept = inner - 2
    for tile in range(tiles - 1):
        value = rounded_relu(convolve(s2, table, kept, 16, tile))
        skip[:, :, span_of(tile)] = value.reshape(kept, 16, LANES)
    shrink_table(down, flat, reduce[...], 32, 2)
    count = (kept - 4) // 2
    for tile in range(count // 2):
        left = jnp.concatenate(
            [
                jnp.concatenate(
                    [
                        skip[2 + 2 * y + dy, :, tile * LANES : tile * LANES + DEPTH]
                        for y in range(count)
                    ],
                    axis=0,
                )
                for dy in range(2)
            ],
            axis=1,
        )
        total = dot(left, down[...])
        halves[0] = total[:, :LANES]
        halves[1] = total[:, LANES:]
        for y in range(count):
            value = halves[0, pl.ds(16 * y + 2, count, 2), :]
            value = value + halves[1, pl.ds(16 * y + 3, count, 2), :]
            flats[count * y : count * (y + 1), span_of(tile)] = value
    result = flats[...].astype(BF)
    for copy in range(small.shape[0]):
        small[copy] = result


def wrap_rows(wide, layers, count):
    wide[1 : layers + 1, 7:8, :] = wide[1 : layers + 1, 7 + count : 8 + count, :]
    wide[1 : layers + 1, 8 + count : 9 + count, :] = wide[1 : layers + 1, 8:9, :]
    wide[0:1] = wide[layers : layers + 1]
    wide[layers + 1 : layers + 2] = wide[1:2]


def middle(
    where,
    own,
    other,
    first,
    second,
    reduce,
    turned,
    swapped,
    window,
    partial,
    wide,
    s,
    table,
    flat,
    down,
    whole,
    halves,
    flats,
):
    across = math.isqrt(own.shape[0])
    side = math.isqrt(own.shape[1])
    cells = side * across
    lanes = side * 64
    span = cells * 64
    row, column = where[0], where[1]
    for i in range(across):
        for place, j in enumerate([across - 1] + list(range(across))):
            start = place * lanes
            size = min(lanes, span + LANES - start)
            for part, gathered in enumerate((own, other)):
                block = gathered[i * across + j, :, :size].astype(F32)
                for y in range(side):
                    wide[
                        1 + side * i + y,
                        8 + side * part : 8 + side * (part + 1),
                        start : start + size,
                    ] = block[side * y : side * (y + 1)]
    wrap_rows(wide, cells, 2 * side)
    stage(wide, s, cells + 2, 16, 7, span + LANES)
    conv_table(table, flat, first[...], 64)
    for tile in range(span // LANES):
        value = rounded_relu(convolve(s, table, cells, 16, tile))
        wide[1 : cells + 1, 8:24, span_of(tile)] = value.astype(F32).reshape(cells, 16, LANES)
    wide[:, :, span : span + LANES] = wide[:, :, 0:LANES]
    wrap_rows(wide, cells, 2 * side)
    stage(wide, s, cells + 2, 16, 7, span + LANES)
    conv_table(table, flat, second[...], 64)
    for tile in range(span // LANES):
        value = rounded_relu(convolve(s, table, cells, 16, tile))
        whole[3 : cells + 3, :, span_of(tile)] = value.reshape(cells, 16, LANES)
    whole[0:3] = whole[cells : cells + 3]
    whole[cells + 3 : cells + 6] = whole[3:6]
    whole[:, :, span : span + 512] = whole[:, :, 0:512]
    window[...] = whole[
        pl.ds(row * side, window.shape[0]),
        :,
        pl.ds(pl.multiple_of(column * lanes, LANES), window.shape[2]),
    ]
    half = cells // 2
    shrunk = half * 64
    quarter = reduce[pl.ds(pl.multiple_of(column * 64, 64), 64), :]
    shrink_table(down, flat, quarter, 64, 0)
    for tile in range(shrunk // LANES):
        left = jnp.concatenate(
            [
                jnp.concatenate(
                    [
                        whole[3 + 2 * y + dy, :, tile * DEPTH : (tile + 1) * DEPTH]
                        for y in range(half)
                    ],
                    axis=0,
                )
                for dy in range(2)
            ],
            axis=1,
        )
        total = dot(left, down[...])
        halves[0] = total[:, :LANES]
        halves[1] = total[:, LANES:]
        for y in range(half):
            value = halves[0, pl.ds(16 * y, side, 2), :]
            value = value + halves[1, pl.ds(16 * y + 1, side, 2), :]
            wide[1 + y, 8 : 8 + side, span_of(tile)] = value.astype(BF).astype(F32)
    wide[1 : half + 1, 8 : 8 + side, shrunk : shrunk + LANES] = wide[
        1 : half + 1, 8 : 8 + side, 0:LANES
    ]
    wrap_rows(wide, half, side)
    stage(wide, s, half + 2, 16, 7, shrunk + LANES)
    mine, theirs = turned[...].astype(F32), swapped[...].astype(F32)
    is_first = where[2] == 0
    stored = jnp.concatenate(
        [jnp.where(is_first, mine, theirs), jnp.where(is_first, theirs, mine)], axis=0
    )
    conv_table(table, flat, stored, 64)
    for tile in range(shrunk // LANES):
        value = convolve(s, table, half, 16, tile)
        for y in range(half):
            flats[side * y : side * (y + 1), span_of(tile)] = value[16 * y : 16 * y + side]
    partial[...] = flats[...].astype(BF)


def bottom(*refs):
    *pieces, weight, out, wide, s, table, flat, whole, flats = refs
    span = pieces[0].shape[1]
    cells = span // 64
    side = cells // 2
    across = math.isqrt(out.shape[0])
    total = 0.0
    for piece in pieces:
        total = total + piece[...].astype(F32)
    total = jnp.maximum(total, 0.0).astype(BF).astype(F32)
    for y in range(cells):
        wide[1 + y, 8 : 8 + side, :span] = total[side * y : side * (y + 1)]
    wide[1 : cells + 1, 8 : 8 + side, span : span + LANES] = wide[
        1 : cells + 1, 8 : 8 + side, 0:LANES
    ]
    wrap_rows(wide, cells, side)
    stage(wide, s, cells + 2, 16, 7, span + LANES)
    conv_table(table, flat, weight[...], 64)
    for tile in range(span // LANES):
        value = convolve(s, table, cells, 16, tile).reshape(cells, 16, LANES)
        whole[2 : cells + 2, :, span_of(tile + 1)] = value[:, :8]
    whole[0:2] = whole[cells : cells + 2]
    whole[cells + 2 : cells + 5] = whole[2:5]
    whole[:, :, 0:LANES] = whole[:, :, span : span + LANES]
    whole[:, :, span + LANES : span + 512] = whole[:, :, LANES:512]
    block = cells // across
    kept = side // 2
    layers = out.shape[1] // kept
    for i in range(across):
        for j in range(across):
            start = (block * j - block * j % 2) * 64
            for y in range(layers):
                flats[kept * y : kept * (y + 1), :] = whole[
                    block * i + y, 0:kept, start : start + out.shape[2]
                ]
            out[i * across + j] = flats[...].astype(BF)


def decoder(
    where,
    near,
    far,
    window,
    skip,
    up,
    m1,
    m2,
    up_fine,
    f1,
    f2,
    out,
    wide,
    s,
    table,
    flat,
    lift,
    columns,
    spread,
):
    across = math.isqrt(near.shape[0])
    kept = window.shape[0] // 4
    layers = near.shape[1] // kept
    odd = where[1] % 2
    for dx in range(2):
        for dy in range(2):
            pair = picked(up[...], dx, dy, 64)
            blank = jnp.zeros((64, LANES), BF)
            for group in range(across):
                value = pair[64 * group : 64 * (group + 1)]
                for cell in range(4):
                    for half in range(2):
                        block = blank
                        if cell - half in (0, 1):
                            block = jnp.where(odd == cell - half, value, 0.0).astype(BF)
                        row = DEPTH * group + 64 * cell
                        lift[2 * dx + dy, row : row + 64, span_of(half)] = block
    groups = []
    for group in range(across):
        for part, parts in enumerate((near, far)):
            total = 0.0
            for k in range(across):
                total = total + parts[k * across + group].astype(F32)
            total = jnp.maximum(total, 0.0)
            for y in range(layers):
                columns[y, kept * part : kept * (part + 1), :512] = total[
                    kept * y : kept * (y + 1)
                ]
        groups.append(
            jnp.concatenate(
                [
                    columns[:layers, :, :512].astype(BF).reshape(layers * 16, 512),
                    jnp.zeros((layers * 16, LANES), BF),
                ],
                axis=1,
            )
        )
    for tile in range(4):
        left = jnp.concatenate(
            [g[:, tile * LANES : tile * LANES + DEPTH] for g in groups], axis=1
        )
        for dx in range(2):
            for dy in range(2):
                value = dot(left, lift[2 * dx + dy])
                for y in range(layers):
                    for half in range(2):
                        spread[2 * tile + half, 2 * y + dy, pl.ds(8 + dx, 2 * kept, 2), :] = value[
                            16 * y : 16 * y + 2 * kept, span_of(half)
                        ]
    count = window.shape[0]
    for tile in range(window.shape[2] // LANES):
        total = spread[tile, 1 : count + 1, 8:24, :] + window[:, :, span_of(tile)].astype(F32)
        wide[:count, 8:24, span_of(tile)] = total.astype(BF).astype(F32)
    ends = 8 + count
    wide[:, 7:8, :] = wide[:, ends - 1 : ends, :]
    wide[:, ends : ends + 1, :] = wide[:, 8:9, :]
    stage(wide, s, count, 16, 7, window.shape[2])
    conv_table(table, flat, m1[...], 64)
    count = count - 2
    for tile in range(6):
        value = rounded_relu(convolve(s, table, count, 16, tile))
        wide[:count, 8:24, span_of(tile)] = value.astype(F32).reshape(count, 16, LANES)
    wide[:, 7:8, :] = wide[:, ends - 1 : ends, :]
    wide[:, ends : ends + 1, :] = wide[:, 8:9, :]
    stage(wide, s, count, 16, 7, 6 * LANES)
    conv_table(table, flat, m2[...], 64)
    count = count - 2
    risen = jnp.concatenate(
        [rounded_relu(convolve(s, table, count, 16, tile)) for tile in range(5)], axis=1
    )
    second_half = lane_group(64, 64) == 1
    zeros = jnp.zeros((64, LANES), F32)
    for dx in range(2):
        for dy in range(2):
            value = picked(up_fine[...], dx, dy, 32)
            for cell, block in enumerate(
                (
                    zeros,
                    jnp.where(second_half, 0.0, value),
                    jnp.where(second_half, value, 0.0),
                    zeros,
                )
            ):
                lift[0, 64 * cell : 64 * (cell + 1), span_of(0)] = block.astype(BF)
            for tile in range(4):
                left = risen[:, tile * LANES : tile * LANES + DEPTH]
                rise = dot(left, lift[0, :DEPTH, :LANES])
                for y in range(count):
                    part = rise[16 * y : 16 * (y + 1)]
                    spread[tile, 2 * y + dy, pl.ds(2 + dx, 7, 2), :] = part[0:7]
                    spread[tile, 2 * y + dy, dx : dx + 1, :] = part[ends - 9 : ends - 8]
    count = 2 * count
    for tile in range(skip.shape[2] // LANES):
        total = spread[tile, :count, 0:16, :] + skip[:, :, span_of(tile)].astype(F32)
        wide[:count, 0:16, span_of(tile)] = total.astype(BF).astype(F32)
    stage(wide, s, count, 16, 0, 4 * LANES)
    conv_table(table, flat, f1[...], 32)
    count = count - 2
    for tile in range(4):
        value = rounded_relu(convolve(s, table, count, 16, tile, DEPTH if tile < 3 else LANES))
        wide[:count, 0:16, span_of(tile)] = value.astype(F32).reshape(count, 16, LANES)
    stage(wide, s, count, 16, 0, 4 * LANES)
    conv_table(table, flat, f2[...], 32)
    count = count - 2
    for tile in range(3):
        value = rounded_relu(convolve(s, table, count, 16, tile))
        out[:, :, span_of(tile)] = value.reshape(count, 16, LANES)


def call(kernel, outs, scratch, *args, scalars=0):
    spaces = [pltpu.SMEM] * scalars + [pltpu.VMEM] * (len(args) - scalars)
    return pl.pallas_call(
        kernel,
        out_shape=outs,
        in_specs=[pl.BlockSpec(memory_space=space) for space in spaces],
        out_specs=jax.tree.map(lambda _: pl.BlockSpec(memory_space=pltpu.VMEM), outs),
        scratch_shapes=scratch,
        name=kernel.__name__,
    )(*args)


def exchange(head, tail, axis, route):
    ahead = [(source, route(source, 1)) for source in range(lax.axis_size(axis))]
    back = [(source, route(source, -1)) for source in range(lax.axis_size(axis))]
    return lax.ppermute(tail, axis, ahead), lax.ppermute(head, axis, back)


def gathered_body(
    features_in,
    encode_fine_first,
    encode_fine_second,
    reduce_fine,
    encode_middle_first,
    encode_middle_second,
    reduce_middle,
    bottom_first,
    bottom_second,
    expand_middle,
    decode_middle_first,
    decode_middle_second,
    expand_fine,
    decode_fine_first,
    decode_fine_second,
):
    devices = lax.axis_size("yz")
    across = math.isqrt(devices)
    place = lax.axis_index("yz")
    where = jnp.stack([place // across, place % across, lax.axis_index("gx")]).astype(jnp.int32)
    fine, ext = features_in.shape[1], features_in.shape[2]
    mid = encode_middle_first.shape[0]
    halo = 4

    def around(source, step):
        return (source + step) % lax.axis_size("gx")

    def along_y(source, step):
        return (source + step * across) % devices

    def along_z(source, step):
        return source // across * across + (source % across + step) % across

    cores = lax.axis_size("gx")
    size = bottom_first.shape[0] // cores
    mine = lax.dynamic_slice_in_dim(bottom_first, lax.axis_index("gx") * size, size, 0)
    turned = lax.ppermute(
        mine, "yz", [(s, s % across * across + s // across) for s in range(devices)]
    )

    cells = features_in.reshape(fine, ext, ext, ext).transpose(2, 1, 3, 0)
    cells = cells.reshape(ext, ext, ext * fine)
    low, high = exchange(cells[:halo], cells[ext - halo :], "yz", along_y)
    cells = jnp.concatenate([low, cells, high], axis=0)
    edge = halo * fine
    low, high = exchange(cells[:, :, :edge], cells[:, :, -edge:], "yz", along_z)
    cells = jnp.concatenate([low, cells, high], axis=2)
    low, high = exchange(cells[:, :halo], cells[:, ext - halo :], "gx", around)

    seen = ext + 2 * halo
    side = ext // 2
    flat = pltpu.VMEM((27 * mid, LANES), F32)
    table = pltpu.VMEM((9, DEPTH, LANES), BF)
    down = pltpu.VMEM((2 * DEPTH, 2 * LANES), BF)
    skip, small = call(
        fine_encoder,
        (
            jax.ShapeDtypeStruct((ext + 4, ext + 4, (ext + 4) * fine), BF),
            jax.ShapeDtypeStruct((devices, side * side, side * mid), BF),
        ),
        [
            pltpu.VMEM((seen, 40, seen * fine), F32),
            pltpu.VMEM((3, seen * 32, seen * fine), BF),
            pltpu.VMEM((3, (seen - 2) * 16, seen * fine), BF),
            table,
            flat,
            down,
            pltpu.VMEM((2, side * 16, LANES), F32),
            pltpu.VMEM((side * side, side * mid), F32),
        ],
        low,
        cells,
        high,
        encode_fine_first,
        encode_fine_second,
        reduce_fine,
    )

    small, turned = lax.optimization_barrier((small, turned))
    swap = [(s, around(s, 1)) for s in range(cores)]
    own = lax.all_to_all(small, "yz", 0, 0)
    other = lax.ppermute(own, "gx", swap)
    swapped = lax.ppermute(turned, "gx", swap)

    total = side * across
    half = total // 2
    window, partial = call(
        middle,
        (
            jax.ShapeDtypeStruct((12, 16, 14 * mid), BF),
            jax.ShapeDtypeStruct((half * side, half * mid), BF),
        ),
        [
            pltpu.VMEM((total + 2, 32, total * mid + LANES), F32),
            pltpu.VMEM((3, (total + 2) * 16, total * mid + LANES), BF),
            table,
            flat,
            down,
            pltpu.VMEM((total + 6, 16, total * mid + 512), BF),
            pltpu.VMEM((2, half * 16, LANES), F32),
            pltpu.VMEM((half * side, half * mid), F32),
        ],
        where,
        own,
        other,
        encode_middle_first,
        encode_middle_second,
        reduce_middle,
        turned,
        swapped,
        scalars=1,
    )

    pieces = [partial] + [
        lax.ppermute(partial, "yz", [(s, s ^ turn) for s in range(devices)])
        for turn in range(1, across)
    ]
    sent = call(
        bottom,
        jax.ShapeDtypeStruct((devices, 7 * side // 2, 8 * mid), BF),
        [
            pltpu.VMEM((half + 2, 32, half * mid + LANES), F32),
            pltpu.VMEM((3, (half + 2) * 16, half * mid + LANES), BF),
            table,
            flat,
            pltpu.VMEM((half + 5, 8, half * mid + 512), F32),
            pltpu.VMEM((7 * side // 2, 8 * mid), F32),
        ],
        *pieces,
        bottom_second,
    )
    near = lax.all_to_all(sent, "yz", 0, 0)
    far = lax.ppermute(near, "gx", swap)

    risen = call(
        decoder,
        jax.ShapeDtypeStruct((ext, 16, ext * fine), BF),
        [
            pltpu.VMEM((16, 32, 1024), F32),
            pltpu.VMEM((3, 256, 1024), BF),
            table,
            flat,
            pltpu.VMEM((4, across * DEPTH, 2 * LANES), BF),
            pltpu.VMEM((8, 16, 512), F32),
            pltpu.VMEM((8, 16, 32, LANES), F32),
        ],
        where,
        near,
        far,
        window,
        skip,
        expand_middle,
        decode_middle_first,
        decode_middle_second,
        expand_fine,
        decode_fine_first,
        decode_fine_second,
        scalars=1,
    )
    risen = risen[:, :ext].reshape(ext, ext, ext, fine).transpose(3, 1, 0, 2)
    return risen.reshape(1, fine, ext, ext * ext)


def with_halo(cells, sides, width):
    for axis, dim in sides:
        count = lax.axis_size(axis)
        head = lax.slice_in_dim(cells, 0, width, axis=dim)
        tail = lax.slice_in_dim(cells, cells.shape[dim] - width, cells.shape[dim], axis=dim)
        cells = jnp.concatenate(
            [
                lax.ppermute(tail, axis, [(i, (i + 1) % count) for i in range(count)]),
                cells,
                lax.ppermute(head, axis, [((i + 1) % count, i) for i in range(count)]),
            ],
            axis=dim,
        )
    return cells


def shortened(x):
    return jax.tree.map(lambda a: a.astype(jnp.bfloat16) if a.dtype == jnp.float32 else a, x)


def from_behind(block, axis, distance):
    devices = range(lax.axis_size(axis))
    route = [((i - distance) % len(devices), i) for i in devices]
    return lax.ppermute(block, axis, route)


def conv_taps(padded, weight, width_in):
    kernel = weight.reshape(weight.shape[0], width_in, 3, 3, 3)
    return lax.conv_general_dilated(
        padded[None],
        kernel,
        (1, 1, 1),
        "VALID",
        dimension_numbers=("NCDHW", "OIDHW", "NCDHW"),
        preferred_element_type=jnp.float32,
    )[0]


def rectify(running):
    return jnp.maximum(running, 0.0).astype(jnp.bfloat16)


def shrink(region, weight):
    kernel = weight.reshape(weight.shape[0], region.shape[0], 2, 2, 2)
    result = lax.conv_general_dilated(
        region[None],
        kernel,
        (2, 2, 2),
        "VALID",
        dimension_numbers=("NCDHW", "OIDHW", "NCDHW"),
        preferred_element_type=jnp.float32,
    )[0]
    return result.astype(jnp.bfloat16)


def expand(region, weight, skipped):
    width_in, extent_x, extent_y, extent_z = region.shape
    width_out = weight.shape[1] // 8
    columns = lax.dot_general(
        weight,
        region.reshape(width_in, -1),
        (((0,), (0,)), ((), ())),
        preferred_element_type=jnp.float32,
    )
    spread = columns.reshape(width_out, 2, 2, 2, extent_x, extent_y, extent_z).transpose(
        0, 4, 1, 5, 2, 6, 3
    )
    spread = spread.reshape(width_out, 2 * extent_x, 2 * extent_y, 2 * extent_z)
    return (spread + skipped.astype(jnp.float32)).astype(jnp.bfloat16)


def x_margins(region):
    return with_halo(region, (("gx", 1),), 1)


def from_peer(plane, offset):
    return from_behind(shortened(plane), "yz", offset).astype(plane.dtype)


def pad_block(region, across):
    extended = x_margins(region)
    below_face = from_peer(extended[:, :, -1:, :], across)
    above_face = from_peer(extended[:, :, :1, :], -across)
    extended = jnp.concatenate([below_face, extended, above_face], axis=2)
    column = lax.axis_index("yz") % across
    last_plane = extended[:, :, :, -1:]
    first_plane = extended[:, :, :, :1]
    behind = jnp.where(column == 0, from_peer(last_plane, 1 - across), from_peer(last_plane, 1))
    ahead = jnp.where(
        column == across - 1, from_peer(first_plane, across - 1), from_peer(first_plane, -1)
    )
    return jnp.concatenate([behind, extended, ahead], axis=3)


def conv_layer(region, weight, across):
    return rectify(conv_taps(pad_block(region, across), weight, region.shape[0]))


def assemble(stored):
    width_out = stored.shape[0] // 4
    return (
        stored.reshape(4, width_out, stored.shape[1])
        .transpose(1, 0, 2)
        .reshape(width_out, 4 * stored.shape[1])
    )


def bottom_layer(region, weight, across):
    width_in = region.shape[0]
    padded = pad_block(region, across)
    gathered = lax.all_gather(weight, "yz", axis=0, tiled=True)
    return rectify(conv_taps(padded, assemble(gathered), width_in))


def body(
    features_in,
    encode_fine_first,
    encode_fine_second,
    reduce_fine,
    encode_middle_first,
    encode_middle_second,
    reduce_middle,
    bottom_first,
    bottom_second,
    expand_middle,
    decode_middle_first,
    decode_middle_second,
    expand_fine,
    decode_fine_first,
    decode_fine_second,
):
    across = math.isqrt(lax.axis_size("yz"))
    width_fine, extent = (features_in.shape[1], features_in.shape[2])
    region = features_in.reshape(width_fine, extent, extent, extent)
    fine_skip = conv_layer(
        conv_layer(region, encode_fine_first, across), encode_fine_second, across
    )
    middle = shrink(fine_skip, reduce_fine)
    middle_skip = conv_layer(
        conv_layer(middle, encode_middle_first, across), encode_middle_second, across
    )
    bottom = shrink(middle_skip, reduce_middle)
    bottom = bottom_layer(bottom_layer(bottom, bottom_first, across), bottom_second, across)
    rising = expand(bottom, expand_middle, middle_skip)
    rising = conv_layer(
        conv_layer(rising, decode_middle_first, across), decode_middle_second, across
    )
    rising = expand(rising, expand_fine, fine_skip)
    rising = conv_layer(conv_layer(rising, decode_fine_first, across), decode_fine_second, across)
    return rising.reshape(1, width_fine, extent, extent * extent)


def solution(mesh):
    placed = (
        P("yz", None, "gx", None),
        P(),
        P(),
        P(),
        P(),
        P(),
        P(),
        P("yz", None),
        P("yz", None),
        P(),
        P(),
        P(),
        P(),
        P(),
        P(),
    )

    def chosen(*args):
        across = math.isqrt(lax.axis_size("yz"))
        stored, channels = args[7].shape[0], args[4].shape[0]
        gathered = lax.axis_size("gx") == 2 and stored == channels
        gathered = gathered and across == 4 and across * channels == args[6].shape[0]
        return (gathered_body if gathered else body)(*args)

    return jax.shard_map(
        chosen, mesh=mesh, in_specs=placed, out_specs=P("yz", None, "gx", None), check_vma=False
    )
```

profile of v0, /device:TPU:0, one launch (start us, length us, event | category | flops | bytes accessed | tf_op | source)
XLA Modules:
  0.0 112.6 jit_solution(12353480285988032175)
XLA Ops:
  0.0 0.0 copy-start
  0.0 1.2 %copy.18 = bf16[1,32,12,144]{1,3,2,0:T(8,128)(2,1)S(1)} copy(bf16[1,32,12,144]{3,1,2,0:T(8,128)(2,1)} %param.15) | data formatting | bytes 221184 | tf_op args[0]
  1.2 0.1 reshape.14
  1.4 0.2 slice.28
  1.6 3.1 %collective-permute-start = (bf16[4,12,384]{2,1,0:T(8,128)(2,1)S(1)}, bf16[4,12,384]{2,1,0:T(8,128)(2,1)S(1)}, u32[]{:S(2)}, u32[]{:S(2)}) collective-permute-start(bf16[4,12,384]{2,1,0:T(8,128)(2,1)S(1)} %copy.19), channel_id=1, source_target_pairs={{0,4},{1,5},{2,6},{3,7},{4,8},{5,9},{6,10},{7,11},{8,12},{9,13},{1... | collective-permute-start | bytes 110600 | tf_op jit(solution)/shard_map/ppermute | solution.py:450
  4.7 0.2 slice.30
  4.9 2.1 %collective-permute-start.1 = (bf16[4,12,384]{2,1,0:T(8,128)(2,1)S(1)}, bf16[4,12,384]{2,1,0:T(8,128)(2,1)S(1)}, u32[]{:S(2)}, u32[]{:S(2)}) collective-permute-start(bf16[4,12,384]{2,1,0:T(8,128)(2,1)S(1)} %copy.21), channel_id=1, source_target_pairs={{0,12},{1,13},{2,14},{3,15},{4,0},{5,1},{6,2},{7,3},{8,4},{9,5},{1... | collective-permute-start | bytes 110600 | tf_op jit(solution)/shard_map/ppermute | solution.py:450
  7.0 0.4 reshape.18
  7.4 1.5 %collective-permute-done = bf16[4,12,384]{2,1,0:T(8,128)(2,1)S(1)} collective-permute-done((bf16[4,12,384]{2,1,0:T(8,128)(2,1)S(1)}, bf16[4,12,384]{2,1,0:T(8,128)(2,1)S(1)}, u32[]{:S(2)}, u32[]{:S(2)}) %collective-permute-start) | collective-permute-done | bytes 36896 | tf_op jit(solution)/shard_map/ppermute | solution.py:450
  8.9 0.5 collective-permute-done.1
  9.5 1.7 %collective-permute-start.2 = (bf16[20,12,128]{2,1,0:T(8,128)(2,1)S(1)}, bf16[20,12,128]{2,1,0:T(8,128)(2,1)S(1)}, u32[]{:S(2)}, u32[]{:S(2)}) collective-permute-start(bf16[20,12,128]{2,1,0:T(8,128)(2,1)S(1)} %get-tuple-element.21), channel_id=1, source_target_pairs={{0,1},{1,2},{2,3},{3,0},{4,5},{5,6},{6,7},{7,4},{8,9},{9,10},{10,1... | collective-permute-start | bytes 184328 | tf_op jit(solution)/shard_map/ppermute | solution.py:450
  11.1 1.3 %collective-permute-start.3 = (bf16[20,12,128]{2,1,0:T(8,128)(2,1)S(1)}, bf16[20,12,128]{2,1,0:T(8,128)(2,1)S(1)}, u32[]{:S(2)}, u32[]{:S(2)}) collective-permute-start(bf16[20,12,128]{2,1,0:T(8,128)(2,1)S(1)} %get-tuple-element.22), channel_id=1, source_target_pairs={{0,3},{1,0},{2,1},{3,2},{4,7},{5,4},{6,5},{7,6},{8,11},{9,8},{10,9... | collective-permute-start | bytes 184328 | tf_op jit(solution)/shard_map/ppermute | solution.py:450
  12.5 0.0 copy-done
  12.5 0.7 collective-permute-start.6
  13.1 1.7 %collective-permute-done.2 = bf16[20,12,128]{2,1,0:T(8,128)(2,1)S(1)} collective-permute-done((bf16[20,12,128]{2,1,0:T(8,128)(2,1)S(1)}, bf16[20,12,128]{2,1,0:T(8,128)(2,1)S(1)}, u32[]{:S(2)}, u32[]{:S(2)}) %collective-permute-start.2) | collective-permute-done | bytes 61472 | tf_op jit(solution)/shard_map/ppermute | solution.py:450
  14.9 1.0 collective-permute-done.3
  15.9 0.1 pad_maximum_fusion.mid
  16.0 0.0 copy-start.1
  16.0 0.1 fusion.1
  16.1 0.1 collective-permute-start.5
  16.1 0.5 collective-permute-start.4
  16.6 0.8 collective-permute-done.5.high
  17.4 0.0 copy-start.11
  17.4 0.2 collective-permute-done.4.low
  17.6 0.0 copy-done.1
  17.6 0.5 copy-done.11
  18.1 0.0 copy-start.12
  18.1 0.6 copy-done.12
  18.7 6.9 %fine_encoder.1 = (bf16[16,16,512]{2,1,0:T(8,128)(2,1)}, bf16[16,36,384]{2,1,0:T(8,128)(2,1)}) custom-call(bf16[20,4,640]{2,1,0:T(4,128)(2,1)} %copy-done.12, bf16[20,12,640]{2,1,0:T(8,128)(2,1)} %copy-done.1, bf16[20,4,640]{2,1,0:T(4,128)(2,1)} %copy-done.11, bf16[32,864]{1,0:T(8,128)(2,1)} %first.2, bf16[32,864]{1,0:T(8,128)(2,1)} %second.2, ...), custom_call_target="tpu_custom_call" | custom-call | tf_op jit(solution)/shard_map/fine_encoder/pallas_call | solution.py:437
  25.6 0.0 collective-permute-done.6.turned
  25.6 0.0 copy-start.6
  25.6 22.2 %all_to_all.10.own = bf16[16,36,384]{2,1,0:T(8,128)(2,1)S(1)} all-to-all(bf16[16,36,384]{2,1,0:T(8,128)(2,1)} %get-tuple-element.12), channel_id=1, replica_groups=mesh['gx'=2,'yz'=16] {'yz'}, dimensions={0} | all-to-all | bytes 884736 | tf_op jit(solution)/shard_map/all_to_all | solution.py:534
  47.8 0.0 copy-start.2
  47.8 0.0 collective-permute-start.7
  47.8 0.0 copy-done.6
  47.8 0.5 collective-permute-start.8
  48.3 0.6 pad_add_fusion.where
  48.9 0.9 collective-permute-done.8.swapped
  49.8 0.0 copy-start.7
  49.8 0.0 collective-permute-done.7.other
  49.9 0.0 copy-done.2
  49.9 0.6 copy-done.7
  50.5 0.8 copy-done.4
  51.3 16.3 %middle.1 = (bf16[12,16,896]{2,1,0:T(8,128)(2,1)}, bf16[72,768]{1,0:T(8,128)(2,1)}) custom-call(s32[3]{0:T(128)} %pad_add_fusion.where, bf16[16,36,384]{2,1,0:T(8,128)(2,1)} %copy-done.2, bf16[16,36,384]{2,1,0:T(8,128)(2,1)} %copy-done.4, bf16[64,1728]{1,0:T(8,128)(2,1)} %first.3, bf16[64,1728]{1,0:T(8,128)(2,1)} %second.3, bf16[256,512]{1,0:T(8,128)(2,1)} %reduce.3, ...), custom_call_target="tpu_custom_call" | custom-call | tf_op jit(solution)/shard_map/middle/pallas_call | solution.py:437
  67.6 0.9 collective-permute-start.11
  68.5 1.1 %collective-permute-start.10 = (bf16[72,768]{1,0:T(8,128)(2,1)}, bf16[72,768]{1,0:T(8,128)(2,1)S(1)}, u32[]{:S(2)}, u32[]{:S(2)}) collective-permute-start(bf16[72,768]{1,0:T(8,128)(2,1)} %get-tuple-element.14.refs_0_), channel_id=1, source_target_pairs={{0,2},{1,3},{2,0},{3,1},{4,6},{5,7},{6,4},{7,5},{8,10},{9,11},{10,... | collective-permute-start | bytes 331784 | tf_op jit(solution)/shard_map/ppermute | solution.py:568
  69.7 1.5 %collective-permute-start.9 = (bf16[72,768]{1,0:T(8,128)(2,1)}, bf16[72,768]{1,0:T(8,128)(2,1)S(1)}, u32[]{:S(2)}, u32[]{:S(2)}) collective-permute-start(bf16[72,768]{1,0:T(8,128)(2,1)} %get-tuple-element.14.refs_0_), channel_id=1, source_target_pairs={{0,1},{1,0},{2,3},{3,2},{4,5},{5,4},{6,7},{7,6},{8,9},{9,8},{10,11... | collective-permute-start | bytes 331784 | tf_op jit(solution)/shard_map/ppermute | solution.py:568
  71.1 3.6 %collective-permute-done.11.refs_3_ = bf16[72,768]{1,0:T(8,128)(2,1)S(1)} collective-permute-done((bf16[72,768]{1,0:T(8,128)(2,1)}, bf16[72,768]{1,0:T(8,128)(2,1)S(1)}, u32[]{:S(2)}, u32[]{:S(2)}) %collective-permute-start.11) | collective-permute-done | bytes 110624 | tf_op jit(solution)/shard_map/ppermute | solution.py:568
  74.7 1.2 %collective-permute-done.10.refs_2_ = bf16[72,768]{1,0:T(8,128)(2,1)S(1)} collective-permute-done((bf16[72,768]{1,0:T(8,128)(2,1)}, bf16[72,768]{1,0:T(8,128)(2,1)S(1)}, u32[]{:S(2)}, u32[]{:S(2)}) %collective-permute-start.10) | collective-permute-done | bytes 110624 | tf_op jit(solution)/shard_map/ppermute | solution.py:568
  75.9 0.0 collective-permute-done.9.refs_1_
  75.9 0.0 copy-done.8
  75.9 0.6 copy-done.9
  76.6 0.6 copy-done.10
  77.2 4.3 %bottom.1 = bf16[16,21,512]{2,1,0:T(8,128)(2,1)} custom-call(bf16[72,768]{1,0:T(8,128)(2,1)} %get-tuple-element.14.refs_0_, bf16[72,768]{1,0:T(8,128)(2,1)} %copy-done.10, bf16[72,768]{1,0:T(8,128)(2,1)} %copy-done.9, bf16[72,768]{1,0:T(8,128)(2,1)} %copy-done.8, bf16[64,1728]{1,0:T(8,128)(2,1)} %refs_4_.1), custom_call_target="tpu_custom_call" | custom-call | tf_op jit(solution)/shard_map/bottom/pallas_call | solution.py:437
  81.5 16.9 %all_to_all.11.near = bf16[16,21,512]{2,1,0:T(8,128)(2,1)S(1)} all-to-all(bf16[16,21,512]{2,1,0:T(8,128)(2,1)} %bottom.1), channel_id=1, replica_groups=mesh['gx'=2,'yz'=16] {'yz'}, dimensions={0} | all-to-all | bytes 688128 | tf_op jit(solution)/shard_map/all_to_all | solution.py:585
  98.4 0.0 collective-permute-start.12
  98.4 1.7 %collective-permute-done.12.far = bf16[16,21,512]{2,1,0:T(8,128)(2,1)S(1)} collective-permute-done((bf16[16,21,512]{2,1,0:T(8,128)(2,1)S(1)}, bf16[16,21,512]{2,1,0:T(8,128)(2,1)S(1)}, u32[]{:S(2)}, u32[]{:S(2)}) %collective-permute-start.12) | collective-permute-done | bytes 344096 | tf_op jit(solution)/shard_map/ppermute | solution.py:586
  100.1 0.0 copy-done.3
  100.1 0.8 copy-done.5
  100.9 9.1 %decoder.1 = bf16[12,16,384]{2,1,0:T(8,128)(2,1)} custom-call(s32[3]{0:T(128)} %pad_add_fusion.where, bf16[16,21,512]{2,1,0:T(8,128)(2,1)} %copy-done.3, bf16[16,21,512]{2,1,0:T(8,128)(2,1)} %copy-done.5, bf16[12,16,896]{2,1,0:T(8,128)(2,1)} %get-tuple-element.15.window, bf16[16,16,512]{2,1,0:T(8,128)(2,1)} %get-tuple-element.16.skip, bf16[256,512]{1,0:T(8,128)(2,1)} %up.1, ...), custom_call_target="tpu_custom_call" | custom-call | tf_op jit(solution)/shard_map/decoder/pallas_call | solution.py:437
  110.0 1.4 %reshape.16 = bf16[12,12,12,32]{3,2,1,0:T(8,128)(2,1)S(1)} reshape(bf16[12,12,384]{2,1,0:T(8,128)(2,1)} %bitcast.23) | data formatting | bytes 221184 | tf_op jit(solution)/shard_map/reshape | solution.py:613
  111.3 0.1 copy.27
  111.5 0.2 reshape.17
  111.7 0.9 copy.23
  (14 shorter events, 0.1 us)
Async XLA Ops:
  0.0 12.5 %copy-start = (bf16[64,1728]{1,0:T(8,128)(2,1)S(1)}, bf16[64,1728]{1,0:T(8,128)(2,1)}, u32[]{:S(2)}) copy-start(bf16[64,1728]{1,0:T(8,128)(2,1)} %param.22) | copy-start | bytes 663556
  1.6 7.3 %collective-permute-start = (bf16[4,12,384]{2,1,0:T(8,128)(2,1)S(1)}, bf16[4,12,384]{2,1,0:T(8,128)(2,1)S(1)}, u32[]{:S(2)}, u32[]{:S(2)}) collective-permute-start(bf16[4,12,384]{2,1,0:T(8,128)(2,1)S(1)} %copy.19), channel_id=1, source_target_pairs={{0,4},{1,5},{2,6},{3,7},{4,8},{5,9},{6,10},{7,11},{8,12},{9,13},{1... | collective-permute-start | bytes 110600 | tf_op jit(solution)/shard_map/ppermute | solution.py:450
  4.9 4.5 %collective-permute-start.1 = (bf16[4,12,384]{2,1,0:T(8,128)(2,1)S(1)}, bf16[4,12,384]{2,1,0:T(8,128)(2,1)S(1)}, u32[]{:S(2)}, u32[]{:S(2)}) collective-permute-start(bf16[4,12,384]{2,1,0:T(8,128)(2,1)S(1)} %copy.21), channel_id=1, source_target_pairs={{0,12},{1,13},{2,14},{3,15},{4,0},{5,1},{6,2},{7,3},{8,4},{9,5},{1... | collective-permute-start | bytes 110600 | tf_op jit(solution)/shard_map/ppermute | solution.py:450
  9.5 5.4 %collective-permute-start.2 = (bf16[20,12,128]{2,1,0:T(8,128)(2,1)S(1)}, bf16[20,12,128]{2,1,0:T(8,128)(2,1)S(1)}, u32[]{:S(2)}, u32[]{:S(2)}) collective-permute-start(bf16[20,12,128]{2,1,0:T(8,128)(2,1)S(1)} %get-tuple-element.21), channel_id=1, source_target_pairs={{0,1},{1,2},{2,3},{3,0},{4,5},{5,6},{6,7},{7,4},{8,9},{9,10},{10,1... | collective-permute-start | bytes 184328 | tf_op jit(solution)/shard_map/ppermute | solution.py:450
  11.1 4.8 %collective-permute-start.3 = (bf16[20,12,128]{2,1,0:T(8,128)(2,1)S(1)}, bf16[20,12,128]{2,1,0:T(8,128)(2,1)S(1)}, u32[]{:S(2)}, u32[]{:S(2)}) collective-permute-start(bf16[20,12,128]{2,1,0:T(8,128)(2,1)S(1)} %get-tuple-element.22), channel_id=1, source_target_pairs={{0,3},{1,0},{2,1},{3,2},{4,7},{5,4},{6,5},{7,6},{8,11},{9,8},{10,9... | collective-permute-start | bytes 184328 | tf_op jit(solution)/shard_map/ppermute | solution.py:450
  12.5 13.1 %collective-permute-start.6 = (bf16[32,1728]{1,0:T(8,128)(2,1)S(1)}, bf16[32,1728]{1,0:T(8,128)(2,1)S(1)}, u32[]{:S(2)}, u32[]{:S(2)}) collective-permute-start(bf16[32,1728]{1,0:T(8,128)(2,1)S(1)} %constant_dynamic-slice_fusion), channel_id=1, source_target_pairs={{0,0},{1,4},{2,8},{3,12},{4,1},{5,5},{6,9},{7,13},{8,2},{9,6},{10,... | collective-permute-start | bytes 331784 | tf_op jit(solution)/shard_map/ppermute | solution.py:490
  16.0 1.6 %copy-start.1 = (bf16[20,12,640]{2,1,0:T(8,128)(2,1)}, bf16[20,12,640]{2,1,0:T(8,128)(2,1)S(1)}, u32[]{:S(2)}) copy-start(bf16[20,12,640]{2,1,0:T(8,128)(2,1)S(1)} %pad_maximum_fusion.mid) | copy-start | bytes 921604
  16.1 1.4 %collective-permute-start.5 = (bf16[20,4,640]{2,1,0:T(4,128)(2,1)S(1)}, bf16[20,4,640]{2,1,0:T(4,128)(2,1)S(1)}, u32[]{:S(2)}, u32[]{:S(2)}) collective-permute-start(bf16[20,4,640]{2,1,0:T(4,128)(2,1)S(1)} %get-tuple-element.19), channel_id=1, source_target_pairs={{0,16},{16,0},{1,17},{17,1},{2,18},{18,2},{3,19},{19,3},{4,20},{20... | collective-permute-start | bytes 307208 | tf_op jit(solution)/shard_map/ppermute | solution.py:450
  16.1 1.4 %collective-permute-start.4 = (bf16[20,4,640]{2,1,0:T(4,128)(2,1)S(1)}, bf16[20,4,640]{2,1,0:T(4,128)(2,1)S(1)}, u32[]{:S(2)}, u32[]{:S(2)}) collective-permute-start(bf16[20,4,640]{2,1,0:T(4,128)(2,1)S(1)} %get-tuple-element.20), channel_id=1, source_target_pairs={{0,16},{16,0},{1,17},{17,1},{2,18},{18,2},{3,19},{19,3},{4,20},{20... | collective-permute-start | bytes 307208 | tf_op jit(solution)/shard_map/ppermute | solution.py:450
  17.4 0.6 copy-start.11
  18.1 0.6 copy-start.12
  25.6 22.2 %copy-start.6 = (bf16[32,1728]{1,0:T(8,128)(2,1)}, bf16[32,1728]{1,0:T(8,128)(2,1)S(1)}, u32[]{:S(2)}) copy-start(bf16[32,1728]{1,0:T(8,128)(2,1)S(1)} %collective-permute-done.6.turned) | copy-start | bytes 331780
  47.8 2.0 %copy-start.2 = (bf16[16,36,384]{2,1,0:T(8,128)(2,1)}, bf16[16,36,384]{2,1,0:T(8,128)(2,1)S(1)}, u32[]{:S(2)}) copy-start(bf16[16,36,384]{2,1,0:T(8,128)(2,1)S(1)} %all_to_all.10.own) | copy-start | bytes 1327108
  47.8 2.0 %collective-permute-start.7 = (bf16[16,36,384]{2,1,0:T(8,128)(2,1)S(1)}, bf16[16,36,384]{2,1,0:T(8,128)(2,1)S(1)}, u32[]{:S(2)}, u32[]{:S(2)}) collective-permute-start(bf16[16,36,384]{2,1,0:T(8,128)(2,1)S(1)} %all_to_all.10.own), channel_id=1, source_target_pairs={{0,16},{16,0},{1,17},{17,1},{2,18},{18,2},{3,19},{19,3},{4,20},{20... | collective-permute-start | bytes 1327112 | tf_op jit(solution)/shard_map/ppermute | solution.py:535
  47.8 2.0 %collective-permute-start.8 = (bf16[32,1728]{1,0:T(8,128)(2,1)S(1)}, bf16[32,1728]{1,0:T(8,128)(2,1)S(1)}, u32[]{:S(2)}, u32[]{:S(2)}) collective-permute-start(bf16[32,1728]{1,0:T(8,128)(2,1)S(1)} %collective-permute-done.6.turned), channel_id=1, source_target_pairs={{0,16},{16,0},{1,17},{17,1},{2,18},{18,2},{3,19},{19,3},{4,20},{20... | collective-permute-start | bytes 331784 | tf_op jit(solution)/shard_map/ppermute | solution.py:536
  49.8 0.7 copy-start.7
  50.5 0.8 copy-start.4
  67.6 7.1 %collective-permute-start.11 = (bf16[72,768]{1,0:T(8,128)(2,1)}, bf16[72,768]{1,0:T(8,128)(2,1)S(1)}, u32[]{:S(2)}, u32[]{:S(2)}) collective-permute-start(bf16[72,768]{1,0:T(8,128)(2,1)} %get-tuple-element.14.refs_0_), channel_id=1, source_target_pairs={{0,3},{1,2},{2,1},{3,0},{4,7},{5,6},{6,5},{7,4},{8,11},{9,10},{10,... | collective-permute-start | bytes 331784 | tf_op jit(solution)/shard_map/ppermute | solution.py:568
  68.5 7.4 %collective-permute-start.10 = (bf16[72,768]{1,0:T(8,128)(2,1)}, bf16[72,768]{1,0:T(8,128)(2,1)S(1)}, u32[]{:S(2)}, u32[]{:S(2)}) collective-permute-start(bf16[72,768]{1,0:T(8,128)(2,1)} %get-tuple-element.14.refs_0_), channel_id=1, source_target_pairs={{0,2},{1,3},{2,0},{3,1},{4,6},{5,7},{6,4},{7,5},{8,10},{9,11},{10,... | collective-permute-start | bytes 331784 | tf_op jit(solution)/shard_map/ppermute | solution.py:568
  69.7 6.3 %collective-permute-start.9 = (bf16[72,768]{1,0:T(8,128)(2,1)}, bf16[72,768]{1,0:T(8,128)(2,1)S(1)}, u32[]{:S(2)}, u32[]{:S(2)}) collective-permute-start(bf16[72,768]{1,0:T(8,128)(2,1)} %get-tuple-element.14.refs_0_), channel_id=1, source_target_pairs={{0,1},{1,0},{2,3},{3,2},{4,5},{5,4},{6,7},{7,6},{8,9},{9,8},{10,11... | collective-permute-start | bytes 331784 | tf_op jit(solution)/shard_map/ppermute | solution.py:568
  74.7 1.2 %copy-start.8 = (bf16[72,768]{1,0:T(8,128)(2,1)}, bf16[72,768]{1,0:T(8,128)(2,1)S(1)}, u32[]{:S(2)}) copy-start(bf16[72,768]{1,0:T(8,128)(2,1)S(1)} %collective-permute-done.11.refs_3_) | copy-start | bytes 331780
  75.9 0.6 copy-start.9
  76.6 0.6 copy-start.10
  98.4 1.7 %copy-start.3 = (bf16[16,21,512]{2,1,0:T(8,128)(2,1)}, bf16[16,21,512]{2,1,0:T(8,128)(2,1)S(1)}, u32[]{:S(2)}) copy-start(bf16[16,21,512]{2,1,0:T(8,128)(2,1)S(1)} %all_to_all.11.near) | copy-start | bytes 1032196
  98.4 1.7 %collective-permute-start.12 = (bf16[16,21,512]{2,1,0:T(8,128)(2,1)S(1)}, bf16[16,21,512]{2,1,0:T(8,128)(2,1)S(1)}, u32[]{:S(2)}, u32[]{:S(2)}) collective-permute-start(bf16[16,21,512]{2,1,0:T(8,128)(2,1)S(1)} %all_to_all.11.near), channel_id=1, source_target_pairs={{0,16},{16,0},{1,17},{17,1},{2,18},{18,2},{3,19},{19,3},{4,20},{20... | collective-permute-start | bytes 1032200 | tf_op jit(solution)/shard_map/ppermute | solution.py:586
  100.1 0.8 copy-start.5
where the time goes:
time: 113 us
  blocking collectives  39.1 us (35%)
  Pallas kernels  36.6 us (32%)
  starting transfers between devices  13.4 us (12%)
  waiting for transfers between devices  13.1 us (12%)
  local copies, waits for them, and re-layouts  9.57 us (8%)
    pallas_call x4, Pallas kernels, call(): pl.pallas_call(kernel, out_shape=outs, in_specs=[pl.BlockSpec(memory_spac...  36.6 us
    all_to_all x1, blocking collectives, gathered_body(): own = lax.all_to_all(small, 'yz', 0, 0)  22.2 us
    all_to_all x1, blocking collectives, gathered_body(): near = lax.all_to_all(sent, 'yz', 0, 0)  16.9 us
    ppermute x6, starting transfers between devices, exchange(): return (lax.ppermute(tail, axis, ahead), lax.ppermute(head, axis, back))  8.74 us
    unnamed x29, local copies, waits for them, and re-layouts  5.88 us
    ppermute x6, waiting for transfers between devices, exchange(): return (lax.ppermute(tail, axis, ahead), lax.ppermute(head, axis, back))  5.69 us
    ppermute x3, waiting for transfers between devices, gathered_body(): lax.ppermute(partial, 'yz', [(s, s ^ turn) for s in range(devices)])  4.8 us
    ppermute x3, starting transfers between devices, gathered_body(): lax.ppermute(partial, 'yz', [(s, s ^ turn) for s in range(devices)])  3.49 us
  transfers between devices with their start and end apart: 13, of which 10 were waited for; matrix products, arithmetic and copies ran while one was open for 1% of the time, Pallas kernels for 6%

commit v1 on v0

--- a/solution.py
+++ b/solution.py
@@ -150,9 +150,7 @@
             value = halves[0, pl.ds(16 * y + 2, count, 2), :]
             value = value + halves[1, pl.ds(16 * y + 3, count, 2), :]
             flats[count * y : count * (y + 1), span_of(tile)] = value
-    result = flats[...].astype(BF)
-    for copy in range(small.shape[0]):
-        small[copy] = result
+    small[...] = flats[...].astype(BF)
 
 
 def wrap_rows(wide, layers, count):
@@ -163,74 +161,44 @@
 
 
 def middle(
-    where,
-    own,
-    other,
-    first,
-    second,
-    reduce,
-    turned,
-    swapped,
-    window,
-    partial,
-    wide,
-    s,
-    table,
-    flat,
-    down,
-    whole,
-    halves,
-    flats,
+    own, other, first, second, reduce, window, sent, wide, s, table, flat, down, whole, halves, flats
 ):
-    across = math.isqrt(own.shape[0])
-    side = math.isqrt(own.shape[1])
-    cells = side * across
-    lanes = side * 64
-    span = cells * 64
-    row, column = where[0], where[1]
-    for i in range(across):
-        for place, j in enumerate([across - 1] + list(range(across))):
-            start = place * lanes
-            size = min(lanes, span + LANES - start)
-            for part, gathered in enumerate((own, other)):
-                block = gathered[i * across + j, :, :size].astype(F32)
-                for y in range(side):
-                    wide[
-                        1 + side * i + y,
-                        8 + side * part : 8 + side * (part + 1),
-                        start : start + size,
-                    ] = block[side * y : side * (y + 1)]
-    wrap_rows(wide, cells, 2 * side)
-    stage(wide, s, cells + 2, 16, 7, span + LANES)
+    span = own.shape[1]
+    side = span // 3 // 64
+    reach = side - 1
+    layers = side + 2 * reach
+    near, far = own[...].astype(F32), other[...].astype(F32)
+    for y in range(layers):
+        start = side * y
+        wide[y, 0:reach, :span] = far[start + 1 : start + side]
+        wide[y, reach : reach + side, :span] = near[start : start + side]
+        wide[y, reach + side : 2 * reach + side, :span] = far[start : start + reach]
+    stage(wide, s, layers, 16, 0, span)
     conv_table(table, flat, first[...], 64)
-    for tile in range(span // LANES):
-        value = rounded_relu(convolve(s, table, cells, 16, tile))
-        wide[1 : cells + 1, 8:24, span_of(tile)] = value.astype(F32).reshape(cells, 16, LANES)
-    wide[:, :, span : span + LANES] = wide[:, :, 0:LANES]
-    wrap_rows(wide, cells, 2 * side)
-    stage(wide, s, cells + 2, 16, 7, span + LANES)
+    layers -= 2
+    tiles = span // LANES - 1
+    for tile in range(tiles):
+        value = rounded_relu(convolve(s, table, layers, 16, tile))
+        wide[:layers, 0:16, span_of(tile)] = value.astype(F32).reshape(layers, 16, LANES)
+    stage(wide, s, layers, 16, 0, tiles * LANES)
     conv_table(table, flat, second[...], 64)
-    for tile in range(span // LANES):
-        value = rounded_relu(convolve(s, table, cells, 16, tile))
-        whole[3 : cells + 3, :, span_of(tile)] = value.reshape(cells, 16, LANES)
-    whole[0:3] = whole[cells : cells + 3]
-    whole[cells + 3 : cells + 6] = whole[3:6]
-    whole[:, :, span : span + 512] = whole[:, :, 0:512]
-    window[...] = whole[
-        pl.ds(row * side, window.shape[0]),
-        :,
-        pl.ds(pl.multiple_of(column * lanes, LANES), window.shape[2]),
-    ]
-    half = cells // 2
-    shrunk = half * 64
-    quarter = reduce[pl.ds(pl.multiple_of(column * 64, 64), 64), :]
-    shrink_table(down, flat, quarter, 64, 0)
-    for tile in range(shrunk // LANES):
-        left = jnp.concatenate(
+    layers -= 2
+    for tile in range(tiles - 1):
+        value = rounded_relu(convolve(s, table, layers, 16, tile)).reshape(layers, 16, LANES)
+        whole[:, :, span_of(tile)] = value
+        wide[:layers, 0:16, span_of(tile)] = value.astype(F32)
+    width = window.shape[2]
+    skipped = layers - side - 3
+    wide[:layers, 16 : 16 + layers - 3, :width] = wide[:layers, 3:layers, :width]
+    wide[:layers, 13 + layers : 16 + layers, :width] = wide[:layers, 0:3, :width]
+    window[...] = wide[:layers, 16:32, :width].astype(BF)
+    half = side // 2
+    lefts = [
+        jnp.concatenate(
             [
                 jnp.concatenate(
                     [
-                        whole[3 + 2 * y + dy, :, tile * DEPTH : (tile + 1) * DEPTH]
+                        whole[skipped + 2 * y + dy, :, (tile + 1) * DEPTH : (tile + 2) * DEPTH]
                         for y in range(half)
                     ],
                     axis=0,
@@ -239,27 +207,81 @@
             ],
             axis=1,
         )
-        total = dot(left, down[...])
-        halves[0] = total[:, :LANES]
-        halves[1] = total[:, LANES:]
-        for y in range(half):
-            value = halves[0, pl.ds(16 * y, side, 2), :]
-            value = value + halves[1, pl.ds(16 * y + 1, side, 2), :]
-            wide[1 + y, 8 : 8 + side, span_of(tile)] = value.astype(BF).astype(F32)
-    wide[1 : half + 1, 8 : 8 + side, shrunk : shrunk + LANES] = wide[
-        1 : half + 1, 8 : 8 + side, 0:LANES
+        for tile in range(2)
     ]
-    wrap_rows(wide, half, side)
-    stage(wide, s, half + 2, 16, 7, shrunk + LANES)
+    across = reduce.shape[0] // 64
+    for quarter in range(across):
+        shrink_table(down, flat, reduce[64 * quarter : 64 * (quarter + 1), :], 64, 0)
+        for tile, left in enumerate(lefts):
+            total = dot(left, down[...])
+            halves[0] = total[:, :LANES]
+            halves[1] = total[:, LANES:]
+            for y in range(half):
+                value = halves[0, pl.ds(16 * y + 3, half, 2), :]
+                value = value + halves[1, pl.ds(16 * y + 4, half, 2), :]
+                row = half * (half * tile + y)
+                flats[row : row + half, :] = value
+        count = half * half
+        fold = (count + 1) // 2
+        last = flats[count : count + 16, :]
+        turn = pltpu.roll(last, 64, 1)
+        flats[count : count + fold, :] = jnp.where(
+            lane_group(fold, 64) == 0, last[:fold], turn[fold : 2 * fold]
+        )
+        result = flats[0 : sent.shape[1], :].astype(BF)
+        for target in range(quarter, sent.shape[0], across):
+            sent[target] = result
+
+
+def bottom_start(gathered, turned, swapped, partial, wide, s, table, flat, flats):
+    span = partial.shape[1]
+    cells = span // 64
+    side = cells // 2
+    core = lax.axis_index("gx")
+    devices = gathered.shape[0] // 2
+    across = math.isqrt(devices)
+    half = cells // across
+    count = half * half
+    fold = (count + 1) // 2
+    low = lane_group(count, 64) == 0
+    for part in range(2):
+        base = (core if part == 0 else 1 - core) * devices
+        for i in range(across):
+            for j in range(0, across, 2):
+                here = gathered[base + across * i + j].astype(F32)
+                after = gathered[base + across * i + j + 1].astype(F32)
+                here_turn, after_turn = pltpu.roll(here, 64, 1), pltpu.roll(after, 64, 1)
+
+                def unfold(one, two):
+                    return jnp.concatenate([one[count : count + fold], two[count : 2 * count - fold]])
+
+                pieces = (
+                    here[:count],
+                    jnp.where(low, unfold(here, here_turn), after_turn[:count]),
+                    jnp.where(low, after_turn[:count], unfold(after_turn, after)),
+                )
+                for turn, piece in enumerate(pieces):
+                    tile = half * (j // 2) + turn
+                    for y in range(half):
+                        wide[
+                            1 + half * i + y,
+                            8 + half * part : 8 + half * (part + 1),
+                            span_of(tile),
+                        ] = piece[half * y : half * (y + 1)]
+    wide[1 : cells + 1, 8 : 8 + side, span : span + LANES] = wide[
+        1 : cells + 1, 8 : 8 + side, 0:LANES
+    ]
+    wrap_rows(wide, cells, side)
+    stage(wide, s, cells + 2, 16, 7, span + LANES)
     mine, theirs = turned[...].astype(F32), swapped[...].astype(F32)
-    is_first = where[2] == 0
+    is_first = core == 0
     stored = jnp.concatenate(
         [jnp.where(is_first, mine, theirs), jnp.where(is_first, theirs, mine)], axis=0
     )
     conv_table(table, flat, stored, 64)
-    for tile in range(shrunk // LANES):
-        value = convolve(s, table, half, 16, tile)
-        for y in range(half):
+    for tile in range(span // LANES):
+        value = convolve(s, table, cells, 16, tile)
+        for y in range(cells):
             flats[side * y : side * (y + 1), span_of(tile)] = value[16 * y : 16 * y + side]
     partial[...] = flats[...].astype(BF)
 
@@ -284,26 +306,28 @@
     conv_table(table, flat, weight[...], 64)
     for tile in range(span // LANES):
         value = convolve(s, table, cells, 16, tile).reshape(cells, 16, LANES)
-        whole[2 : cells + 2, :, span_of(tile + 1)] = value[:, :8]
+        whole[2 : cells + 2, :, span_of(tile + 2)] = value[:, :8]
     whole[0:2] = whole[cells : cells + 2]
     whole[cells + 2 : cells + 5] = whole[2:5]
-    whole[:, :, 0:LANES] = whole[:, :, span : span + LANES]
-    whole[:, :, span + LANES : span + 512] = whole[:, :, LANES:512]
+    whole[:, :, 0 : 2 * LANES] = whole[:, :, span : span + 2 * LANES]
     block = cells // across
     kept = side // 2
-    layers = out.shape[1] // kept
+    layers = block + 4
     for i in range(across):
         for j in range(across):
             start = (block * j - block * j % 2) * 64
-            for y in range(layers):
-                flats[kept * y : kept * (y + 1), :] = whole[
-                    block * i + y, 0:kept, start : start + out.shape[2]
-                ]
+            for tile in range(4):
+                for y in range(layers):
+                    row = kept * (layers * tile + y)
+                    flats[row : row + kept, :] = whole[
+                        block * i + y,
+                        0:kept,
+                        start + tile * LANES : start + (tile + 1) * LANES,
+                    ]
             out[i * across + j] = flats[...].astype(BF)
 
 
 def decoder(
-    where,
     near,
     far,
     window,
@@ -325,8 +349,8 @@
 ):
     across = math.isqrt(near.shape[0])
     kept = window.shape[0] // 4
-    layers = near.shape[1] // kept
-    odd = where[1] % 2
+    layers = kept + 4
+    odd = lax.axis_index("yz") % across % 2
     for dx in range(2):
         for dy in range(2):
             pair = picked(up[...], dx, dy, 64)
@@ -347,10 +371,12 @@
             for k in range(across):
                 total = total + parts[k * across + group].astype(F32)
             total = jnp.maximum(total, 0.0)
-            for y in range(layers):
-                columns[y, kept * part : kept * (part + 1), :512] = total[
-                    kept * y : kept * (y + 1)
-                ]
+            for tile in range(4):
+                for y in range(layers):
+                    row = kept * (layers * tile + y)
+                    columns[y, kept * part : kept * (part + 1), span_of(tile)] = total[
+                        row : row + kept
+                    ]
         groups.append(
             jnp.concatenate(
                 [
@@ -432,16 +458,19 @@
         out[:, :, span_of(tile)] = value.reshape(count, 16, LANES)
 
 
-def call(kernel, outs, scratch, *args, scalars=0):
-    spaces = [pltpu.SMEM] * scalars + [pltpu.VMEM] * (len(args) - scalars)
+def call(kernel, outs, scratch, *args):
     return pl.pallas_call(
         kernel,
-        out_shape=outs,
-        in_specs=[pl.BlockSpec(memory_space=space) for space in spaces],
+        out_shape=jax.tree.map(lambda out: pltpu.VMEM(out.shape, out.dtype), outs),
+        in_specs=[pl.BlockSpec(memory_space=pltpu.VMEM)] * len(args),
         out_specs=jax.tree.map(lambda _: pl.BlockSpec(memory_space=pltpu.VMEM), outs),
         scratch_shapes=scratch,
         name=kernel.__name__,
-    )(*args)
+    )(*[near_by(arg) for arg in args])
+
+
+def near_by(arg):
+    return pltpu.with_memory_space_constraint(arg, pltpu.MemorySpace.VMEM)
 
 
 def exchange(head, tail, axis, route):
@@ -469,8 +498,6 @@
 ):
     devices = lax.axis_size("yz")
     across = math.isqrt(devices)
-    place = lax.axis_index("yz")
-    where = jnp.stack([place // across, place % across, lax.axis_index("gx")]).astype(jnp.int32)
     fine, ext = features_in.shape[1], features_in.shape[2]
     mid = encode_middle_first.shape[0]
     halo = 4
@@ -509,7 +536,7 @@
         fine_encoder,
         (
             jax.ShapeDtypeStruct((ext + 4, ext + 4, (ext + 4) * fine), BF),
-            jax.ShapeDtypeStruct((devices, side * side, side * mid), BF),
+            jax.ShapeDtypeStruct((side * side, side * mid), BF),
         ),
         [
             pltpu.VMEM((seen, 40, seen * fine), F32),
@@ -531,37 +558,54 @@
 
     small, turned = lax.optimization_barrier((small, turned))
     swap = [(s, around(s, 1)) for s in range(cores)]
-    own = lax.all_to_all(small, "yz", 0, 0)
+    swapped = lax.ppermute(turned, "gx", swap)
+    reach = (side - 1) * side
+    low, high = exchange(small[:reach], small[side:], "yz", along_y)
+    small = jnp.concatenate([low, small, high], axis=0)
+    low, high = exchange(small, small, "yz", along_z)
+    own = jnp.concatenate([low, small, high], axis=1)
     other = lax.ppermute(own, "gx", swap)
-    swapped = lax.ppermute(turned, "gx", swap)
 
     total = side * across
     half = total // 2
-    window, partial = call(
+    layers, span = 3 * side - 2, 3 * side * mid
+    window, sent = call(
         middle,
         (
-            jax.ShapeDtypeStruct((12, 16, 14 * mid), BF),
-            jax.ShapeDtypeStruct((half * side, half * mid), BF),
+            jax.ShapeDtypeStruct((layers - 4, 16, 14 * mid), BF),
+            jax.ShapeDtypeStruct((devices * cores, 16, LANES), BF),
         ),
         [
-            pltpu.VMEM((total + 2, 32, total * mid + LANES), F32),
-            pltpu.VMEM((3, (total + 2) * 16, total * mid + LANES), BF),
+            pltpu.VMEM((layers, 32, span), F32),
+            pltpu.VMEM((3, layers * 16, span), BF),
             table,
             flat,
             down,
-            pltpu.VMEM((total + 6, 16, total * mid + 512), BF),
-            pltpu.VMEM((2, half * 16, LANES), F32),
-            pltpu.VMEM((half * side, half * mid), F32),
+            pltpu.VMEM((layers - 4, 16, 14 * mid), BF),
+            pltpu.VMEM((2, side * 8, LANES), F32),
+            pltpu.VMEM((32, LANES), F32),
         ],
-        where,
         own,
         other,
         encode_middle_first,
         encode_middle_second,
         reduce_middle,
+    )
+    sent, swapped = lax.optimization_barrier((sent, swapped))
+    gathered = lax.all_to_all(sent, ("gx", "yz"), 0, 0)
+    partial = call(
+        bottom_start,
+        jax.ShapeDtypeStruct((half * side, half * mid), BF),
+        [
+            pltpu.VMEM((half + 2, 32, half * mid + LANES), F32),
+            pltpu.VMEM((3, (half + 2) * 16, half * mid + LANES), BF),
+            table,
+            flat,
+            pltpu.VMEM((half * side, half * mid), F32),
+        ],
+        gathered,
         turned,
         swapped,
-        scalars=1,
     )
 
     pieces = [partial] + [
@@ -570,14 +614,14 @@
     ]
     sent = call(
         bottom,
-        jax.ShapeDtypeStruct((devices, 7 * side // 2, 8 * mid), BF),
+        jax.ShapeDtypeStruct((devices, 88, LANES), BF),
         [
             pltpu.VMEM((half + 2, 32, half * mid + LANES), F32),
             pltpu.VMEM((3, (half + 2) * 16, half * mid + LANES), BF),
             table,
             flat,
-            pltpu.VMEM((half + 5, 8, half * mid + 512), F32),
-            pltpu.VMEM((7 * side // 2, 8 * mid), F32),
+            pltpu.VMEM((half + 5, 8, half * mid + 2 * LANES), F32),
+            pltpu.VMEM((88, LANES), F32),
         ],
         *pieces,
         bottom_second,
@@ -597,7 +641,6 @@
             pltpu.VMEM((8, 16, 512), F32),
             pltpu.VMEM((8, 16, 32, LANES), F32),
         ],
-        where,
         near,
         far,
         window,
@@ -608,7 +651,6 @@
         expand_fine,
         decode_fine_first,
         decode_fine_second,
-        scalars=1,
     )
     risen = risen[:, :ext].reshape(ext, ext, ext, fine).transpose(3, 1, 0, 2)
     return risen.reshape(1, fine, ext, ext * ext)

time: 113 us -> 94.9 us (0.84)
  Pallas kernels: 36.6 us -> 21.3 us
  blocking collectives: 39.1 us -> 27.2 us
  starting transfers between devices: 13.4 us -> 21.7 us
  waiting for transfers between devices: 13.1 us -> 20 us
  local copies, waits for them, and re-layouts: 9.57 us -> 4.13 us
    pallas_call x4 -> x5, Pallas kernels: 36.6 us -> 21.3 us  [call(): pl.pallas_call(kernel, out_shape=jax.tree.map(lambda out: pltpu.VMEM(out....]
    all_to_all x1, blocking collectives: 22.2 us -> 12 us  [gathered_body(): gathered = lax.all_to_all(sent, ('gx', 'yz'), 0, 0)]
    ppermute x6 -> x10, starting transfers between devices: 8.74 us -> 16.9 us  [exchange(): return (lax.ppermute(tail, axis, ahead), lax.ppermute(head, axis, back))]
    ppermute x6 -> x10, waiting for transfers between devices: 5.69 us -> 12.8 us  [exchange(): return (lax.ppermute(tail, axis, ahead), lax.ppermute(head, axis, back))]
    unnamed x29 -> x31, local copies, waits for them, and re-layouts: 5.88 us -> 1.34 us
    all_to_all x1, blocking collectives: 16.9 us -> 15.2 us  [gathered_body(): near = lax.all_to_all(sent, 'yz', 0, 0)]
  transfers between devices with their start and end apart: 13 -> 17, of which waited for: 10 -> 13; matrix products, arithmetic and copies ran while one was open for 1% -> 1% of each run, Pallas kernels for 6% -> 11%
where the time goes in v1:
time: 94.9 us; the launch traced here: 94.7 us
  blocking collectives  27.2 us (29%)
  starting transfers between devices  21.7 us (23%)
  Pallas kernels  21.3 us (22%)
  waiting for transfers between devices  20 us (21%)
  local copies, waits for them, and re-layouts  4.13 us (4%)
    pallas_call x5, Pallas kernels, call(): pl.pallas_call(kernel, out_shape=jax.tree.map(lambda out: pltpu.VMEM(out....  21.3 us
    ppermute x10, starting transfers between devices, exchange(): return (lax.ppermute(tail, axis, ahead), lax.ppermute(head, axis, back))  16.9 us
    all_to_all x1, blocking collectives, gathered_body(): near = lax.all_to_all(sent, 'yz', 0, 0)  15.2 us
    ppermute x10, waiting for transfers between devices, exchange(): return (lax.ppermute(tail, axis, ahead), lax.ppermute(head, axis, back))  12.8 us
    all_to_all x1, blocking collectives, gathered_body(): gathered = lax.all_to_all(sent, ('gx', 'yz'), 0, 0)  12 us
    ppermute x3, waiting for transfers between devices, gathered_body(): lax.ppermute(partial, 'yz', [(s, s ^ turn) for s in range(devices)])  4.59 us
    ppermute x3, starting transfers between devices, gathered_body(): lax.ppermute(partial, 'yz', [(s, s ^ turn) for s in range(devices)])  3.55 us
  transfers between devices with their start and end apart: 17, of which 13 were waited for; matrix products, arithmetic and copies ran while one was open for 1% of the time, Pallas kernels for 11%

profile of v1, /device:TPU:0, one launch (start us, length us, event | category | flops | bytes accessed | tf_op | source)
XLA Modules:
  0.0 94.7 jit_solution(3238434006226114018)
XLA Ops:
  0.0 1.2 %copy.18 = bf16[1,32,12,144]{1,3,2,0:T(8,128)(2,1)S(1)} copy(bf16[1,32,12,144]{3,1,2,0:T(8,128)(2,1)} %param.15) | data formatting | bytes 221184 | tf_op args[0]
  1.2 0.1 reshape.14
  1.4 0.2 slice.34
  1.6 3.1 %collective-permute-start = (bf16[4,12,384]{2,1,0:T(8,128)(2,1)S(1)}, bf16[4,12,384]{2,1,0:T(8,128)(2,1)S(1)}, u32[]{:S(2)}, u32[]{:S(2)}) collective-permute-start(bf16[4,12,384]{2,1,0:T(8,128)(2,1)S(1)} %copy.19), channel_id=1, source_target_pairs={{0,4},{1,5},{2,6},{3,7},{4,8},{5,9},{6,10},{7,11},{8,12},{9,13},{1... | collective-permute-start | bytes 110600 | tf_op jit(solution)/shard_map/ppermute | solution.py:479
  4.7 0.2 slice.36
  4.9 2.1 %collective-permute-start.1 = (bf16[4,12,384]{2,1,0:T(8,128)(2,1)S(1)}, bf16[4,12,384]{2,1,0:T(8,128)(2,1)S(1)}, u32[]{:S(2)}, u32[]{:S(2)}) collective-permute-start(bf16[4,12,384]{2,1,0:T(8,128)(2,1)S(1)} %copy.21), channel_id=1, source_target_pairs={{0,12},{1,13},{2,14},{3,15},{4,0},{5,1},{6,2},{7,3},{8,4},{9,5},{1... | collective-permute-start | bytes 110600 | tf_op jit(solution)/shard_map/ppermute | solution.py:479
  7.0 0.4 reshape.18
  7.4 1.5 %collective-permute-done = bf16[4,12,384]{2,1,0:T(8,128)(2,1)S(1)} collective-permute-done((bf16[4,12,384]{2,1,0:T(8,128)(2,1)S(1)}, bf16[4,12,384]{2,1,0:T(8,128)(2,1)S(1)}, u32[]{:S(2)}, u32[]{:S(2)}) %collective-permute-start) | collective-permute-done | bytes 36896 | tf_op jit(solution)/shard_map/ppermute | solution.py:479
  8.9 0.5 collective-permute-done.1
  9.5 1.7 %collective-permute-start.2 = (bf16[20,12,128]{2,1,0:T(8,128)(2,1)S(1)}, bf16[20,12,128]{2,1,0:T(8,128)(2,1)S(1)}, u32[]{:S(2)}, u32[]{:S(2)}) collective-permute-start(bf16[20,12,128]{2,1,0:T(8,128)(2,1)S(1)} %get-tuple-element.25), channel_id=1, source_target_pairs={{0,1},{1,2},{2,3},{3,0},{4,5},{5,6},{6,7},{7,4},{8,9},{9,10},{10,1... | collective-permute-start | bytes 184328 | tf_op jit(solution)/shard_map/ppermute | solution.py:479
  11.1 1.3 %collective-permute-start.3 = (bf16[20,12,128]{2,1,0:T(8,128)(2,1)S(1)}, bf16[20,12,128]{2,1,0:T(8,128)(2,1)S(1)}, u32[]{:S(2)}, u32[]{:S(2)}) collective-permute-start(bf16[20,12,128]{2,1,0:T(8,128)(2,1)S(1)} %get-tuple-element.26), channel_id=1, source_target_pairs={{0,3},{1,0},{2,1},{3,2},{4,7},{5,4},{6,5},{7,6},{8,11},{9,8},{10,9... | collective-permute-start | bytes 184328 | tf_op jit(solution)/shard_map/ppermute | solution.py:479
  12.5 0.7 collective-permute-start.6
  13.1 1.7 %collective-permute-done.2 = bf16[20,12,128]{2,1,0:T(8,128)(2,1)S(1)} collective-permute-done((bf16[20,12,128]{2,1,0:T(8,128)(2,1)S(1)}, bf16[20,12,128]{2,1,0:T(8,128)(2,1)S(1)}, u32[]{:S(2)}, u32[]{:S(2)}) %collective-permute-start.2) | collective-permute-done | bytes 61472 | tf_op jit(solution)/shard_map/ppermute | solution.py:479
  14.9 1.0 %collective-permute-done.3 = bf16[20,12,128]{2,1,0:T(8,128)(2,1)S(1)} collective-permute-done((bf16[20,12,128]{2,1,0:T(8,128)(2,1)S(1)}, bf16[20,12,128]{2,1,0:T(8,128)(2,1)S(1)}, u32[]{:S(2)}, u32[]{:S(2)}) %collective-permute-start.3) | collective-permute-done | bytes 61472 | tf_op jit(solution)/shard_map/ppermute | solution.py:479
  15.9 0.1 pad_maximum_fusion.mid
  16.0 0.0 copy-start.8
  16.0 0.0 copy-start.9
  16.0 0.0 copy-start.13
  16.0 0.1 fusion.1
  16.1 0.1 collective-permute-start.5
  16.2 0.5 collective-permute-start.4
  16.7 0.8 collective-permute-done.5.high
  17.5 0.2 collective-permute-done.4.low
  17.6 5.0 %fine_encoder.1 = (bf16[16,16,512]{2,1,0:T(8,128)(2,1)S(1)}, bf16[36,384]{1,0:T(8,128)(2,1)S(1)}) custom-call(bf16[20,4,640]{2,1,0:T(4,128)(2,1)S(1)} %collective-permute-done.4.low, bf16[20,12,640]{2,1,0:T(8,128)(2,1)S(1)} %pad_maximum_fusion.mid, bf16[20,4,640]{2,1,0:T(4,128)(2,1)S(1)} %collective-permute-done.5.high, bf16[32,864]{1,0:T(8,128)(2,1)S(1)} %copy-done.8, ...), custom_call_target="tpu_custom_call" | custom-call | tf_op jit(solution)/shard_map/fine_encoder/pallas_call | solution.py:462
  22.6 0.0 collective-permute-done.6.turned
  22.6 1.1 %collective-permute-start.7 = (bf16[30,384]{1,0:T(8,128)(2,1)S(1)}, bf16[30,384]{1,0:T(8,128)(2,1)S(1)}, u32[]{:S(2)}, u32[]{:S(2)}) collective-permute-start(bf16[30,384]{1,0:T(8,128)(2,1)S(1)} %get-tuple-element.27), channel_id=1, source_target_pairs={{0,4},{1,5},{2,6},{3,7},{4,8},{5,9},{6,10},{7,11},{8,12},{9,13},{1... | collective-permute-start | bytes 69128 | tf_op jit(solution)/shard_map/ppermute | solution.py:479
  23.8 2.8 %collective-permute-start.8 = (bf16[30,384]{1,0:T(8,128)(2,1)S(1)}, bf16[30,384]{1,0:T(8,128)(2,1)S(1)}, u32[]{:S(2)}, u32[]{:S(2)}) collective-permute-start(bf16[30,384]{1,0:T(8,128)(2,1)S(1)} %get-tuple-element.28), channel_id=1, source_target_pairs={{0,12},{1,13},{2,14},{3,15},{4,0},{5,1},{6,2},{7,3},{8,4},{9,5},{1... | collective-permute-start | bytes 69128 | tf_op jit(solution)/shard_map/ppermute | solution.py:479
  26.5 1.9 %collective-permute-done.7 = bf16[30,384]{1,0:T(8,128)(2,1)S(1)} collective-permute-done((bf16[30,384]{1,0:T(8,128)(2,1)S(1)}, bf16[30,384]{1,0:T(8,128)(2,1)S(1)}, u32[]{:S(2)}, u32[]{:S(2)}) %collective-permute-start.7) | collective-permute-done | bytes 23072 | tf_op jit(solution)/shard_map/ppermute | solution.py:479
  28.4 0.0 collective-permute-done.8
  28.4 0.0 copy-start.2
  28.4 4.3 %collective-permute-start.10 = (bf16[96,384]{1,0:T(8,128)(2,1)S(1)}, bf16[96,384]{1,0:T(8,128)(2,1)S(1)}, u32[]{:S(2)}, u32[]{:S(2)}) collective-permute-start(bf16[96,384]{1,0:T(8,128)(2,1)S(1)} %pad_maximum_fusion.2), channel_id=1, source_target_pairs={{0,3},{1,0},{2,1},{3,2},{4,7},{5,4},{6,5},{7,6},{8,11},{9,8},{10,9... | collective-permute-start | bytes 221192 | tf_op jit(solution)/shard_map/ppermute | solution.py:479
  32.7 0.0 collective-permute-start.9
  32.7 2.0 %collective-permute-done.10 = bf16[96,384]{1,0:T(8,128)(2,1)S(1)} collective-permute-done((bf16[96,384]{1,0:T(8,128)(2,1)S(1)}, bf16[96,384]{1,0:T(8,128)(2,1)S(1)}, u32[]{:S(2)}, u32[]{:S(2)}) %collective-permute-start.10) | collective-permute-done | bytes 73760 | tf_op jit(solution)/shard_map/ppermute | solution.py:479
  34.7 3.3 %collective-permute-done.9 = bf16[96,384]{1,0:T(8,128)(2,1)S(1)} collective-permute-done((bf16[96,384]{1,0:T(8,128)(2,1)S(1)}, bf16[96,384]{1,0:T(8,128)(2,1)S(1)}, u32[]{:S(2)}, u32[]{:S(2)}) %collective-permute-start.9) | collective-permute-done | bytes 73760 | tf_op jit(solution)/shard_map/ppermute | solution.py:479
  38.0 0.1 collective-permute-start.11
  38.1 0.5 collective-permute-start.12
  38.6 1.0 %collective-permute-done.11.other = bf16[96,1152]{1,0:T(8,128)(2,1)S(1)} collective-permute-done((bf16[96,1152]{1,0:T(8,128)(2,1)S(1)}, bf16[96,1152]{1,0:T(8,128)(2,1)S(1)}, u32[]{:S(2)}, u32[]{:S(2)}) %collective-permute-start.11) | collective-permute-done | bytes 221216 | tf_op jit(solution)/shard_map/ppermute | solution.py:567
  39.5 0.0 copy-done.2
  39.5 5.3 %middle.1 = (bf16[12,16,896]{2,1,0:T(8,128)(2,1)S(1)}, bf16[32,16,128]{2,1,0:T(8,128)(2,1)S(1)}) custom-call(bf16[96,1152]{1,0:T(8,128)(2,1)S(1)} %pad_maximum_fusion.1.own, bf16[96,1152]{1,0:T(8,128)(2,1)S(1)} %collective-permute-done.11.other, bf16[64,1728]{1,0:T(8,128)(2,1)S(1)} %copy-done.5, bf16[64,1728]{1,0:T(8,128)(2,1)S(1)} %copy-done.6, ...), custom_call_target="tpu_custom_call" | custom-call | tf_op jit(solution)/shard_map/middle/pallas_call | solution.py:462
  44.8 0.0 collective-permute-done.12.swapped
  44.8 12.0 %all_to_all.10.gathered = bf16[32,16,128]{2,1,0:T(8,128)(2,1)S(1)} all-to-all(bf16[32,16,128]{2,1,0:T(8,128)(2,1)S(1)} %get-tuple-element.17), channel_id=1, replica_groups=mesh['gx'=2,'yz'=16] {'gx','yz'}, dimensions={0} | all-to-all | bytes 262144 | tf_op jit(solution)/shard_map/all_to_all | solution.py:595
  56.8 1.9 %bottom_start.1.refs_0_ = bf16[72,768]{1,0:T(8,128)(2,1)S(1)} custom-call(bf16[32,16,128]{2,1,0:T(8,128)(2,1)S(1)} %all_to_all.10.gathered, bf16[32,1728]{1,0:T(8,128)(2,1)S(1)} %collective-permute-done.6.turned, bf16[32,1728]{1,0:T(8,128)(2,1)S(1)} %collective-permute-done.12.swapped), custom_call_target="tpu_custom_call" | custom-call | tf_op jit(solution)/shard_map/bottom_start/pallas_call | solution.py:462
  58.7 1.2 %collective-permute-start.15 = (bf16[72,768]{1,0:T(8,128)(2,1)S(1)}, bf16[72,768]{1,0:T(8,128)(2,1)S(1)}, u32[]{:S(2)}, u32[]{:S(2)}) collective-permute-start(bf16[72,768]{1,0:T(8,128)(2,1)S(1)} %bottom_start.1.refs_0_), channel_id=1, source_target_pairs={{0,3},{1,2},{2,1},{3,0},{4,7},{5,6},{6,5},{7,4},{8,11},{9,10},{10,... | collective-permute-start | bytes 331784 | tf_op jit(solution)/shard_map/ppermute | solution.py:612
  60.0 1.3 %collective-permute-start.14 = (bf16[72,768]{1,0:T(8,128)(2,1)S(1)}, bf16[72,768]{1,0:T(8,128)(2,1)S(1)}, u32[]{:S(2)}, u32[]{:S(2)}) collective-permute-start(bf16[72,768]{1,0:T(8,128)(2,1)S(1)} %bottom_start.1.refs_0_), channel_id=1, source_target_pairs={{0,2},{1,3},{2,0},{3,1},{4,6},{5,7},{6,4},{7,5},{8,10},{9,11},{10,... | collective-permute-start | bytes 331784 | tf_op jit(solution)/shard_map/ppermute | solution.py:612
  61.3 1.0 %collective-permute-start.13 = (bf16[72,768]{1,0:T(8,128)(2,1)S(1)}, bf16[72,768]{1,0:T(8,128)(2,1)S(1)}, u32[]{:S(2)}, u32[]{:S(2)}) collective-permute-start(bf16[72,768]{1,0:T(8,128)(2,1)S(1)} %bottom_start.1.refs_0_), channel_id=1, source_target_pairs={{0,1},{1,0},{2,3},{3,2},{4,5},{5,4},{6,7},{7,6},{8,9},{9,8},{10,11... | collective-permute-start | bytes 331784 | tf_op jit(solution)/shard_map/ppermute | solution.py:612
  62.3 3.3 %collective-permute-done.15.refs_3_ = bf16[72,768]{1,0:T(8,128)(2,1)S(1)} collective-permute-done((bf16[72,768]{1,0:T(8,128)(2,1)S(1)}, bf16[72,768]{1,0:T(8,128)(2,1)S(1)}, u32[]{:S(2)}, u32[]{:S(2)}) %collective-permute-start.15) | collective-permute-done | bytes 110624 | tf_op jit(solution)/shard_map/ppermute | solution.py:612
  65.6 1.2 %collective-permute-done.14.refs_2_ = bf16[72,768]{1,0:T(8,128)(2,1)S(1)} collective-permute-done((bf16[72,768]{1,0:T(8,128)(2,1)S(1)}, bf16[72,768]{1,0:T(8,128)(2,1)S(1)}, u32[]{:S(2)}, u32[]{:S(2)}) %collective-permute-start.14) | collective-permute-done | bytes 110624 | tf_op jit(solution)/shard_map/ppermute | solution.py:612
  66.9 0.0 collective-permute-done.13.refs_1_
  66.9 0.0 copy-start.11
  66.9 0.0 copy-start.12
  66.9 2.2 %bottom.1 = bf16[16,88,128]{2,1,0:T(8,128)(2,1)S(1)} custom-call(bf16[72,768]{1,0:T(8,128)(2,1)S(1)} %bottom_start.1.refs_0_, bf16[72,768]{1,0:T(8,128)(2,1)S(1)} %collective-permute-done.13.refs_1_, bf16[72,768]{1,0:T(8,128)(2,1)S(1)} %collective-permute-done.14.refs_2_, bf16[72,768]{1,0:T(8,128)(2,1)S(1)} %collective-permute-done.15.refs_3_, ...), custom_call_target="tpu_custom_call" | custom-call | tf_op jit(solution)/shard_map/bottom/pallas_call | solution.py:462
  69.1 0.0 copy-start.1
  69.1 0.0 copy-start.3
  69.1 0.0 copy-start.4
  69.1 15.2 %all_to_all.11.near = bf16[16,88,128]{2,1,0:T(8,128)(2,1)S(1)} all-to-all(bf16[16,88,128]{2,1,0:T(8,128)(2,1)S(1)} %bottom.1), channel_id=1, replica_groups=mesh['gx'=2,'yz'=16] {'yz'}, dimensions={0} | all-to-all | bytes 720896 | tf_op jit(solution)/shard_map/all_to_all | solution.py:629
  84.3 0.0 collective-permute-start.16
  84.3 1.7 %collective-permute-done.16.far = bf16[16,88,128]{2,1,0:T(8,128)(2,1)S(1)} collective-permute-done((bf16[16,88,128]{2,1,0:T(8,128)(2,1)S(1)}, bf16[16,88,128]{2,1,0:T(8,128)(2,1)S(1)}, u32[]{:S(2)}, u32[]{:S(2)}) %collective-permute-start.16) | collective-permute-done | bytes 360480 | tf_op jit(solution)/shard_map/ppermute | solution.py:630
  86.0 0.0 copy-done.1
  86.0 0.0 copy-done.3
  86.0 6.9 %decoder.1 = bf16[12,16,384]{2,1,0:T(8,128)(2,1)S(1)} custom-call(bf16[16,88,128]{2,1,0:T(8,128)(2,1)S(1)} %all_to_all.11.near, bf16[16,88,128]{2,1,0:T(8,128)(2,1)S(1)} %collective-permute-done.16.far, bf16[12,16,896]{2,1,0:T(8,128)(2,1)S(1)} %get-tuple-element.19.window, bf16[16,16,512]{2,1,0:T(8,128)(2,1)S(1)} %get-tuple-element.20.skip, ...), custom_call_target="tpu_custom_call" | custom-call | tf_op jit(solution)/shard_map/decoder/pallas_call | solution.py:462
  92.9 0.4 reshape.16
  93.4 0.1 copy.27
  93.5 0.2 reshape.17
  93.7 0.9 copy.23
  (27 shorter events, 0.2 us)
Async XLA Ops:
  0.0 12.5 %copy-start = (bf16[64,1728]{1,0:T(8,128)(2,1)S(1)}, bf16[64,1728]{1,0:T(8,128)(2,1)}, u32[]{:S(2)}) copy-start(bf16[64,1728]{1,0:T(8,128)(2,1)} %param.22) | copy-start | bytes 663556
  1.6 7.3 %collective-permute-start = (bf16[4,12,384]{2,1,0:T(8,128)(2,1)S(1)}, bf16[4,12,384]{2,1,0:T(8,128)(2,1)S(1)}, u32[]{:S(2)}, u32[]{:S(2)}) collective-permute-start(bf16[4,12,384]{2,1,0:T(8,128)(2,1)S(1)} %copy.19), channel_id=1, source_target_pairs={{0,4},{1,5},{2,6},{3,7},{4,8},{5,9},{6,10},{7,11},{8,12},{9,13},{1... | collective-permute-start | bytes 110600 | tf_op jit(solution)/shard_map/ppermute | solution.py:479
  4.9 4.5 %collective-permute-start.1 = (bf16[4,12,384]{2,1,0:T(8,128)(2,1)S(1)}, bf16[4,12,384]{2,1,0:T(8,128)(2,1)S(1)}, u32[]{:S(2)}, u32[]{:S(2)}) collective-permute-start(bf16[4,12,384]{2,1,0:T(8,128)(2,1)S(1)} %copy.21), channel_id=1, source_target_pairs={{0,12},{1,13},{2,14},{3,15},{4,0},{5,1},{6,2},{7,3},{8,4},{9,5},{1... | collective-permute-start | bytes 110600 | tf_op jit(solution)/shard_map/ppermute | solution.py:479
  9.5 5.4 %collective-permute-start.2 = (bf16[20,12,128]{2,1,0:T(8,128)(2,1)S(1)}, bf16[20,12,128]{2,1,0:T(8,128)(2,1)S(1)}, u32[]{:S(2)}, u32[]{:S(2)}) collective-permute-start(bf16[20,12,128]{2,1,0:T(8,128)(2,1)S(1)} %get-tuple-element.25), channel_id=1, source_target_pairs={{0,1},{1,2},{2,3},{3,0},{4,5},{5,6},{6,7},{7,4},{8,9},{9,10},{10,1... | collective-permute-start | bytes 184328 | tf_op jit(solution)/shard_map/ppermute | solution.py:479
  11.1 4.8 %collective-permute-start.3 = (bf16[20,12,128]{2,1,0:T(8,128)(2,1)S(1)}, bf16[20,12,128]{2,1,0:T(8,128)(2,1)S(1)}, u32[]{:S(2)}, u32[]{:S(2)}) collective-permute-start(bf16[20,12,128]{2,1,0:T(8,128)(2,1)S(1)} %get-tuple-element.26), channel_id=1, source_target_pairs={{0,3},{1,0},{2,1},{3,2},{4,7},{5,4},{6,5},{7,6},{8,11},{9,8},{10,9... | collective-permute-start | bytes 184328 | tf_op jit(solution)/shard_map/ppermute | solution.py:479
  12.5 10.1 %collective-permute-start.6 = (bf16[32,1728]{1,0:T(8,128)(2,1)S(1)}, bf16[32,1728]{1,0:T(8,128)(2,1)S(1)}, u32[]{:S(2)}, u32[]{:S(2)}) collective-permute-start(bf16[32,1728]{1,0:T(8,128)(2,1)S(1)} %constant_dynamic-slice_fusion), channel_id=1, source_target_pairs={{0,0},{1,4},{2,8},{3,12},{4,1},{5,5},{6,9},{7,13},{8,2},{9,6},{10,... | collective-permute-start | bytes 331784 | tf_op jit(solution)/shard_map/ppermute | solution.py:517
  16.0 1.6 %copy-start.8 = (bf16[32,864]{1,0:T(8,128)(2,1)S(1)}, bf16[32,864]{1,0:T(8,128)(2,1)}, u32[]{:S(2)}) copy-start(bf16[32,864]{1,0:T(8,128)(2,1)} %first.2) | copy-start | bytes 165892
  16.0 1.6 %copy-start.9 = (bf16[32,864]{1,0:T(8,128)(2,1)S(1)}, bf16[32,864]{1,0:T(8,128)(2,1)}, u32[]{:S(2)}) copy-start(bf16[32,864]{1,0:T(8,128)(2,1)} %second.2) | copy-start | bytes 165892
  16.0 1.6 %copy-start.13 = (bf16[64,256]{1,0:T(8,128)(2,1)S(1)}, bf16[64,256]{1,0:T(8,128)(2,1)}, u32[]{:S(2)}) copy-start(bf16[64,256]{1,0:T(8,128)(2,1)} %reduce.2) | copy-start | bytes 98308
  16.1 1.4 %collective-permute-start.5 = (bf16[20,4,640]{2,1,0:T(4,128)(2,1)S(1)}, bf16[20,4,640]{2,1,0:T(4,128)(2,1)S(1)}, u32[]{:S(2)}, u32[]{:S(2)}) collective-permute-start(bf16[20,4,640]{2,1,0:T(4,128)(2,1)S(1)} %get-tuple-element.23), channel_id=1, source_target_pairs={{0,16},{16,0},{1,17},{17,1},{2,18},{18,2},{3,19},{19,3},{4,20},{20... | collective-permute-start | bytes 307208 | tf_op jit(solution)/shard_map/ppermute | solution.py:479
  16.2 1.4 %collective-permute-start.4 = (bf16[20,4,640]{2,1,0:T(4,128)(2,1)S(1)}, bf16[20,4,640]{2,1,0:T(4,128)(2,1)S(1)}, u32[]{:S(2)}, u32[]{:S(2)}) collective-permute-start(bf16[20,4,640]{2,1,0:T(4,128)(2,1)S(1)} %get-tuple-element.24), channel_id=1, source_target_pairs={{0,16},{16,0},{1,17},{17,1},{2,18},{18,2},{3,19},{19,3},{4,20},{20... | collective-permute-start | bytes 307208 | tf_op jit(solution)/shard_map/ppermute | solution.py:479
  17.6 21.9 %copy-start.6 = (bf16[64,1728]{1,0:T(8,128)(2,1)S(1)}, bf16[64,1728]{1,0:T(8,128)(2,1)}, u32[]{:S(2)}) copy-start(bf16[64,1728]{1,0:T(8,128)(2,1)} %second.3) | copy-start | bytes 663556
  22.6 5.7 %collective-permute-start.7 = (bf16[30,384]{1,0:T(8,128)(2,1)S(1)}, bf16[30,384]{1,0:T(8,128)(2,1)S(1)}, u32[]{:S(2)}, u32[]{:S(2)}) collective-permute-start(bf16[30,384]{1,0:T(8,128)(2,1)S(1)} %get-tuple-element.27), channel_id=1, source_target_pairs={{0,4},{1,5},{2,6},{3,7},{4,8},{5,9},{6,10},{7,11},{8,12},{9,13},{1... | collective-permute-start | bytes 69128 | tf_op jit(solution)/shard_map/ppermute | solution.py:479
  23.8 4.6 %collective-permute-start.8 = (bf16[30,384]{1,0:T(8,128)(2,1)S(1)}, bf16[30,384]{1,0:T(8,128)(2,1)S(1)}, u32[]{:S(2)}, u32[]{:S(2)}) collective-permute-start(bf16[30,384]{1,0:T(8,128)(2,1)S(1)} %get-tuple-element.28), channel_id=1, source_target_pairs={{0,12},{1,13},{2,14},{3,15},{4,0},{5,1},{6,2},{7,3},{8,4},{9,5},{1... | collective-permute-start | bytes 69128 | tf_op jit(solution)/shard_map/ppermute | solution.py:479
  28.4 11.1 %copy-start.5 = (bf16[64,1728]{1,0:T(8,128)(2,1)S(1)}, bf16[64,1728]{1,0:T(8,128)(2,1)}, u32[]{:S(2)}) copy-start(bf16[64,1728]{1,0:T(8,128)(2,1)} %first.3) | copy-start | bytes 663556
  28.4 11.1 %copy-start.2 = (bf16[256,512]{1,0:T(8,128)(2,1)S(1)}, bf16[256,512]{1,0:T(8,128)(2,1)}, u32[]{:S(2)}) copy-start(bf16[256,512]{1,0:T(8,128)(2,1)} %reduce.3) | copy-start | bytes 786436
  28.4 6.3 %collective-permute-start.10 = (bf16[96,384]{1,0:T(8,128)(2,1)S(1)}, bf16[96,384]{1,0:T(8,128)(2,1)S(1)}, u32[]{:S(2)}, u32[]{:S(2)}) collective-permute-start(bf16[96,384]{1,0:T(8,128)(2,1)S(1)} %pad_maximum_fusion.2), channel_id=1, source_target_pairs={{0,3},{1,0},{2,1},{3,2},{4,7},{5,4},{6,5},{7,6},{8,11},{9,8},{10,9... | collective-permute-start | bytes 221192 | tf_op jit(solution)/shard_map/ppermute | solution.py:479
  32.7 5.3 %collective-permute-start.9 = (bf16[96,384]{1,0:T(8,128)(2,1)S(1)}, bf16[96,384]{1,0:T(8,128)(2,1)S(1)}, u32[]{:S(2)}, u32[]{:S(2)}) collective-permute-start(bf16[96,384]{1,0:T(8,128)(2,1)S(1)} %pad_maximum_fusion.2), channel_id=1, source_target_pairs={{0,1},{1,2},{2,3},{3,0},{4,5},{5,6},{6,7},{7,4},{8,9},{9,10},{10,1... | collective-permute-start | bytes 221192 | tf_op jit(solution)/shard_map/ppermute | solution.py:479
  38.0 1.5 %collective-permute-start.11 = (bf16[96,1152]{1,0:T(8,128)(2,1)S(1)}, bf16[96,1152]{1,0:T(8,128)(2,1)S(1)}, u32[]{:S(2)}, u32[]{:S(2)}) collective-permute-start(bf16[96,1152]{1,0:T(8,128)(2,1)S(1)} %pad_maximum_fusion.1.own), channel_id=1, source_target_pairs={{0,16},{16,0},{1,17},{17,1},{2,18},{18,2},{3,19},{19,3},{4,20},{20... | collective-permute-start | bytes 663560 | tf_op jit(solution)/shard_map/ppermute | solution.py:567
  38.1 6.8 %collective-permute-start.12 = (bf16[32,1728]{1,0:T(8,128)(2,1)S(1)}, bf16[32,1728]{1,0:T(8,128)(2,1)S(1)}, u32[]{:S(2)}, u32[]{:S(2)}) collective-permute-start(bf16[32,1728]{1,0:T(8,128)(2,1)S(1)} %collective-permute-done.6.turned), channel_id=1, source_target_pairs={{0,16},{16,0},{1,17},{17,1},{2,18},{18,2},{3,19},{19,3},{4,20},{20... | collective-permute-start | bytes 331784 | tf_op jit(solution)/shard_map/ppermute | solution.py:561
  56.8 10.1 %copy-start.7 = (bf16[64,1728]{1,0:T(8,128)(2,1)S(1)}, bf16[64,1728]{1,0:T(8,128)(2,1)}, u32[]{:S(2)}) copy-start(bf16[64,1728]{1,0:T(8,128)(2,1)} %refs_4_.1) | copy-start | bytes 663556
  58.7 6.9 %collective-permute-start.15 = (bf16[72,768]{1,0:T(8,128)(2,1)S(1)}, bf16[72,768]{1,0:T(8,128)(2,1)S(1)}, u32[]{:S(2)}, u32[]{:S(2)}) collective-permute-start(bf16[72,768]{1,0:T(8,128)(2,1)S(1)} %bottom_start.1.refs_0_), channel_id=1, source_target_pairs={{0,3},{1,2},{2,1},{3,0},{4,7},{5,6},{6,5},{7,4},{8,11},{9,10},{10,... | collective-permute-start | bytes 331784 | tf_op jit(solution)/shard_map/ppermute | solution.py:612
  60.0 6.9 %collective-permute-start.14 = (bf16[72,768]{1,0:T(8,128)(2,1)S(1)}, bf16[72,768]{1,0:T(8,128)(2,1)S(1)}, u32[]{:S(2)}, u32[]{:S(2)}) collective-permute-start(bf16[72,768]{1,0:T(8,128)(2,1)S(1)} %bottom_start.1.refs_0_), channel_id=1, source_target_pairs={{0,2},{1,3},{2,0},{3,1},{4,6},{5,7},{6,4},{7,5},{8,10},{9,11},{10,... | collective-permute-start | bytes 331784 | tf_op jit(solution)/shard_map/ppermute | solution.py:612
  61.3 5.6 %collective-permute-start.13 = (bf16[72,768]{1,0:T(8,128)(2,1)S(1)}, bf16[72,768]{1,0:T(8,128)(2,1)S(1)}, u32[]{:S(2)}, u32[]{:S(2)}) collective-permute-start(bf16[72,768]{1,0:T(8,128)(2,1)S(1)} %bottom_start.1.refs_0_), channel_id=1, source_target_pairs={{0,1},{1,0},{2,3},{3,2},{4,5},{5,4},{6,7},{7,6},{8,9},{9,8},{10,11... | collective-permute-start | bytes 331784 | tf_op jit(solution)/shard_map/ppermute | solution.py:612
  66.9 19.1 %copy-start.10 = (bf16[32,864]{1,0:T(8,128)(2,1)S(1)}, bf16[32,864]{1,0:T(8,128)(2,1)}, u32[]{:S(2)}) copy-start(bf16[32,864]{1,0:T(8,128)(2,1)} %f1.1) | copy-start | bytes 165892
  66.9 19.1 %copy-start.11 = (bf16[32,864]{1,0:T(8,128)(2,1)S(1)}, bf16[32,864]{1,0:T(8,128)(2,1)}, u32[]{:S(2)}) copy-start(bf16[32,864]{1,0:T(8,128)(2,1)} %f2.1) | copy-start | bytes 165892
  66.9 19.1 %copy-start.12 = (bf16[64,256]{1,0:T(8,128)(2,1)S(1)}, bf16[64,256]{1,0:T(8,128)(2,1)}, u32[]{:S(2)}) copy-start(bf16[64,256]{1,0:T(8,128)(2,1)} %up_fine.1) | copy-start | bytes 98308
  69.1 16.9 %copy-start.1 = (bf16[256,512]{1,0:T(8,128)(2,1)S(1)}, bf16[256,512]{1,0:T(8,128)(2,1)}, u32[]{:S(2)}) copy-start(bf16[256,512]{1,0:T(8,128)(2,1)} %up.1) | copy-start | bytes 786436
  69.1 16.9 %copy-start.3 = (bf16[64,1728]{1,0:T(8,128)(2,1)S(1)}, bf16[64,1728]{1,0:T(8,128)(2,1)}, u32[]{:S(2)}) copy-start(bf16[64,1728]{1,0:T(8,128)(2,1)} %m1.1) | copy-start | bytes 663556
  69.1 16.9 %copy-start.4 = (bf16[64,1728]{1,0:T(8,128)(2,1)S(1)}, bf16[64,1728]{1,0:T(8,128)(2,1)}, u32[]{:S(2)}) copy-start(bf16[64,1728]{1,0:T(8,128)(2,1)} %m2.1) | copy-start | bytes 663556
  84.3 1.7 %collective-permute-start.16 = (bf16[16,88,128]{2,1,0:T(8,128)(2,1)S(1)}, bf16[16,88,128]{2,1,0:T(8,128)(2,1)S(1)}, u32[]{:S(2)}, u32[]{:S(2)}) collective-permute-start(bf16[16,88,128]{2,1,0:T(8,128)(2,1)S(1)} %all_to_all.11.near), channel_id=1, source_target_pairs={{0,16},{16,0},{1,17},{17,1},{2,18},{18,2},{3,19},{19,3},{4,20},{20... | collective-permute-start | bytes 1081352 | tf_op jit(solution)/shard_map/ppermute | solution.py:630

commit v2 on v1

--- a/solution.py
+++ b/solution.py
@@ -48,7 +48,8 @@
             for row, block in blocks(
                 taps, DEPTH // channels, channels, channels, lambda z, k: z - k
             ):
-                table[3 * dy + dx, row : row + channels, :] = block
+                row += DEPTH * dx
+                table[row : row + channels, span_of(dy)] = block
 
 
 def shrink_table(table, flat, weight, channels, offset):
@@ -87,14 +88,12 @@
     height = layers * rows
     start = tile * LANES
     left = jnp.concatenate(
-        [
-            shifted[dx, dy * rows : dy * rows + height, start : start + depth]
-            for dy in range(3)
-            for dx in range(3)
-        ],
-        axis=1,
-    )
-    return dot(left, table[:, :depth, :].reshape(9 * depth, LANES))
+        [shifted[dx, 0 : height + 2 * rows, start : start + depth] for dx in range(3)], axis=1
+    )
+    right = jnp.concatenate([table[DEPTH * dx : DEPTH * dx + depth, :] for dx in range(3)], axis=0)
+    pair = dot(left[: height + rows], right[:, : 2 * LANES])
+    last = dot(left[2 * rows :], right[:, 2 * LANES :])
+    return pair[:height, :LANES] + pair[rows:, LANES:] + last
 
 
 def rounded_relu(value):
@@ -530,7 +529,7 @@
     seen = ext + 2 * halo
     side = ext // 2
     flat = pltpu.VMEM((27 * mid, LANES), F32)
-    table = pltpu.VMEM((9, DEPTH, LANES), BF)
+    table = pltpu.VMEM((3 * DEPTH, 3 * LANES), BF)
     down = pltpu.VMEM((2 * DEPTH, 2 * LANES), BF)
     skip, small = call(
         fine_encoder,

time: 94.9 us -> 90.8 us (0.957)
  Pallas kernels: 21.3 us -> 17.2 us
    pallas_call x5, Pallas kernels: 21.3 us -> 17.2 us  [call(): pl.pallas_call(kernel, out_shape=jax.tree.map(lambda out: pltpu.VMEM(out....]
  transfers between devices with their start and end apart: 17 -> 17, of which waited for: 13 -> 13; matrix products, arithmetic and copies ran while one was open for 1% -> 1% of each run, Pallas kernels for 11% -> 9%
where the time goes in v2:
time: 90.8 us; the launch traced here: 90.6 us
  blocking collectives  27.2 us (30%)
  starting transfers between devices  21.7 us (24%)
  waiting for transfers between devices  20 us (22%)
  Pallas kernels  17.2 us (19%)
  local copies, waits for them, and re-layouts  4.13 us (5%)
    pallas_call x5, Pallas kernels, call(): pl.pallas_call(kernel, out_shape=jax.tree.map(lambda out: pltpu.VMEM(out....  17.2 us
    ppermute x10, starting transfers between devices, exchange(): return (lax.ppermute(tail, axis, ahead), lax.ppermute(head, axis, back))  16.9 us
    all_to_all x1, blocking collectives, gathered_body(): near = lax.all_to_all(sent, 'yz', 0, 0)  15.2 us
    ppermute x10, waiting for transfers between devices, exchange(): return (lax.ppermute(tail, axis, ahead), lax.ppermute(head, axis, back))  12.8 us
    all_to_all x1, blocking collectives, gathered_body(): gathered = lax.all_to_all(sent, ('gx', 'yz'), 0, 0)  12 us
    ppermute x3, waiting for transfers between devices, gathered_body(): lax.ppermute(partial, 'yz', [(s, s ^ turn) for s in range(devices)])  4.59 us
    ppermute x3, starting transfers between devices, gathered_body(): lax.ppermute(partial, 'yz', [(s, s ^ turn) for s in range(devices)])  3.55 us
  transfers between devices with their start and end apart: 17, of which 13 were waited for; matrix products, arithmetic and copies ran while one was open for 1% of the time, Pallas kernels for 9%

profile of v2, /device:TPU:0, one launch (start us, length us, event | category | flops | bytes accessed | tf_op | source)
XLA Modules:
  0.0 90.6 jit_solution(11076539873439077466)
XLA Ops:
  0.0 1.2 %copy.18 = bf16[1,32,12,144]{1,3,2,0:T(8,128)(2,1)S(1)} copy(bf16[1,32,12,144]{3,1,2,0:T(8,128)(2,1)} %param.15) | data formatting | bytes 221184 | tf_op args[0]
  1.2 0.1 reshape.14
  1.4 0.2 slice.34
  1.6 3.1 %collective-permute-start = (bf16[4,12,384]{2,1,0:T(8,128)(2,1)S(1)}, bf16[4,12,384]{2,1,0:T(8,128)(2,1)S(1)}, u32[]{:S(2)}, u32[]{:S(2)}) collective-permute-start(bf16[4,12,384]{2,1,0:T(8,128)(2,1)S(1)} %copy.19), channel_id=1, source_target_pairs={{0,4},{1,5},{2,6},{3,7},{4,8},{5,9},{6,10},{7,11},{8,12},{9,13},{1... | collective-permute-start | bytes 110600 | tf_op jit(solution)/shard_map/ppermute | solution.py:478
  4.7 0.2 slice.36
  4.9 2.1 %collective-permute-start.1 = (bf16[4,12,384]{2,1,0:T(8,128)(2,1)S(1)}, bf16[4,12,384]{2,1,0:T(8,128)(2,1)S(1)}, u32[]{:S(2)}, u32[]{:S(2)}) collective-permute-start(bf16[4,12,384]{2,1,0:T(8,128)(2,1)S(1)} %copy.21), channel_id=1, source_target_pairs={{0,12},{1,13},{2,14},{3,15},{4,0},{5,1},{6,2},{7,3},{8,4},{9,5},{1... | collective-permute-start | bytes 110600 | tf_op jit(solution)/shard_map/ppermute | solution.py:478
  7.0 0.4 reshape.18
  7.4 1.5 %collective-permute-done = bf16[4,12,384]{2,1,0:T(8,128)(2,1)S(1)} collective-permute-done((bf16[4,12,384]{2,1,0:T(8,128)(2,1)S(1)}, bf16[4,12,384]{2,1,0:T(8,128)(2,1)S(1)}, u32[]{:S(2)}, u32[]{:S(2)}) %collective-permute-start) | collective-permute-done | bytes 36896 | tf_op jit(solution)/shard_map/ppermute | solution.py:478
  8.9 0.5 collective-permute-done.1
  9.5 1.7 %collective-permute-start.2 = (bf16[20,12,128]{2,1,0:T(8,128)(2,1)S(1)}, bf16[20,12,128]{2,1,0:T(8,128)(2,1)S(1)}, u32[]{:S(2)}, u32[]{:S(2)}) collective-permute-start(bf16[20,12,128]{2,1,0:T(8,128)(2,1)S(1)} %get-tuple-element.25), channel_id=1, source_target_pairs={{0,1},{1,2},{2,3},{3,0},{4,5},{5,6},{6,7},{7,4},{8,9},{9,10},{10,1... | collective-permute-start | bytes 184328 | tf_op jit(solution)/shard_map/ppermute | solution.py:478
  11.1 1.3 %collective-permute-start.3 = (bf16[20,12,128]{2,1,0:T(8,128)(2,1)S(1)}, bf16[20,12,128]{2,1,0:T(8,128)(2,1)S(1)}, u32[]{:S(2)}, u32[]{:S(2)}) collective-permute-start(bf16[20,12,128]{2,1,0:T(8,128)(2,1)S(1)} %get-tuple-element.26), channel_id=1, source_target_pairs={{0,3},{1,0},{2,1},{3,2},{4,7},{5,4},{6,5},{7,6},{8,11},{9,8},{10,9... | collective-permute-start | bytes 184328 | tf_op jit(solution)/shard_map/ppermute | solution.py:478
  12.5 0.7 collective-permute-start.6
  13.1 1.7 %collective-permute-done.2 = bf16[20,12,128]{2,1,0:T(8,128)(2,1)S(1)} collective-permute-done((bf16[20,12,128]{2,1,0:T(8,128)(2,1)S(1)}, bf16[20,12,128]{2,1,0:T(8,128)(2,1)S(1)}, u32[]{:S(2)}, u32[]{:S(2)}) %collective-permute-start.2) | collective-permute-done | bytes 61472 | tf_op jit(solution)/shard_map/ppermute | solution.py:478
  14.9 1.0 %collective-permute-done.3 = bf16[20,12,128]{2,1,0:T(8,128)(2,1)S(1)} collective-permute-done((bf16[20,12,128]{2,1,0:T(8,128)(2,1)S(1)}, bf16[20,12,128]{2,1,0:T(8,128)(2,1)S(1)}, u32[]{:S(2)}, u32[]{:S(2)}) %collective-permute-start.3) | collective-permute-done | bytes 61472 | tf_op jit(solution)/shard_map/ppermute | solution.py:478
  15.9 0.1 pad_maximum_fusion.mid
  16.0 0.0 copy-start.8
  16.0 0.0 copy-start.9
  16.0 0.0 copy-start.13
  16.0 0.1 fusion.1
  16.1 0.1 collective-permute-start.5
  16.2 0.5 collective-permute-start.4
  16.7 0.8 collective-permute-done.5.high
  17.5 0.2 collective-permute-done.4.low
  17.6 3.8 %fine_encoder.1 = (bf16[16,16,512]{2,1,0:T(8,128)(2,1)S(1)}, bf16[36,384]{1,0:T(8,128)(2,1)S(1)}) custom-call(bf16[20,4,640]{2,1,0:T(4,128)(2,1)S(1)} %collective-permute-done.4.low, bf16[20,12,640]{2,1,0:T(8,128)(2,1)S(1)} %pad_maximum_fusion.mid, bf16[20,4,640]{2,1,0:T(4,128)(2,1)S(1)} %collective-permute-done.5.high, bf16[32,864]{1,0:T(8,128)(2,1)S(1)} %copy-done.8, ...), custom_call_target="tpu_custom_call" | custom-call | tf_op jit(solution)/shard_map/fine_encoder/pallas_call | solution.py:461
  21.4 0.0 collective-permute-done.6.turned
  21.4 1.4 %collective-permute-start.7 = (bf16[30,384]{1,0:T(8,128)(2,1)S(1)}, bf16[30,384]{1,0:T(8,128)(2,1)S(1)}, u32[]{:S(2)}, u32[]{:S(2)}) collective-permute-start(bf16[30,384]{1,0:T(8,128)(2,1)S(1)} %get-tuple-element.27), channel_id=1, source_target_pairs={{0,4},{1,5},{2,6},{3,7},{4,8},{5,9},{6,10},{7,11},{8,12},{9,13},{1... | collective-permute-start | bytes 69128 | tf_op jit(solution)/shard_map/ppermute | solution.py:478
  22.8 3.5 %collective-permute-start.8 = (bf16[30,384]{1,0:T(8,128)(2,1)S(1)}, bf16[30,384]{1,0:T(8,128)(2,1)S(1)}, u32[]{:S(2)}, u32[]{:S(2)}) collective-permute-start(bf16[30,384]{1,0:T(8,128)(2,1)S(1)} %get-tuple-element.28), channel_id=1, source_target_pairs={{0,12},{1,13},{2,14},{3,15},{4,0},{5,1},{6,2},{7,3},{8,4},{9,5},{1... | collective-permute-start | bytes 69128 | tf_op jit(solution)/shard_map/ppermute | solution.py:478
  26.3 1.9 %collective-permute-done.7 = bf16[30,384]{1,0:T(8,128)(2,1)S(1)} collective-permute-done((bf16[30,384]{1,0:T(8,128)(2,1)S(1)}, bf16[30,384]{1,0:T(8,128)(2,1)S(1)}, u32[]{:S(2)}, u32[]{:S(2)}) %collective-permute-start.7) | collective-permute-done | bytes 23072 | tf_op jit(solution)/shard_map/ppermute | solution.py:478
  28.2 0.0 collective-permute-done.8
  28.2 0.0 copy-start.2
  28.3 3.2 %collective-permute-start.10 = (bf16[96,384]{1,0:T(8,128)(2,1)S(1)}, bf16[96,384]{1,0:T(8,128)(2,1)S(1)}, u32[]{:S(2)}, u32[]{:S(2)}) collective-permute-start(bf16[96,384]{1,0:T(8,128)(2,1)S(1)} %pad_maximum_fusion.2), channel_id=1, source_target_pairs={{0,3},{1,0},{2,1},{3,2},{4,7},{5,4},{6,5},{7,6},{8,11},{9,8},{10,9... | collective-permute-start | bytes 221192 | tf_op jit(solution)/shard_map/ppermute | solution.py:478
  31.5 0.0 collective-permute-start.9
  31.5 2.0 %collective-permute-done.10 = bf16[96,384]{1,0:T(8,128)(2,1)S(1)} collective-permute-done((bf16[96,384]{1,0:T(8,128)(2,1)S(1)}, bf16[96,384]{1,0:T(8,128)(2,1)S(1)}, u32[]{:S(2)}, u32[]{:S(2)}) %collective-permute-start.10) | collective-permute-done | bytes 73760 | tf_op jit(solution)/shard_map/ppermute | solution.py:478
  33.5 3.3 %collective-permute-done.9 = bf16[96,384]{1,0:T(8,128)(2,1)S(1)} collective-permute-done((bf16[96,384]{1,0:T(8,128)(2,1)S(1)}, bf16[96,384]{1,0:T(8,128)(2,1)S(1)}, u32[]{:S(2)}, u32[]{:S(2)}) %collective-permute-start.9) | collective-permute-done | bytes 73760 | tf_op jit(solution)/shard_map/ppermute | solution.py:478
  36.8 0.1 collective-permute-start.11
  36.8 0.5 collective-permute-start.12
  37.3 1.0 %collective-permute-done.11.other = bf16[96,1152]{1,0:T(8,128)(2,1)S(1)} collective-permute-done((bf16[96,1152]{1,0:T(8,128)(2,1)S(1)}, bf16[96,1152]{1,0:T(8,128)(2,1)S(1)}, u32[]{:S(2)}, u32[]{:S(2)}) %collective-permute-start.11) | collective-permute-done | bytes 221216 | tf_op jit(solution)/shard_map/ppermute | solution.py:566
  38.3 4.0 %middle.1 = (bf16[12,16,896]{2,1,0:T(8,128)(2,1)S(1)}, bf16[32,16,128]{2,1,0:T(8,128)(2,1)S(1)}) custom-call(bf16[96,1152]{1,0:T(8,128)(2,1)S(1)} %pad_maximum_fusion.1.own, bf16[96,1152]{1,0:T(8,128)(2,1)S(1)} %collective-permute-done.11.other, bf16[64,1728]{1,0:T(8,128)(2,1)S(1)} %copy-done.5, bf16[64,1728]{1,0:T(8,128)(2,1)S(1)} %copy-done.6, ...), custom_call_target="tpu_custom_call" | custom-call | tf_op jit(solution)/shard_map/middle/pallas_call | solution.py:461
  42.4 0.0 collective-permute-done.12.swapped
  42.4 12.0 %all_to_all.10.gathered = bf16[32,16,128]{2,1,0:T(8,128)(2,1)S(1)} all-to-all(bf16[32,16,128]{2,1,0:T(8,128)(2,1)S(1)} %get-tuple-element.17), channel_id=1, replica_groups=mesh['gx'=2,'yz'=16] {'gx','yz'}, dimensions={0} | all-to-all | bytes 262144 | tf_op jit(solution)/shard_map/all_to_all | solution.py:594
  54.3 1.6 %bottom_start.1.refs_0_ = bf16[72,768]{1,0:T(8,128)(2,1)S(1)} custom-call(bf16[32,16,128]{2,1,0:T(8,128)(2,1)S(1)} %all_to_all.10.gathered, bf16[32,1728]{1,0:T(8,128)(2,1)S(1)} %collective-permute-done.6.turned, bf16[32,1728]{1,0:T(8,128)(2,1)S(1)} %collective-permute-done.12.swapped), custom_call_target="tpu_custom_call" | custom-call | tf_op jit(solution)/shard_map/bottom_start/pallas_call | solution.py:461
  55.9 1.2 %collective-permute-start.15 = (bf16[72,768]{1,0:T(8,128)(2,1)S(1)}, bf16[72,768]{1,0:T(8,128)(2,1)S(1)}, u32[]{:S(2)}, u32[]{:S(2)}) collective-permute-start(bf16[72,768]{1,0:T(8,128)(2,1)S(1)} %bottom_start.1.refs_0_), channel_id=1, source_target_pairs={{0,3},{1,2},{2,1},{3,0},{4,7},{5,6},{6,5},{7,4},{8,11},{9,10},{10,... | collective-permute-start | bytes 331784 | tf_op jit(solution)/shard_map/ppermute | solution.py:611
  57.2 1.4 %collective-permute-start.14 = (bf16[72,768]{1,0:T(8,128)(2,1)S(1)}, bf16[72,768]{1,0:T(8,128)(2,1)S(1)}, u32[]{:S(2)}, u32[]{:S(2)}) collective-permute-start(bf16[72,768]{1,0:T(8,128)(2,1)S(1)} %bottom_start.1.refs_0_), channel_id=1, source_target_pairs={{0,2},{1,3},{2,0},{3,1},{4,6},{5,7},{6,4},{7,5},{8,10},{9,11},{10,... | collective-permute-start | bytes 331784 | tf_op jit(solution)/shard_map/ppermute | solution.py:611
  58.5 1.0 %collective-permute-start.13 = (bf16[72,768]{1,0:T(8,128)(2,1)S(1)}, bf16[72,768]{1,0:T(8,128)(2,1)S(1)}, u32[]{:S(2)}, u32[]{:S(2)}) collective-permute-start(bf16[72,768]{1,0:T(8,128)(2,1)S(1)} %bottom_start.1.refs_0_), channel_id=1, source_target_pairs={{0,1},{1,0},{2,3},{3,2},{4,5},{5,4},{6,7},{7,6},{8,9},{9,8},{10,11... | collective-permute-start | bytes 331784 | tf_op jit(solution)/shard_map/ppermute | solution.py:611
  59.5 3.3 %collective-permute-done.15.refs_3_ = bf16[72,768]{1,0:T(8,128)(2,1)S(1)} collective-permute-done((bf16[72,768]{1,0:T(8,128)(2,1)S(1)}, bf16[72,768]{1,0:T(8,128)(2,1)S(1)}, u32[]{:S(2)}, u32[]{:S(2)}) %collective-permute-start.15) | collective-permute-done | bytes 110624 | tf_op jit(solution)/shard_map/ppermute | solution.py:611
  62.8 1.2 %collective-permute-done.14.refs_2_ = bf16[72,768]{1,0:T(8,128)(2,1)S(1)} collective-permute-done((bf16[72,768]{1,0:T(8,128)(2,1)S(1)}, bf16[72,768]{1,0:T(8,128)(2,1)S(1)}, u32[]{:S(2)}, u32[]{:S(2)}) %collective-permute-start.14) | collective-permute-done | bytes 110624 | tf_op jit(solution)/shard_map/ppermute | solution.py:611
  64.1 0.0 collective-permute-done.13.refs_1_
  64.1 0.0 copy-start.11
  64.1 0.0 copy-start.12
  64.1 1.8 %bottom.1 = bf16[16,88,128]{2,1,0:T(8,128)(2,1)S(1)} custom-call(bf16[72,768]{1,0:T(8,128)(2,1)S(1)} %bottom_start.1.refs_0_, bf16[72,768]{1,0:T(8,128)(2,1)S(1)} %collective-permute-done.13.refs_1_, bf16[72,768]{1,0:T(8,128)(2,1)S(1)} %collective-permute-done.14.refs_2_, bf16[72,768]{1,0:T(8,128)(2,1)S(1)} %collective-permute-done.15.refs_3_, ...), custom_call_target="tpu_custom_call" | custom-call | tf_op jit(solution)/shard_map/bottom/pallas_call | solution.py:461
  65.9 0.0 copy-start.1
  65.9 0.0 copy-start.3
  65.9 0.0 copy-start.4
  65.9 15.2 %all_to_all.11.near = bf16[16,88,128]{2,1,0:T(8,128)(2,1)S(1)} all-to-all(bf16[16,88,128]{2,1,0:T(8,128)(2,1)S(1)} %bottom.1), channel_id=1, replica_groups=mesh['gx'=2,'yz'=16] {'yz'}, dimensions={0} | all-to-all | bytes 720896 | tf_op jit(solution)/shard_map/all_to_all | solution.py:628
  81.1 0.0 collective-permute-start.16
  81.1 1.7 %collective-permute-done.16.far = bf16[16,88,128]{2,1,0:T(8,128)(2,1)S(1)} collective-permute-done((bf16[16,88,128]{2,1,0:T(8,128)(2,1)S(1)}, bf16[16,88,128]{2,1,0:T(8,128)(2,1)S(1)}, u32[]{:S(2)}, u32[]{:S(2)}) %collective-permute-start.16) | collective-permute-done | bytes 360480 | tf_op jit(solution)/shard_map/ppermute | solution.py:629
  82.8 0.0 copy-done.1
  82.8 0.0 copy-done.3
  82.8 0.0 copy-done.4
  82.8 6.1 %decoder.1 = bf16[12,16,384]{2,1,0:T(8,128)(2,1)S(1)} custom-call(bf16[16,88,128]{2,1,0:T(8,128)(2,1)S(1)} %all_to_all.11.near, bf16[16,88,128]{2,1,0:T(8,128)(2,1)S(1)} %collective-permute-done.16.far, bf16[12,16,896]{2,1,0:T(8,128)(2,1)S(1)} %get-tuple-element.19.window, bf16[16,16,512]{2,1,0:T(8,128)(2,1)S(1)} %get-tuple-element.20.skip, ...), custom_call_target="tpu_custom_call" | custom-call | tf_op jit(solution)/shard_map/decoder/pallas_call | solution.py:461
  88.9 0.4 reshape.16
  89.4 0.1 copy.27
  89.5 0.2 reshape.17
  89.7 0.9 %copy.23 = bf16[1,32,12,144]{3,1,2,0:T(8,128)(2,1)} copy(bf16[1,32,12,144]{1,3,2,0:T(8,128)(2,1)S(1)} %reshape.17) | data formatting | bytes 221184 | tf_op jit(solution)/shard_map/reshape | solution.py:655
  (27 shorter events, 0.2 us)
Async XLA Ops:
  0.0 12.5 %copy-start = (bf16[64,1728]{1,0:T(8,128)(2,1)S(1)}, bf16[64,1728]{1,0:T(8,128)(2,1)}, u32[]{:S(2)}) copy-start(bf16[64,1728]{1,0:T(8,128)(2,1)} %param.22) | copy-start | bytes 663556
  1.6 7.3 %collective-permute-start = (bf16[4,12,384]{2,1,0:T(8,128)(2,1)S(1)}, bf16[4,12,384]{2,1,0:T(8,128)(2,1)S(1)}, u32[]{:S(2)}, u32[]{:S(2)}) collective-permute-start(bf16[4,12,384]{2,1,0:T(8,128)(2,1)S(1)} %copy.19), channel_id=1, source_target_pairs={{0,4},{1,5},{2,6},{3,7},{4,8},{5,9},{6,10},{7,11},{8,12},{9,13},{1... | collective-permute-start | bytes 110600 | tf_op jit(solution)/shard_map/ppermute | solution.py:478
  4.9 4.5 %collective-permute-start.1 = (bf16[4,12,384]{2,1,0:T(8,128)(2,1)S(1)}, bf16[4,12,384]{2,1,0:T(8,128)(2,1)S(1)}, u32[]{:S(2)}, u32[]{:S(2)}) collective-permute-start(bf16[4,12,384]{2,1,0:T(8,128)(2,1)S(1)} %copy.21), channel_id=1, source_target_pairs={{0,12},{1,13},{2,14},{3,15},{4,0},{5,1},{6,2},{7,3},{8,4},{9,5},{1... | collective-permute-start | bytes 110600 | tf_op jit(solution)/shard_map/ppermute | solution.py:478
  9.5 5.4 %collective-permute-start.2 = (bf16[20,12,128]{2,1,0:T(8,128)(2,1)S(1)}, bf16[20,12,128]{2,1,0:T(8,128)(2,1)S(1)}, u32[]{:S(2)}, u32[]{:S(2)}) collective-permute-start(bf16[20,12,128]{2,1,0:T(8,128)(2,1)S(1)} %get-tuple-element.25), channel_id=1, source_target_pairs={{0,1},{1,2},{2,3},{3,0},{4,5},{5,6},{6,7},{7,4},{8,9},{9,10},{10,1... | collective-permute-start | bytes 184328 | tf_op jit(solution)/shard_map/ppermute | solution.py:478
  11.1 4.8 %collective-permute-start.3 = (bf16[20,12,128]{2,1,0:T(8,128)(2,1)S(1)}, bf16[20,12,128]{2,1,0:T(8,128)(2,1)S(1)}, u32[]{:S(2)}, u32[]{:S(2)}) collective-permute-start(bf16[20,12,128]{2,1,0:T(8,128)(2,1)S(1)} %get-tuple-element.26), channel_id=1, source_target_pairs={{0,3},{1,0},{2,1},{3,2},{4,7},{5,4},{6,5},{7,6},{8,11},{9,8},{10,9... | collective-permute-start | bytes 184328 | tf_op jit(solution)/shard_map/ppermute | solution.py:478
  12.5 8.9 %collective-permute-start.6 = (bf16[32,1728]{1,0:T(8,128)(2,1)S(1)}, bf16[32,1728]{1,0:T(8,128)(2,1)S(1)}, u32[]{:S(2)}, u32[]{:S(2)}) collective-permute-start(bf16[32,1728]{1,0:T(8,128)(2,1)S(1)} %constant_dynamic-slice_fusion), channel_id=1, source_target_pairs={{0,0},{1,4},{2,8},{3,12},{4,1},{5,5},{6,9},{7,13},{8,2},{9,6},{10,... | collective-permute-start | bytes 331784 | tf_op jit(solution)/shard_map/ppermute | solution.py:516
  16.0 1.6 %copy-start.8 = (bf16[32,864]{1,0:T(8,128)(2,1)S(1)}, bf16[32,864]{1,0:T(8,128)(2,1)}, u32[]{:S(2)}) copy-start(bf16[32,864]{1,0:T(8,128)(2,1)} %first.2) | copy-start | bytes 165892
  16.0 1.6 %copy-start.9 = (bf16[32,864]{1,0:T(8,128)(2,1)S(1)}, bf16[32,864]{1,0:T(8,128)(2,1)}, u32[]{:S(2)}) copy-start(bf16[32,864]{1,0:T(8,128)(2,1)} %second.2) | copy-start | bytes 165892
  16.0 1.6 %copy-start.13 = (bf16[64,256]{1,0:T(8,128)(2,1)S(1)}, bf16[64,256]{1,0:T(8,128)(2,1)}, u32[]{:S(2)}) copy-start(bf16[64,256]{1,0:T(8,128)(2,1)} %reduce.2) | copy-start | bytes 98308
  16.1 1.4 %collective-permute-start.5 = (bf16[20,4,640]{2,1,0:T(4,128)(2,1)S(1)}, bf16[20,4,640]{2,1,0:T(4,128)(2,1)S(1)}, u32[]{:S(2)}, u32[]{:S(2)}) collective-permute-start(bf16[20,4,640]{2,1,0:T(4,128)(2,1)S(1)} %get-tuple-element.23), channel_id=1, source_target_pairs={{0,16},{16,0},{1,17},{17,1},{2,18},{18,2},{3,19},{19,3},{4,20},{20... | collective-permute-start | bytes 307208 | tf_op jit(solution)/shard_map/ppermute | solution.py:478
  16.2 1.4 %collective-permute-start.4 = (bf16[20,4,640]{2,1,0:T(4,128)(2,1)S(1)}, bf16[20,4,640]{2,1,0:T(4,128)(2,1)S(1)}, u32[]{:S(2)}, u32[]{:S(2)}) collective-permute-start(bf16[20,4,640]{2,1,0:T(4,128)(2,1)S(1)} %get-tuple-element.24), channel_id=1, source_target_pairs={{0,16},{16,0},{1,17},{17,1},{2,18},{18,2},{3,19},{19,3},{4,20},{20... | collective-permute-start | bytes 307208 | tf_op jit(solution)/shard_map/ppermute | solution.py:478
  17.6 20.7 %copy-start.6 = (bf16[64,1728]{1,0:T(8,128)(2,1)S(1)}, bf16[64,1728]{1,0:T(8,128)(2,1)}, u32[]{:S(2)}) copy-start(bf16[64,1728]{1,0:T(8,128)(2,1)} %second.3) | copy-start | bytes 663556
  21.4 6.8 %collective-permute-start.7 = (bf16[30,384]{1,0:T(8,128)(2,1)S(1)}, bf16[30,384]{1,0:T(8,128)(2,1)S(1)}, u32[]{:S(2)}, u32[]{:S(2)}) collective-permute-start(bf16[30,384]{1,0:T(8,128)(2,1)S(1)} %get-tuple-element.27), channel_id=1, source_target_pairs={{0,4},{1,5},{2,6},{3,7},{4,8},{5,9},{6,10},{7,11},{8,12},{9,13},{1... | collective-permute-start | bytes 69128 | tf_op jit(solution)/shard_map/ppermute | solution.py:478
  22.8 5.4 %collective-permute-start.8 = (bf16[30,384]{1,0:T(8,128)(2,1)S(1)}, bf16[30,384]{1,0:T(8,128)(2,1)S(1)}, u32[]{:S(2)}, u32[]{:S(2)}) collective-permute-start(bf16[30,384]{1,0:T(8,128)(2,1)S(1)} %get-tuple-element.28), channel_id=1, source_target_pairs={{0,12},{1,13},{2,14},{3,15},{4,0},{5,1},{6,2},{7,3},{8,4},{9,5},{1... | collective-permute-start | bytes 69128 | tf_op jit(solution)/shard_map/ppermute | solution.py:478
  28.2 10.1 %copy-start.5 = (bf16[64,1728]{1,0:T(8,128)(2,1)S(1)}, bf16[64,1728]{1,0:T(8,128)(2,1)}, u32[]{:S(2)}) copy-start(bf16[64,1728]{1,0:T(8,128)(2,1)} %first.3) | copy-start | bytes 663556
  28.2 10.1 %copy-start.2 = (bf16[256,512]{1,0:T(8,128)(2,1)S(1)}, bf16[256,512]{1,0:T(8,128)(2,1)}, u32[]{:S(2)}) copy-start(bf16[256,512]{1,0:T(8,128)(2,1)} %reduce.3) | copy-start | bytes 786436
  28.3 5.2 %collective-permute-start.10 = (bf16[96,384]{1,0:T(8,128)(2,1)S(1)}, bf16[96,384]{1,0:T(8,128)(2,1)S(1)}, u32[]{:S(2)}, u32[]{:S(2)}) collective-permute-start(bf16[96,384]{1,0:T(8,128)(2,1)S(1)} %pad_maximum_fusion.2), channel_id=1, source_target_pairs={{0,3},{1,0},{2,1},{3,2},{4,7},{5,4},{6,5},{7,6},{8,11},{9,8},{10,9... | collective-permute-start | bytes 221192 | tf_op jit(solution)/shard_map/ppermute | solution.py:478
  31.5 5.3 %collective-permute-start.9 = (bf16[96,384]{1,0:T(8,128)(2,1)S(1)}, bf16[96,384]{1,0:T(8,128)(2,1)S(1)}, u32[]{:S(2)}, u32[]{:S(2)}) collective-permute-start(bf16[96,384]{1,0:T(8,128)(2,1)S(1)} %pad_maximum_fusion.2), channel_id=1, source_target_pairs={{0,1},{1,2},{2,3},{3,0},{4,5},{5,6},{6,7},{7,4},{8,9},{9,10},{10,1... | collective-permute-start | bytes 221192 | tf_op jit(solution)/shard_map/ppermute | solution.py:478
  36.8 1.5 %collective-permute-start.11 = (bf16[96,1152]{1,0:T(8,128)(2,1)S(1)}, bf16[96,1152]{1,0:T(8,128)(2,1)S(1)}, u32[]{:S(2)}, u32[]{:S(2)}) collective-permute-start(bf16[96,1152]{1,0:T(8,128)(2,1)S(1)} %pad_maximum_fusion.1.own), channel_id=1, source_target_pairs={{0,16},{16,0},{1,17},{17,1},{2,18},{18,2},{3,19},{19,3},{4,20},{20... | collective-permute-start | bytes 663560 | tf_op jit(solution)/shard_map/ppermute | solution.py:566
  36.8 5.5 %collective-permute-start.12 = (bf16[32,1728]{1,0:T(8,128)(2,1)S(1)}, bf16[32,1728]{1,0:T(8,128)(2,1)S(1)}, u32[]{:S(2)}, u32[]{:S(2)}) collective-permute-start(bf16[32,1728]{1,0:T(8,128)(2,1)S(1)} %collective-permute-done.6.turned), channel_id=1, source_target_pairs={{0,16},{16,0},{1,17},{17,1},{2,18},{18,2},{3,19},{19,3},{4,20},{20... | collective-permute-start | bytes 331784 | tf_op jit(solution)/shard_map/ppermute | solution.py:560
  54.3 9.7 %copy-start.7 = (bf16[64,1728]{1,0:T(8,128)(2,1)S(1)}, bf16[64,1728]{1,0:T(8,128)(2,1)}, u32[]{:S(2)}) copy-start(bf16[64,1728]{1,0:T(8,128)(2,1)} %refs_4_.1) | copy-start | bytes 663556
  55.9 6.9 %collective-permute-start.15 = (bf16[72,768]{1,0:T(8,128)(2,1)S(1)}, bf16[72,768]{1,0:T(8,128)(2,1)S(1)}, u32[]{:S(2)}, u32[]{:S(2)}) collective-permute-start(bf16[72,768]{1,0:T(8,128)(2,1)S(1)} %bottom_start.1.refs_0_), channel_id=1, source_target_pairs={{0,3},{1,2},{2,1},{3,0},{4,7},{5,6},{6,5},{7,4},{8,11},{9,10},{10,... | collective-permute-start | bytes 331784 | tf_op jit(solution)/shard_map/ppermute | solution.py:611
  57.2 6.9 %collective-permute-start.14 = (bf16[72,768]{1,0:T(8,128)(2,1)S(1)}, bf16[72,768]{1,0:T(8,128)(2,1)S(1)}, u32[]{:S(2)}, u32[]{:S(2)}) collective-permute-start(bf16[72,768]{1,0:T(8,128)(2,1)S(1)} %bottom_start.1.refs_0_), channel_id=1, source_target_pairs={{0,2},{1,3},{2,0},{3,1},{4,6},{5,7},{6,4},{7,5},{8,10},{9,11},{10,... | collective-permute-start | bytes 331784 | tf_op jit(solution)/shard_map/ppermute | solution.py:611
  58.5 5.6 %collective-permute-start.13 = (bf16[72,768]{1,0:T(8,128)(2,1)S(1)}, bf16[72,768]{1,0:T(8,128)(2,1)S(1)}, u32[]{:S(2)}, u32[]{:S(2)}) collective-permute-start(bf16[72,768]{1,0:T(8,128)(2,1)S(1)} %bottom_start.1.refs_0_), channel_id=1, source_target_pairs={{0,1},{1,0},{2,3},{3,2},{4,5},{5,4},{6,7},{7,6},{8,9},{9,8},{10,11... | collective-permute-start | bytes 331784 | tf_op jit(solution)/shard_map/ppermute | solution.py:611
  64.1 18.7 %copy-start.10 = (bf16[32,864]{1,0:T(8,128)(2,1)S(1)}, bf16[32,864]{1,0:T(8,128)(2,1)}, u32[]{:S(2)}) copy-start(bf16[32,864]{1,0:T(8,128)(2,1)} %f1.1) | copy-start | bytes 165892
  64.1 18.7 %copy-start.11 = (bf16[32,864]{1,0:T(8,128)(2,1)S(1)}, bf16[32,864]{1,0:T(8,128)(2,1)}, u32[]{:S(2)}) copy-start(bf16[32,864]{1,0:T(8,128)(2,1)} %f2.1) | copy-start | bytes 165892
  64.1 18.7 %copy-start.12 = (bf16[64,256]{1,0:T(8,128)(2,1)S(1)}, bf16[64,256]{1,0:T(8,128)(2,1)}, u32[]{:S(2)}) copy-start(bf16[64,256]{1,0:T(8,128)(2,1)} %up_fine.1) | copy-start | bytes 98308
  65.9 16.9 %copy-start.1 = (bf16[256,512]{1,0:T(8,128)(2,1)S(1)}, bf16[256,512]{1,0:T(8,128)(2,1)}, u32[]{:S(2)}) copy-start(bf16[256,512]{1,0:T(8,128)(2,1)} %up.1) | copy-start | bytes 786436
  65.9 16.9 %copy-start.3 = (bf16[64,1728]{1,0:T(8,128)(2,1)S(1)}, bf16[64,1728]{1,0:T(8,128)(2,1)}, u32[]{:S(2)}) copy-start(bf16[64,1728]{1,0:T(8,128)(2,1)} %m1.1) | copy-start | bytes 663556
  65.9 16.9 %copy-start.4 = (bf16[64,1728]{1,0:T(8,128)(2,1)S(1)}, bf16[64,1728]{1,0:T(8,128)(2,1)}, u32[]{:S(2)}) copy-start(bf16[64,1728]{1,0:T(8,128)(2,1)} %m2.1) | copy-start | bytes 663556
  81.1 1.7 %collective-permute-start.16 = (bf16[16,88,128]{2,1,0:T(8,128)(2,1)S(1)}, bf16[16,88,128]{2,1,0:T(8,128)(2,1)S(1)}, u32[]{:S(2)}, u32[]{:S(2)}) collective-permute-start(bf16[16,88,128]{2,1,0:T(8,128)(2,1)S(1)} %all_to_all.11.near), channel_id=1, source_target_pairs={{0,16},{16,0},{1,17},{17,1},{2,18},{18,2},{3,19},{19,3},{4,20},{20... | collective-permute-start | bytes 1081352 | tf_op jit(solution)/shard_map/ppermute | solution.py:629

commit v3 on v2

--- a/solution.py
+++ b/solution.py
@@ -11,6 +11,7 @@
 F32 = jnp.float32
 LANES = 128
 DEPTH = 256
+GRANT = 24 << 20
 
 
 def dot(a, b):
@@ -104,8 +105,57 @@
     return slice(tile * LANES, (tile + 1) * LANES)
 
 
+def fine_tables(first, second, reduce, first_table, second_table, down, flat):
+    conv_table(first_table, flat, first[...], 32)
+    conv_table(second_table, flat, second[...], 32)
+    shrink_table(down, flat, reduce[...], 32, 2)
+
+
+def middle_tables(first, second, reduce, first_table, second_table, downs, flat):
+    conv_table(first_table, flat, first[...], 64)
+    conv_table(second_table, flat, second[...], 64)
+    for quarter in range(downs.shape[0]):
+        rows = reduce[64 * quarter : 64 * (quarter + 1), :]
+        shrink_table(downs.at[quarter], flat, rows, 64, 0)
+
+
+def decoder_tables(bottom, up, m1, m2, up_fine, f1, f2, *refs):
+    bottom_table, lift, m1_table, m2_table, lift_fine, f1_table, f2_table, flat = refs
+    conv_table(bottom_table, flat, bottom[...], 64)
+    conv_table(m1_table, flat, m1[...], 64)
+    conv_table(m2_table, flat, m2[...], 64)
+    conv_table(f1_table, flat, f1[...], 32)
+    conv_table(f2_table, flat, f2[...], 32)
+    across = lift.shape[1] // DEPTH
+    odd = lax.axis_index("yz") % across % 2
+    blank = jnp.zeros((64, LANES), BF)
+    second_half = lane_group(64, 64) == 1
+    for dx in range(2):
+        for dy in range(2):
+            pair = picked(up[...], dx, dy, 64)
+            for group in range(across):
+                value = pair[64 * group : 64 * (group + 1)]
+                for cell in range(4):
+                    for half in range(2):
+                        block = blank
+                        if cell - half in (0, 1):
+                            block = jnp.where(odd == cell - half, value, 0.0).astype(BF)
+                        row = DEPTH * group + 64 * cell
+                        lift[2 * dx + dy, row : row + 64, span_of(half)] = block
+            value = picked(up_fine[...], dx, dy, 32)
+            for cell, block in enumerate(
+                (
+                    blank,
+                    jnp.where(second_half, 0.0, value).astype(BF),
+                    jnp.where(second_half, value, 0.0).astype(BF),
+                    blank,
+                )
+            ):
+                lift_fine[2 * dx + dy, 64 * cell : 64 * (cell + 1), :] = block
+
+
 def fine_encoder(
-    low, mid, high, first, second, reduce, skip, small, wide, s1, s2, table, flat, down, halves, flats
+    low, mid, high, first_table, second_table, down, skip, small, wide, s1, s2, halves, flats
 ):
     layers, width = mid.shape[0], mid.shape[2]
     start = 0
@@ -113,20 +163,17 @@
         wide[:, start : start + piece.shape[1], :] = piece[...].astype(F32)
         start += piece.shape[1]
     stage(wide, s1, layers, 32, 0, width)
-    conv_table(table, flat, first[...], 32)
     inner = layers - 2
     tiles = width // LANES
     for tile in range(tiles):
         depth = DEPTH if tile + 1 < tiles else LANES
-        value = rounded_relu(convolve(s1, table, inner, 32, tile, depth))
+        value = rounded_relu(convolve(s1, first_table, inner, 32, tile, depth))
         wide[:inner, :32, span_of(tile)] = value.astype(F32).reshape(inner, 32, LANES)
     stage(wide, s2, inner, 16, 0, width)
-    conv_table(table, flat, second[...], 32)
     kept = inner - 2
     for tile in range(tiles - 1):
-        value = rounded_relu(convolve(s2, table, kept, 16, tile))
+        value = rounded_relu(convolve(s2, second_table, kept, 16, tile))
         skip[:, :, span_of(tile)] = value.reshape(kept, 16, LANES)
-    shrink_table(down, flat, reduce[...], 32, 2)
     count = (kept - 4) // 2
     for tile in range(count // 2):
         left = jnp.concatenate(
@@ -160,7 +207,7 @@
 
 
 def middle(
-    own, other, first, second, reduce, window, sent, wide, s, table, flat, down, whole, halves, flats
+    own, other, first_table, second_table, downs, window, sent, wide, s, whole, halves, flats
 ):
     span = own.shape[1]
     side = span // 3 // 64
@@ -173,17 +220,15 @@
         wide[y, reach : reach + side, :span] = near[start : start + side]
         wide[y, reach + side : 2 * reach + side, :span] = far[start : start + reach]
     stage(wide, s, layers, 16, 0, span)
-    conv_table(table, flat, first[...], 64)
     layers -= 2
     tiles = span // LANES - 1
     for tile in range(tiles):
-        value = rounded_relu(convolve(s, table, layers, 16, tile))
+        value = rounded_relu(convolve(s, first_table, layers, 16, tile))
         wide[:layers, 0:16, span_of(tile)] = value.astype(F32).reshape(layers, 16, LANES)
     stage(wide, s, layers, 16, 0, tiles * LANES)
-    conv_table(table, flat, second[...], 64)
     layers -= 2
     for tile in range(tiles - 1):
-        value = rounded_relu(convolve(s, table, layers, 16, tile)).reshape(layers, 16, LANES)
+        value = rounded_relu(convolve(s, second_table, layers, 16, tile)).reshape(layers, 16, LANES)
         whole[:, :, span_of(tile)] = value
         wide[:layers, 0:16, span_of(tile)] = value.astype(F32)
     width = window.shape[2]
@@ -208,11 +253,10 @@
         )
         for tile in range(2)
     ]
-    across = reduce.shape[0] // 64
+    across = downs.shape[0]
     for quarter in range(across):
-        shrink_table(down, flat, reduce[64 * quarter : 64 * (quarter + 1), :], 64, 0)
         for tile, left in enumerate(lefts):
-            total = dot(left, down[...])
+            total = dot(left, downs[quarter])
             halves[0] = total[:, :LANES]
             halves[1] = total[:, LANES:]
             for y in range(half):
@@ -286,7 +330,7 @@
 
 
 def bottom(*refs):
-    *pieces, weight, out, wide, s, table, flat, whole, flats = refs
+    *pieces, table, out, wide, s, whole, flats = refs
     span = pieces[0].shape[1]
     cells = span // 64
     side = cells // 2
@@ -302,7 +346,6 @@
     ]
     wrap_rows(wide, cells, side)
     stage(wide, s, cells + 2, 16, 7, span + LANES)
-    conv_table(table, flat, weight[...], 64)
     for tile in range(span // LANES):
         value = convolve(s, table, cells, 16, tile).reshape(cells, 16, LANES)
         whole[2 : cells + 2, :, span_of(tile + 2)] = value[:, :8]
@@ -331,38 +374,21 @@
     far,
     window,
     skip,
-    up,
-    m1,
-    m2,
-    up_fine,
-    f1,
-    f2,
+    lift,
+    m1_table,
+    m2_table,
+    lift_fine,
+    f1_table,
+    f2_table,
     out,
     wide,
     s,
-    table,
-    flat,
-    lift,
     columns,
     spread,
 ):
     across = math.isqrt(near.shape[0])
     kept = window.shape[0] // 4
     layers = kept + 4
-    odd = lax.axis_index("yz") % across % 2
-    for dx in range(2):
-        for dy in range(2):
-            pair = picked(up[...], dx, dy, 64)
-            blank = jnp.zeros((64, LANES), BF)
-            for group in range(across):
-                value = pair[64 * group : 64 * (group + 1)]
-                for cell in range(4):
-                    for half in range(2):
-                        block = blank
-                        if cell - half in (0, 1):
-                            block = jnp.where(odd == cell - half, value, 0.0).astype(BF)
-                        row = DEPTH * group + 64 * cell
-                        lift[2 * dx + dy, row : row + 64, span_of(half)] = block
     groups = []
     for group in range(across):
         for part, parts in enumerate((near, far)):
@@ -405,36 +431,22 @@
     wide[:, 7:8, :] = wide[:, ends - 1 : ends, :]
     wide[:, ends : ends + 1, :] = wide[:, 8:9, :]
     stage(wide, s, count, 16, 7, window.shape[2])
-    conv_table(table, flat, m1[...], 64)
     count = count - 2
     for tile in range(6):
-        value = rounded_relu(convolve(s, table, count, 16, tile))
+        value = rounded_relu(convolve(s, m1_table, count, 16, tile))
         wide[:count, 8:24, span_of(tile)] = value.astype(F32).reshape(count, 16, LANES)
     wide[:, 7:8, :] = wide[:, ends - 1 : ends, :]
     wide[:, ends : ends + 1, :] = wide[:, 8:9, :]
     stage(wide, s, count, 16, 7, 6 * LANES)
-    conv_table(table, flat, m2[...], 64)
     count = count - 2
     risen = jnp.concatenate(
-        [rounded_relu(convolve(s, table, count, 16, tile)) for tile in range(5)], axis=1
-    )
-    second_half = lane_group(64, 64) == 1
-    zeros = jnp.zeros((64, LANES), F32)
+        [rounded_relu(convolve(s, m2_table, count, 16, tile)) for tile in range(5)], axis=1
+    )
     for dx in range(2):
         for dy in range(2):
-            value = picked(up_fine[...], dx, dy, 32)
-            for cell, block in enumerate(
-                (
-                    zeros,
-                    jnp.where(second_half, 0.0, value),
-                    jnp.where(second_half, value, 0.0),
-                    zeros,
-                )
-            ):
-                lift[0, 64 * cell : 64 * (cell + 1), span_of(0)] = block.astype(BF)
             for tile in range(4):
                 left = risen[:, tile * LANES : tile * LANES + DEPTH]
-                rise = dot(left, lift[0, :DEPTH, :LANES])
+                rise = dot(left, lift_fine[2 * dx + dy])
                 for y in range(count):
                     part = rise[16 * y : 16 * (y + 1)]
                     spread[tile, 2 * y + dy, pl.ds(2 + dx, 7, 2), :] = part[0:7]
@@ -444,16 +456,14 @@
         total = spread[tile, :count, 0:16, :] + skip[:, :, span_of(tile)].astype(F32)
         wide[:count, 0:16, span_of(tile)] = total.astype(BF).astype(F32)
     stage(wide, s, count, 16, 0, 4 * LANES)
-    conv_table(table, flat, f1[...], 32)
     count = count - 2
     for tile in range(4):
-        value = rounded_relu(convolve(s, table, count, 16, tile, DEPTH if tile < 3 else LANES))
+        value = rounded_relu(convolve(s, f1_table, count, 16, tile, DEPTH if tile < 3 else LANES))
         wide[:count, 0:16, span_of(tile)] = value.astype(F32).reshape(count, 16, LANES)
     stage(wide, s, count, 16, 0, 4 * LANES)
-    conv_table(table, flat, f2[...], 32)
     count = count - 2
     for tile in range(3):
-        value = rounded_relu(convolve(s, table, count, 16, tile))
+        value = rounded_relu(convolve(s, f2_table, count, 16, tile))
         out[:, :, span_of(tile)] = value.reshape(count, 16, LANES)
 
 
@@ -464,6 +474,7 @@
         in_specs=[pl.BlockSpec(memory_space=pltpu.VMEM)] * len(args),
         out_specs=jax.tree.map(lambda _: pl.BlockSpec(memory_space=pltpu.VMEM), outs),
         scratch_shapes=scratch,
+        compiler_params=pltpu.CompilerParams(vmem_limit_bytes=GRANT),
         name=kernel.__name__,
     )(*[near_by(arg) for arg in args])
 
@@ -510,6 +521,48 @@
     def along_z(source, step):
         return source // across * across + (source % across + step) % across
 
+    seen = ext + 2 * halo
+    side = ext // 2
+    flat = pltpu.VMEM((27 * mid, LANES), F32)
+    table = jax.ShapeDtypeStruct((3 * DEPTH, 3 * LANES), BF)
+    down = jax.ShapeDtypeStruct((2 * DEPTH, 2 * LANES), BF)
+    fine_tabs = call(
+        fine_tables,
+        (table, table, down),
+        [flat],
+        encode_fine_first,
+        encode_fine_second,
+        reduce_fine,
+    )
+    middle_tabs = call(
+        middle_tables,
+        (table, table, jax.ShapeDtypeStruct((across, *down.shape), BF)),
+        [flat],
+        encode_middle_first,
+        encode_middle_second,
+        reduce_middle,
+    )
+    bottom_tab, *decoder_tabs = call(
+        decoder_tables,
+        (
+            table,
+            jax.ShapeDtypeStruct((4, across * DEPTH, 2 * LANES), BF),
+            table,
+            table,
+            jax.ShapeDtypeStruct((4, DEPTH, LANES), BF),
+            table,
+            table,
+        ),
+        [flat],
+        bottom_second,
+        expand_middle,
+        decode_middle_first,
+        decode_middle_second,
+        expand_fine,
+        decode_fine_first,
+        decode_fine_second,
+    )
+
     cores = lax.axis_size("gx")
     size = bottom_first.shape[0] // cores
     mine = lax.dynamic_slice_in_dim(bottom_first, lax.axis_index("gx") * size, size, 0)
@@ -526,11 +579,6 @@
     cells = jnp.concatenate([low, cells, high], axis=2)
     low, high = exchange(cells[:, :halo], cells[:, ext - halo :], "gx", around)
 
-    seen = ext + 2 * halo
-    side = ext // 2
-    flat = pltpu.VMEM((27 * mid, LANES), F32)
-    table = pltpu.VMEM((3 * DEPTH, 3 * LANES), BF)
-    down = pltpu.VMEM((2 * DEPTH, 2 * LANES), BF)
     skip, small = call(
         fine_encoder,
         (
@@ -541,18 +589,13 @@
             pltpu.VMEM((seen, 40, seen * fine), F32),
             pltpu.VMEM((3, seen * 32, seen * fine), BF),
             pltpu.VMEM((3, (seen - 2) * 16, seen * fine), BF),
-            table,
-            flat,
-            down,
             pltpu.VMEM((2, side * 16, LANES), F32),
             pltpu.VMEM((side * side, side * mid), F32),
         ],
         low,
         cells,
         high,
-        encode_fine_first,
-        encode_fine_second,
-        reduce_fine,
+        *fine_tabs,
     )
 
     small, turned = lax.optimization_barrier((small, turned))
@@ -577,18 +620,13 @@
         [
             pltpu.VMEM((layers, 32, span), F32),
             pltpu.VMEM((3, layers * 16, span), BF),
-            table,
-            flat,
-            down,
             pltpu.VMEM((layers - 4, 16, 14 * mid), BF),
             pltpu.VMEM((2, side * 8, LANES), F32),
             pltpu.VMEM((32, LANES), F32),
         ],
         own,
         other,
-        encode_middle_first,
-        encode_middle_second,
-        reduce_middle,
+        *middle_tabs,
     )
     sent, swapped = lax.optimization_barrier((sent, swapped))
     gathered = lax.all_to_all(sent, ("gx", "yz"), 0, 0)
@@ -598,7 +636,7 @@
         [
             pltpu.VMEM((half + 2, 32, half * mid + LANES), F32),
             pltpu.VMEM((3, (half + 2) * 16, half * mid + LANES), BF),
-            table,
+            pltpu.VMEM(table.shape, BF),
             flat,
             pltpu.VMEM((half * side, half * mid), F32),
         ],
@@ -617,13 +655,11 @@
         [
             pltpu.VMEM((half + 2, 32, half * mid + LANES), F32),
             pltpu.VMEM((3, (half + 2) * 16, half * mid + LANES), BF),
-            table,
-            flat,
             pltpu.VMEM((half + 5, 8, half * mid + 2 * LANES), F32),
             pltpu.VMEM((88, LANES), F32),
         ],
         *pieces,
-        bottom_second,
+        bottom_tab,
     )
     near = lax.all_to_all(sent, "yz", 0, 0)
     far = lax.ppermute(near, "gx", swap)
@@ -634,9 +670,6 @@
         [
             pltpu.VMEM((16, 32, 1024), F32),
             pltpu.VMEM((3, 256, 1024), BF),
-            table,
-            flat,
-            pltpu.VMEM((4, across * DEPTH, 2 * LANES), BF),
             pltpu.VMEM((8, 16, 512), F32),
             pltpu.VMEM((8, 16, 32, LANES), F32),
         ],
@@ -644,12 +677,7 @@
         far,
         window,
         skip,
-        expand_middle,
-        decode_middle_first,
-        decode_middle_second,
-        expand_fine,
-        decode_fine_first,
-        decode_fine_second,
+        *decoder_tabs,
     )
     risen = risen[:, :ext].reshape(ext, ext, ext, fine).transpose(3, 1, 0, 2)
     return risen.reshape(1, fine, ext, ext * ext)

time: 90.8 us -> 88.6 us (0.976)
  waiting for transfers between devices: 20 us -> 17 us
    ppermute x3, waiting for transfers between devices: 4.59 us -> 3.06 us  [gathered_body(): lax.ppermute(partial, 'yz', [(s, s ^ turn) for s in range(devices)])]
    pallas_call x5 -> x8, Pallas kernels: 17.2 us -> 17.7 us  [call(): pl.pallas_call(kernel, out_shape=jax.tree.map(lambda out: pltpu.VMEM(out....]
  transfers between devices with their start and end apart: 17 -> 17, of which waited for: 13 -> 13; matrix products, arithmetic and copies ran while one was open for 1% -> 1% of each run, Pallas kernels for 9% -> 11%
where the time goes in v3:
time: 88.6 us; the launch traced here: 88.4 us
  blocking collectives  27.1 us (31%)
  starting transfers between devices  22.1 us (25%)
  Pallas kernels  17.7 us (20%)
  waiting for transfers between devices  17 us (19%)
  local copies, waits for them, and re-layouts  4.14 us (5%)
    pallas_call x8, Pallas kernels, call(): pl.pallas_call(kernel, out_shape=jax.tree.map(lambda out: pltpu.VMEM(out....  17.7 us
    ppermute x10, starting transfers between devices, exchange(): return (lax.ppermute(tail, axis, ahead), lax.ppermute(head, axis, back))  17.2 us
    all_to_all x1, blocking collectives, gathered_body(): near = lax.all_to_all(sent, 'yz', 0, 0)  15.1 us
    ppermute x10, waiting for transfers between devices, exchange(): return (lax.ppermute(tail, axis, ahead), lax.ppermute(head, axis, back))  12.1 us
    all_to_all x1, blocking collectives, gathered_body(): gathered = lax.all_to_all(sent, ('gx', 'yz'), 0, 0)  12 us
    ppermute x3, starting transfers between devices, gathered_body(): lax.ppermute(partial, 'yz', [(s, s ^ turn) for s in range(devices)])  3.55 us
    ppermute x3, waiting for transfers between devices, gathered_body(): lax.ppermute(partial, 'yz', [(s, s ^ turn) for s in range(devices)])  3.06 us
  transfers between devices with their start and end apart: 17, of which 13 were waited for; matrix products, arithmetic and copies ran while one was open for 1% of the time, Pallas kernels for 11%

profile of v3, /device:TPU:0, one launch (start us, length us, event | category | flops | bytes accessed | tf_op | source)
XLA Modules:
  0.0 88.4 jit_solution(7002403475657275497)
XLA Ops:
  0.0 1.2 %copy.18 = bf16[1,32,12,144]{1,3,2,0:T(8,128)(2,1)S(1)} copy(bf16[1,32,12,144]{3,1,2,0:T(8,128)(2,1)} %param.15) | data formatting | bytes 221184 | tf_op args[0]
  1.2 0.1 reshape.14
  1.4 0.0 copy-start.8
  1.4 0.0 copy-start.9
  1.4 0.0 copy-start.13
  1.5 0.2 slice.34
  1.6 3.1 %collective-permute-start = (bf16[4,12,384]{2,1,0:T(8,128)(2,1)S(1)}, bf16[4,12,384]{2,1,0:T(8,128)(2,1)S(1)}, u32[]{:S(2)}, u32[]{:S(2)}) collective-permute-start(bf16[4,12,384]{2,1,0:T(8,128)(2,1)S(1)} %copy.19), channel_id=1, source_target_pairs={{0,4},{1,5},{2,6},{3,7},{4,8},{5,9},{6,10},{7,11},{8,12},{9,13},{1... | collective-permute-start | bytes 110600 | tf_op jit(solution)/shard_map/ppermute | solution.py:489
  4.7 0.2 slice.36
  4.9 2.1 %collective-permute-start.1 = (bf16[4,12,384]{2,1,0:T(8,128)(2,1)S(1)}, bf16[4,12,384]{2,1,0:T(8,128)(2,1)S(1)}, u32[]{:S(2)}, u32[]{:S(2)}) collective-permute-start(bf16[4,12,384]{2,1,0:T(8,128)(2,1)S(1)} %copy.21), channel_id=1, source_target_pairs={{0,12},{1,13},{2,14},{3,15},{4,0},{5,1},{6,2},{7,3},{8,4},{9,5},{1... | collective-permute-start | bytes 110600 | tf_op jit(solution)/shard_map/ppermute | solution.py:489
  7.0 0.4 reshape.18
  7.5 1.5 %collective-permute-done = bf16[4,12,384]{2,1,0:T(8,128)(2,1)S(1)} collective-permute-done((bf16[4,12,384]{2,1,0:T(8,128)(2,1)S(1)}, bf16[4,12,384]{2,1,0:T(8,128)(2,1)S(1)}, u32[]{:S(2)}, u32[]{:S(2)}) %collective-permute-start) | collective-permute-done | bytes 36896 | tf_op jit(solution)/shard_map/ppermute | solution.py:489
  9.0 0.5 collective-permute-done.1
  9.5 1.7 %collective-permute-start.2 = (bf16[20,12,128]{2,1,0:T(8,128)(2,1)S(1)}, bf16[20,12,128]{2,1,0:T(8,128)(2,1)S(1)}, u32[]{:S(2)}, u32[]{:S(2)}) collective-permute-start(bf16[20,12,128]{2,1,0:T(8,128)(2,1)S(1)} %get-tuple-element.51), channel_id=1, source_target_pairs={{0,1},{1,2},{2,3},{3,0},{4,5},{5,6},{6,7},{7,4},{8,9},{9,10},{10,1... | collective-permute-start | bytes 184328 | tf_op jit(solution)/shard_map/ppermute | solution.py:489
  11.2 1.3 %collective-permute-start.3 = (bf16[20,12,128]{2,1,0:T(8,128)(2,1)S(1)}, bf16[20,12,128]{2,1,0:T(8,128)(2,1)S(1)}, u32[]{:S(2)}, u32[]{:S(2)}) collective-permute-start(bf16[20,12,128]{2,1,0:T(8,128)(2,1)S(1)} %get-tuple-element.52), channel_id=1, source_target_pairs={{0,3},{1,0},{2,1},{3,2},{4,7},{5,4},{6,5},{7,6},{8,11},{9,8},{10,9... | collective-permute-start | bytes 184328 | tf_op jit(solution)/shard_map/ppermute | solution.py:489
  12.5 0.0 copy-start.1
  12.5 0.0 copy-start.6
  12.5 0.0 copy-start.7
  12.5 0.8 collective-permute-start.6
  13.4 1.6 %collective-permute-done.2 = bf16[20,12,128]{2,1,0:T(8,128)(2,1)S(1)} collective-permute-done((bf16[20,12,128]{2,1,0:T(8,128)(2,1)S(1)}, bf16[20,12,128]{2,1,0:T(8,128)(2,1)S(1)}, u32[]{:S(2)}, u32[]{:S(2)}) %collective-permute-start.2) | collective-permute-done | bytes 61472 | tf_op jit(solution)/shard_map/ppermute | solution.py:489
  14.9 1.0 %collective-permute-done.3 = bf16[20,12,128]{2,1,0:T(8,128)(2,1)S(1)} collective-permute-done((bf16[20,12,128]{2,1,0:T(8,128)(2,1)S(1)}, bf16[20,12,128]{2,1,0:T(8,128)(2,1)S(1)}, u32[]{:S(2)}, u32[]{:S(2)}) %collective-permute-start.3) | collective-permute-done | bytes 61472 | tf_op jit(solution)/shard_map/ppermute | solution.py:489
  16.0 0.1 pad_maximum_fusion.mid
  16.0 0.1 fusion.1
  16.1 0.1 collective-permute-start.5
  16.2 0.5 collective-permute-start.4
  16.7 0.4 fine_tables.1
  17.1 0.4 collective-permute-done.5.high
  17.5 0.2 collective-permute-done.4.low
  17.6 3.6 %fine_encoder.1 = (bf16[16,16,512]{2,1,0:T(8,128)(2,1)S(1)}, bf16[36,384]{1,0:T(8,128)(2,1)S(1)}) custom-call(bf16[20,4,640]{2,1,0:T(4,128)(2,1)S(1)} %collective-permute-done.4.low, bf16[20,12,640]{2,1,0:T(8,128)(2,1)S(1)} %pad_maximum_fusion.mid, bf16[20,4,640]{2,1,0:T(4,128)(2,1)S(1)} %collective-permute-done.5.high, ...), custom_call_target="tpu_custom_call" | custom-call | tf_op jit(solution)/shard_map/fine_encoder/pallas_call | solution.py:471
  21.3 1.8 %collective-permute-start.7 = (bf16[30,384]{1,0:T(8,128)(2,1)S(1)}, bf16[30,384]{1,0:T(8,128)(2,1)S(1)}, u32[]{:S(2)}, u32[]{:S(2)}) collective-permute-start(bf16[30,384]{1,0:T(8,128)(2,1)S(1)} %get-tuple-element.53), channel_id=1, source_target_pairs={{0,4},{1,5},{2,6},{3,7},{4,8},{5,9},{6,10},{7,11},{8,12},{9,13},{1... | collective-permute-start | bytes 69128 | tf_op jit(solution)/shard_map/ppermute | solution.py:489
  23.0 3.5 %collective-permute-start.8 = (bf16[30,384]{1,0:T(8,128)(2,1)S(1)}, bf16[30,384]{1,0:T(8,128)(2,1)S(1)}, u32[]{:S(2)}, u32[]{:S(2)}) collective-permute-start(bf16[30,384]{1,0:T(8,128)(2,1)S(1)} %get-tuple-element.54), channel_id=1, source_target_pairs={{0,12},{1,13},{2,14},{3,15},{4,0},{5,1},{6,2},{7,3},{8,4},{9,5},{1... | collective-permute-start | bytes 69128 | tf_op jit(solution)/shard_map/ppermute | solution.py:489
  26.5 1.7 %collective-permute-done.7 = bf16[30,384]{1,0:T(8,128)(2,1)S(1)} collective-permute-done((bf16[30,384]{1,0:T(8,128)(2,1)S(1)}, bf16[30,384]{1,0:T(8,128)(2,1)S(1)}, u32[]{:S(2)}, u32[]{:S(2)}) %collective-permute-start.7) | collective-permute-done | bytes 23072 | tf_op jit(solution)/shard_map/ppermute | solution.py:489
  28.3 0.0 collective-permute-done.8
  28.3 3.2 %collective-permute-start.10 = (bf16[96,384]{1,0:T(8,128)(2,1)S(1)}, bf16[96,384]{1,0:T(8,128)(2,1)S(1)}, u32[]{:S(2)}, u32[]{:S(2)}) collective-permute-start(bf16[96,384]{1,0:T(8,128)(2,1)S(1)} %pad_maximum_fusion.2), channel_id=1, source_target_pairs={{0,3},{1,0},{2,1},{3,2},{4,7},{5,4},{6,5},{7,6},{8,11},{9,8},{10,9... | collective-permute-start | bytes 221192 | tf_op jit(solution)/shard_map/ppermute | solution.py:489
  31.5 0.0 collective-permute-start.9
  31.5 2.2 %collective-permute-done.10 = bf16[96,384]{1,0:T(8,128)(2,1)S(1)} collective-permute-done((bf16[96,384]{1,0:T(8,128)(2,1)S(1)}, bf16[96,384]{1,0:T(8,128)(2,1)S(1)}, u32[]{:S(2)}, u32[]{:S(2)}) %collective-permute-start.10) | collective-permute-done | bytes 73760 | tf_op jit(solution)/shard_map/ppermute | solution.py:489
  33.7 3.1 %collective-permute-done.9 = bf16[96,384]{1,0:T(8,128)(2,1)S(1)} collective-permute-done((bf16[96,384]{1,0:T(8,128)(2,1)S(1)}, bf16[96,384]{1,0:T(8,128)(2,1)S(1)}, u32[]{:S(2)}, u32[]{:S(2)}) %collective-permute-start.9) | collective-permute-done | bytes 73760 | tf_op jit(solution)/shard_map/ppermute | solution.py:489
  36.8 0.0 copy-start.2
  36.8 0.0 copy-start.3
  36.8 0.0 copy-start.4
  36.8 0.0 copy-start.5
  36.8 0.0 copy-start.10
  36.9 0.0 copy-start.11
  36.9 0.0 copy-start.12
  36.9 0.1 collective-permute-start.11
  37.0 0.5 collective-permute-start.12
  37.5 0.8 middle_tables.1
  38.3 0.1 collective-permute-done.11.other
  38.4 3.5 %middle.1 = (bf16[12,16,896]{2,1,0:T(8,128)(2,1)S(1)}, bf16[32,16,128]{2,1,0:T(8,128)(2,1)S(1)}) custom-call(bf16[96,1152]{1,0:T(8,128)(2,1)S(1)} %pad_maximum_fusion.1.own, bf16[96,1152]{1,0:T(8,128)(2,1)S(1)} %collective-permute-done.11.other, bf16[768,384]{1,0:T(8,128)(2,1)S(1)} %get-tuple-element.31.first_table, ...), custom_call_target="tpu_custom_call" | custom-call | tf_op jit(solution)/shard_map/middle/pallas_call | solution.py:471
  41.9 12.0 %all_to_all.10.gathered = bf16[32,16,128]{2,1,0:T(8,128)(2,1)S(1)} all-to-all(bf16[32,16,128]{2,1,0:T(8,128)(2,1)S(1)} %get-tuple-element.36), channel_id=1, replica_groups=mesh['gx'=2,'yz'=16] {'gx','yz'}, dimensions={0} | all-to-all | bytes 262144 | tf_op jit(solution)/shard_map/all_to_all | solution.py:632
  53.9 1.6 %bottom_start.1.refs_0_ = bf16[72,768]{1,0:T(8,128)(2,1)S(1)} custom-call(bf16[32,16,128]{2,1,0:T(8,128)(2,1)S(1)} %all_to_all.10.gathered, bf16[32,1728]{1,0:T(8,128)(2,1)S(1)} %collective-permute-done.6.turned, bf16[32,1728]{1,0:T(8,128)(2,1)S(1)} %collective-permute-done.12.swapped), custom_call_target="tpu_custom_call" | custom-call | tf_op jit(solution)/shard_map/bottom_start/pallas_call | solution.py:471
  55.5 1.2 %collective-permute-start.15 = (bf16[72,768]{1,0:T(8,128)(2,1)S(1)}, bf16[72,768]{1,0:T(8,128)(2,1)S(1)}, u32[]{:S(2)}, u32[]{:S(2)}) collective-permute-start(bf16[72,768]{1,0:T(8,128)(2,1)S(1)} %bottom_start.1.refs_0_), channel_id=1, source_target_pairs={{0,3},{1,2},{2,1},{3,0},{4,7},{5,6},{6,5},{7,4},{8,11},{9,10},{10,... | collective-permute-start | bytes 331784 | tf_op jit(solution)/shard_map/ppermute | solution.py:649
  56.8 1.3 %collective-permute-start.14 = (bf16[72,768]{1,0:T(8,128)(2,1)S(1)}, bf16[72,768]{1,0:T(8,128)(2,1)S(1)}, u32[]{:S(2)}, u32[]{:S(2)}) collective-permute-start(bf16[72,768]{1,0:T(8,128)(2,1)S(1)} %bottom_start.1.refs_0_), channel_id=1, source_target_pairs={{0,2},{1,3},{2,0},{3,1},{4,6},{5,7},{6,4},{7,5},{8,10},{9,11},{10,... | collective-permute-start | bytes 331784 | tf_op jit(solution)/shard_map/ppermute | solution.py:649
  58.1 1.0 %collective-permute-start.13 = (bf16[72,768]{1,0:T(8,128)(2,1)S(1)}, bf16[72,768]{1,0:T(8,128)(2,1)S(1)}, u32[]{:S(2)}, u32[]{:S(2)}) collective-permute-start(bf16[72,768]{1,0:T(8,128)(2,1)S(1)} %bottom_start.1.refs_0_), channel_id=1, source_target_pairs={{0,1},{1,0},{2,3},{3,2},{4,5},{5,4},{6,7},{7,6},{8,9},{9,8},{10,11... | collective-permute-start | bytes 331784 | tf_op jit(solution)/shard_map/ppermute | solution.py:649
  59.1 1.5 %decoder_tables.1 = (bf16[768,384]{1,0:T(8,128)(2,1)S(1)}, bf16[4,1024,256]{2,1,0:T(8,128)(2,1)S(1)}, bf16[768,384]{1,0:T(8,128)(2,1)S(1)}, bf16[768,384]{1,0:T(...) custom-call(bf16[64,1728]{1,0:T(8,128)(2,1)S(1)} %copy-done.3, ...), custom_call_target="tpu_custom_call" | custom-call | tf_op jit(solution)/shard_map/decoder_tables/pallas_call | solution.py:471
  60.6 1.8 %collective-permute-done.15.refs_3_ = bf16[72,768]{1,0:T(8,128)(2,1)S(1)} collective-permute-done((bf16[72,768]{1,0:T(8,128)(2,1)S(1)}, bf16[72,768]{1,0:T(8,128)(2,1)S(1)}, u32[]{:S(2)}, u32[]{:S(2)}) %collective-permute-start.15) | collective-permute-done | bytes 110624 | tf_op jit(solution)/shard_map/ppermute | solution.py:649
  62.4 1.2 %collective-permute-done.14.refs_2_ = bf16[72,768]{1,0:T(8,128)(2,1)S(1)} collective-permute-done((bf16[72,768]{1,0:T(8,128)(2,1)S(1)}, bf16[72,768]{1,0:T(8,128)(2,1)S(1)}, u32[]{:S(2)}, u32[]{:S(2)}) %collective-permute-start.14) | collective-permute-done | bytes 110624 | tf_op jit(solution)/shard_map/ppermute | solution.py:649
  63.7 1.5 %bottom.3 = bf16[16,88,128]{2,1,0:T(8,128)(2,1)S(1)} custom-call(bf16[72,768]{1,0:T(8,128)(2,1)S(1)} %bottom_start.1.refs_0_, bf16[72,768]{1,0:T(8,128)(2,1)S(1)} %collective-permute-done.13.refs_1_, bf16[72,768]{1,0:T(8,128)(2,1)S(1)} %collective-permute-done.14.refs_2_, bf16[72,768]{1,0:T(8,128)(2,1)S(1)} %collective-permute-done.15.refs_3_, ...), custom_call_target="tpu_custom_call" | custom-call | tf_op jit(solution)/shard_map/bottom/pallas_call | solution.py:471
  65.2 15.1 %all_to_all.11.near = bf16[16,88,128]{2,1,0:T(8,128)(2,1)S(1)} all-to-all(bf16[16,88,128]{2,1,0:T(8,128)(2,1)S(1)} %bottom.3), channel_id=1, replica_groups=mesh['gx'=2,'yz'=16] {'yz'}, dimensions={0} | all-to-all | bytes 720896 | tf_op jit(solution)/shard_map/all_to_all | solution.py:664
  80.3 1.7 %collective-permute-done.16.far = bf16[16,88,128]{2,1,0:T(8,128)(2,1)S(1)} collective-permute-done((bf16[16,88,128]{2,1,0:T(8,128)(2,1)S(1)}, bf16[16,88,128]{2,1,0:T(8,128)(2,1)S(1)}, u32[]{:S(2)}, u32[]{:S(2)}) %collective-permute-start.16) | collective-permute-done | bytes 360480 | tf_op jit(solution)/shard_map/ppermute | solution.py:665
  82.0 4.8 %decoder.1 = bf16[12,16,384]{2,1,0:T(8,128)(2,1)S(1)} custom-call(bf16[16,88,128]{2,1,0:T(8,128)(2,1)S(1)} %all_to_all.11.near, bf16[16,88,128]{2,1,0:T(8,128)(2,1)S(1)} %collective-permute-done.16.far, bf16[12,16,896]{2,1,0:T(8,128)(2,1)S(1)} %get-tuple-element.39.window, bf16[16,16,512]{2,1,0:T(8,128)(2,1)S(1)} %get-tuple-element.40.skip, ...), custom_call_target="tpu_custom_call" | custom-call | tf_op jit(solution)/shard_map/decoder/pallas_call | solution.py:471
  86.7 0.4 reshape.16
  87.2 0.1 copy.27
  87.3 0.2 reshape.17
  87.5 0.9 %copy.23 = bf16[1,32,12,144]{3,1,2,0:T(8,128)(2,1)} copy(bf16[1,32,12,144]{1,3,2,0:T(8,128)(2,1)S(1)} %reshape.17) | data formatting | bytes 221184 | tf_op jit(solution)/shard_map/reshape | solution.py:683
  (30 shorter events, 0.2 us)
Async XLA Ops:
  0.0 12.5 %copy-start = (bf16[64,1728]{1,0:T(8,128)(2,1)S(1)}, bf16[64,1728]{1,0:T(8,128)(2,1)}, u32[]{:S(2)}) copy-start(bf16[64,1728]{1,0:T(8,128)(2,1)} %param.22) | copy-start | bytes 663556
  1.4 15.3 %copy-start.8 = (bf16[32,864]{1,0:T(8,128)(2,1)S(1)}, bf16[32,864]{1,0:T(8,128)(2,1)}, u32[]{:S(2)}) copy-start(bf16[32,864]{1,0:T(8,128)(2,1)} %first.2) | copy-start | bytes 165892
  1.4 15.3 %copy-start.9 = (bf16[32,864]{1,0:T(8,128)(2,1)S(1)}, bf16[32,864]{1,0:T(8,128)(2,1)}, u32[]{:S(2)}) copy-start(bf16[32,864]{1,0:T(8,128)(2,1)} %second.2) | copy-start | bytes 165892
  1.4 15.3 %copy-start.13 = (bf16[64,256]{1,0:T(8,128)(2,1)S(1)}, bf16[64,256]{1,0:T(8,128)(2,1)}, u32[]{:S(2)}) copy-start(bf16[64,256]{1,0:T(8,128)(2,1)} %reduce.2) | copy-start | bytes 98308
  1.6 7.3 %collective-permute-start = (bf16[4,12,384]{2,1,0:T(8,128)(2,1)S(1)}, bf16[4,12,384]{2,1,0:T(8,128)(2,1)S(1)}, u32[]{:S(2)}, u32[]{:S(2)}) collective-permute-start(bf16[4,12,384]{2,1,0:T(8,128)(2,1)S(1)} %copy.19), channel_id=1, source_target_pairs={{0,4},{1,5},{2,6},{3,7},{4,8},{5,9},{6,10},{7,11},{8,12},{9,13},{1... | collective-permute-start | bytes 110600 | tf_op jit(solution)/shard_map/ppermute | solution.py:489
  4.9 4.5 %collective-permute-start.1 = (bf16[4,12,384]{2,1,0:T(8,128)(2,1)S(1)}, bf16[4,12,384]{2,1,0:T(8,128)(2,1)S(1)}, u32[]{:S(2)}, u32[]{:S(2)}) collective-permute-start(bf16[4,12,384]{2,1,0:T(8,128)(2,1)S(1)} %copy.21), channel_id=1, source_target_pairs={{0,12},{1,13},{2,14},{3,15},{4,0},{5,1},{6,2},{7,3},{8,4},{9,5},{1... | collective-permute-start | bytes 110600 | tf_op jit(solution)/shard_map/ppermute | solution.py:489
  9.5 5.4 %collective-permute-start.2 = (bf16[20,12,128]{2,1,0:T(8,128)(2,1)S(1)}, bf16[20,12,128]{2,1,0:T(8,128)(2,1)S(1)}, u32[]{:S(2)}, u32[]{:S(2)}) collective-permute-start(bf16[20,12,128]{2,1,0:T(8,128)(2,1)S(1)} %get-tuple-element.51), channel_id=1, source_target_pairs={{0,1},{1,2},{2,3},{3,0},{4,5},{5,6},{6,7},{7,4},{8,9},{9,10},{10,1... | collective-permute-start | bytes 184328 | tf_op jit(solution)/shard_map/ppermute | solution.py:489
  11.2 4.8 %collective-permute-start.3 = (bf16[20,12,128]{2,1,0:T(8,128)(2,1)S(1)}, bf16[20,12,128]{2,1,0:T(8,128)(2,1)S(1)}, u32[]{:S(2)}, u32[]{:S(2)}) collective-permute-start(bf16[20,12,128]{2,1,0:T(8,128)(2,1)S(1)} %get-tuple-element.52), channel_id=1, source_target_pairs={{0,3},{1,0},{2,1},{3,2},{4,7},{5,4},{6,5},{7,6},{8,11},{9,8},{10,9... | collective-permute-start | bytes 184328 | tf_op jit(solution)/shard_map/ppermute | solution.py:489
  12.5 24.9 %copy-start.1 = (bf16[256,512]{1,0:T(8,128)(2,1)S(1)}, bf16[256,512]{1,0:T(8,128)(2,1)}, u32[]{:S(2)}) copy-start(bf16[256,512]{1,0:T(8,128)(2,1)} %reduce.3) | copy-start | bytes 786436
  12.5 24.9 %copy-start.6 = (bf16[64,1728]{1,0:T(8,128)(2,1)S(1)}, bf16[64,1728]{1,0:T(8,128)(2,1)}, u32[]{:S(2)}) copy-start(bf16[64,1728]{1,0:T(8,128)(2,1)} %first.3) | copy-start | bytes 663556
  12.5 24.9 %copy-start.7 = (bf16[64,1728]{1,0:T(8,128)(2,1)S(1)}, bf16[64,1728]{1,0:T(8,128)(2,1)}, u32[]{:S(2)}) copy-start(bf16[64,1728]{1,0:T(8,128)(2,1)} %second.3) | copy-start | bytes 663556
  12.5 8.7 %collective-permute-start.6 = (bf16[32,1728]{1,0:T(8,128)(2,1)S(1)}, bf16[32,1728]{1,0:T(8,128)(2,1)S(1)}, u32[]{:S(2)}, u32[]{:S(2)}) collective-permute-start(bf16[32,1728]{1,0:T(8,128)(2,1)S(1)} %constant_dynamic-slice_fusion), channel_id=1, source_target_pairs={{0,0},{1,4},{2,8},{3,12},{4,1},{5,5},{6,9},{7,13},{8,2},{9,6},{10,... | collective-permute-start | bytes 331784 | tf_op jit(solution)/shard_map/ppermute | solution.py:569
  16.1 1.4 %collective-permute-start.5 = (bf16[20,4,640]{2,1,0:T(4,128)(2,1)S(1)}, bf16[20,4,640]{2,1,0:T(4,128)(2,1)S(1)}, u32[]{:S(2)}, u32[]{:S(2)}) collective-permute-start(bf16[20,4,640]{2,1,0:T(4,128)(2,1)S(1)} %get-tuple-element.49), channel_id=1, source_target_pairs={{0,16},{16,0},{1,17},{17,1},{2,18},{18,2},{3,19},{19,3},{4,20},{20... | collective-permute-start | bytes 307208 | tf_op jit(solution)/shard_map/ppermute | solution.py:489
  16.2 1.4 %collective-permute-start.4 = (bf16[20,4,640]{2,1,0:T(4,128)(2,1)S(1)}, bf16[20,4,640]{2,1,0:T(4,128)(2,1)S(1)}, u32[]{:S(2)}, u32[]{:S(2)}) collective-permute-start(bf16[20,4,640]{2,1,0:T(4,128)(2,1)S(1)} %get-tuple-element.50), channel_id=1, source_target_pairs={{0,16},{16,0},{1,17},{17,1},{2,18},{18,2},{3,19},{19,3},{4,20},{20... | collective-permute-start | bytes 307208 | tf_op jit(solution)/shard_map/ppermute | solution.py:489
  21.3 7.0 %collective-permute-start.7 = (bf16[30,384]{1,0:T(8,128)(2,1)S(1)}, bf16[30,384]{1,0:T(8,128)(2,1)S(1)}, u32[]{:S(2)}, u32[]{:S(2)}) collective-permute-start(bf16[30,384]{1,0:T(8,128)(2,1)S(1)} %get-tuple-element.53), channel_id=1, source_target_pairs={{0,4},{1,5},{2,6},{3,7},{4,8},{5,9},{6,10},{7,11},{8,12},{9,13},{1... | collective-permute-start | bytes 69128 | tf_op jit(solution)/shard_map/ppermute | solution.py:489
  23.0 5.2 %collective-permute-start.8 = (bf16[30,384]{1,0:T(8,128)(2,1)S(1)}, bf16[30,384]{1,0:T(8,128)(2,1)S(1)}, u32[]{:S(2)}, u32[]{:S(2)}) collective-permute-start(bf16[30,384]{1,0:T(8,128)(2,1)S(1)} %get-tuple-element.54), channel_id=1, source_target_pairs={{0,12},{1,13},{2,14},{3,15},{4,0},{5,1},{6,2},{7,3},{8,4},{9,5},{1... | collective-permute-start | bytes 69128 | tf_op jit(solution)/shard_map/ppermute | solution.py:489
  28.3 5.4 %collective-permute-start.10 = (bf16[96,384]{1,0:T(8,128)(2,1)S(1)}, bf16[96,384]{1,0:T(8,128)(2,1)S(1)}, u32[]{:S(2)}, u32[]{:S(2)}) collective-permute-start(bf16[96,384]{1,0:T(8,128)(2,1)S(1)} %pad_maximum_fusion.2), channel_id=1, source_target_pairs={{0,3},{1,0},{2,1},{3,2},{4,7},{5,4},{6,5},{7,6},{8,11},{9,8},{10,9... | collective-permute-start | bytes 221192 | tf_op jit(solution)/shard_map/ppermute | solution.py:489
  31.5 5.3 %collective-permute-start.9 = (bf16[96,384]{1,0:T(8,128)(2,1)S(1)}, bf16[96,384]{1,0:T(8,128)(2,1)S(1)}, u32[]{:S(2)}, u32[]{:S(2)}) collective-permute-start(bf16[96,384]{1,0:T(8,128)(2,1)S(1)} %pad_maximum_fusion.2), channel_id=1, source_target_pairs={{0,1},{1,2},{2,3},{3,0},{4,5},{5,6},{6,7},{7,4},{8,9},{9,10},{10,1... | collective-permute-start | bytes 221192 | tf_op jit(solution)/shard_map/ppermute | solution.py:489
  36.8 22.3 %copy-start.2 = (bf16[256,512]{1,0:T(8,128)(2,1)S(1)}, bf16[256,512]{1,0:T(8,128)(2,1)}, u32[]{:S(2)}) copy-start(bf16[256,512]{1,0:T(8,128)(2,1)} %up.1) | copy-start | bytes 786436
  36.8 22.3 %copy-start.3 = (bf16[64,1728]{1,0:T(8,128)(2,1)S(1)}, bf16[64,1728]{1,0:T(8,128)(2,1)}, u32[]{:S(2)}) copy-start(bf16[64,1728]{1,0:T(8,128)(2,1)} %bottom.2) | copy-start | bytes 663556
  36.8 22.3 %copy-start.4 = (bf16[64,1728]{1,0:T(8,128)(2,1)S(1)}, bf16[64,1728]{1,0:T(8,128)(2,1)}, u32[]{:S(2)}) copy-start(bf16[64,1728]{1,0:T(8,128)(2,1)} %m1.1) | copy-start | bytes 663556
  36.8 22.3 %copy-start.5 = (bf16[64,1728]{1,0:T(8,128)(2,1)S(1)}, bf16[64,1728]{1,0:T(8,128)(2,1)}, u32[]{:S(2)}) copy-start(bf16[64,1728]{1,0:T(8,128)(2,1)} %m2.1) | copy-start | bytes 663556
  36.8 22.3 %copy-start.10 = (bf16[32,864]{1,0:T(8,128)(2,1)S(1)}, bf16[32,864]{1,0:T(8,128)(2,1)}, u32[]{:S(2)}) copy-start(bf16[32,864]{1,0:T(8,128)(2,1)} %f1.1) | copy-start | bytes 165892
  36.9 22.3 %copy-start.11 = (bf16[32,864]{1,0:T(8,128)(2,1)S(1)}, bf16[32,864]{1,0:T(8,128)(2,1)}, u32[]{:S(2)}) copy-start(bf16[32,864]{1,0:T(8,128)(2,1)} %f2.1) | copy-start | bytes 165892
  36.9 22.3 %copy-start.12 = (bf16[64,256]{1,0:T(8,128)(2,1)S(1)}, bf16[64,256]{1,0:T(8,128)(2,1)}, u32[]{:S(2)}) copy-start(bf16[64,256]{1,0:T(8,128)(2,1)} %up_fine.1) | copy-start | bytes 98308
  36.9 1.5 %collective-permute-start.11 = (bf16[96,1152]{1,0:T(8,128)(2,1)S(1)}, bf16[96,1152]{1,0:T(8,128)(2,1)S(1)}, u32[]{:S(2)}, u32[]{:S(2)}) collective-permute-start(bf16[96,1152]{1,0:T(8,128)(2,1)S(1)} %pad_maximum_fusion.1.own), channel_id=1, source_target_pairs={{0,16},{16,0},{1,17},{17,1},{2,18},{18,2},{3,19},{19,3},{4,20},{20... | collective-permute-start | bytes 663560 | tf_op jit(solution)/shard_map/ppermute | solution.py:609
  37.0 4.9 %collective-permute-start.12 = (bf16[32,1728]{1,0:T(8,128)(2,1)S(1)}, bf16[32,1728]{1,0:T(8,128)(2,1)S(1)}, u32[]{:S(2)}, u32[]{:S(2)}) collective-permute-start(bf16[32,1728]{1,0:T(8,128)(2,1)S(1)} %collective-permute-done.6.turned), channel_id=1, source_target_pairs={{0,16},{16,0},{1,17},{17,1},{2,18},{18,2},{3,19},{19,3},{4,20},{20... | collective-permute-start | bytes 331784 | tf_op jit(solution)/shard_map/ppermute | solution.py:603
  55.5 6.9 %collective-permute-start.15 = (bf16[72,768]{1,0:T(8,128)(2,1)S(1)}, bf16[72,768]{1,0:T(8,128)(2,1)S(1)}, u32[]{:S(2)}, u32[]{:S(2)}) collective-permute-start(bf16[72,768]{1,0:T(8,128)(2,1)S(1)} %bottom_start.1.refs_0_), channel_id=1, source_target_pairs={{0,3},{1,2},{2,1},{3,0},{4,7},{5,6},{6,5},{7,4},{8,11},{9,10},{10,... | collective-permute-start | bytes 331784 | tf_op jit(solution)/shard_map/ppermute | solution.py:649
  56.8 6.9 %collective-permute-start.14 = (bf16[72,768]{1,0:T(8,128)(2,1)S(1)}, bf16[72,768]{1,0:T(8,128)(2,1)S(1)}, u32[]{:S(2)}, u32[]{:S(2)}) collective-permute-start(bf16[72,768]{1,0:T(8,128)(2,1)S(1)} %bottom_start.1.refs_0_), channel_id=1, source_target_pairs={{0,2},{1,3},{2,0},{3,1},{4,6},{5,7},{6,4},{7,5},{8,10},{9,11},{10,... | collective-permute-start | bytes 331784 | tf_op jit(solution)/shard_map/ppermute | solution.py:649
  58.1 5.6 %collective-permute-start.13 = (bf16[72,768]{1,0:T(8,128)(2,1)S(1)}, bf16[72,768]{1,0:T(8,128)(2,1)S(1)}, u32[]{:S(2)}, u32[]{:S(2)}) collective-permute-start(bf16[72,768]{1,0:T(8,128)(2,1)S(1)} %bottom_start.1.refs_0_), channel_id=1, source_target_pairs={{0,1},{1,0},{2,3},{3,2},{4,5},{5,4},{6,7},{7,6},{8,9},{9,8},{10,11... | collective-permute-start | bytes 331784 | tf_op jit(solution)/shard_map/ppermute | solution.py:649
  80.3 1.7 %collective-permute-start.16 = (bf16[16,88,128]{2,1,0:T(8,128)(2,1)S(1)}, bf16[16,88,128]{2,1,0:T(8,128)(2,1)S(1)}, u32[]{:S(2)}, u32[]{:S(2)}) collective-permute-start(bf16[16,88,128]{2,1,0:T(8,128)(2,1)S(1)} %all_to_all.11.near), channel_id=1, source_target_pairs={{0,16},{16,0},{1,17},{17,1},{2,18},{18,2},{3,19},{19,3},{4,20},{20... | collective-permute-start | bytes 1081352 | tf_op jit(solution)/shard_map/ppermute | solution.py:665

commit v4 on v3

--- a/solution.py
+++ b/solution.py
@@ -111,12 +111,13 @@
     shrink_table(down, flat, reduce[...], 32, 2)
 
 
-def middle_tables(first, second, reduce, first_table, second_table, downs, flat):
+def middle_tables(first, second, reduce, first_table, second_table, down, flat):
     conv_table(first_table, flat, first[...], 64)
     conv_table(second_table, flat, second[...], 64)
-    for quarter in range(downs.shape[0]):
-        rows = reduce[64 * quarter : 64 * (quarter + 1), :]
-        shrink_table(downs.at[quarter], flat, rows, 64, 0)
+    across = reduce.shape[0] // 64
+    column = lax.axis_index("yz") % across
+    rows = reduce[pl.ds(pl.multiple_of(column * 64, 64), 64), :]
+    shrink_table(down, flat, rows, 64, 0)
 
 
 def decoder_tables(bottom, up, m1, m2, up_fine, f1, f2, *refs):
@@ -195,8 +196,11 @@
         for y in range(count):
             value = halves[0, pl.ds(16 * y + 2, count, 2), :]
             value = value + halves[1, pl.ds(16 * y + 3, count, 2), :]
-            flats[count * y : count * (y + 1), span_of(tile)] = value
-    small[...] = flats[...].astype(BF)
+            row = count * (count * tile + y)
+            flats[row : row + count, :] = value
+    result = flats[...].astype(BF)
+    for copy in range(small.shape[0]):
+        small[copy] = result
 
 
 def wrap_rows(wide, layers, count):
@@ -206,44 +210,62 @@
     wide[layers + 1 : layers + 2] = wide[1:2]
 
 
+def wrap_x(wide, layers, count):
+    wide[:layers, 7:8, :] = wide[:layers, 7 + count : 8 + count, :]
+    wide[:layers, 8 + count : 9 + count, :] = wide[:layers, 8:9, :]
+
+
 def middle(
-    own, other, first_table, second_table, downs, window, sent, wide, s, whole, halves, flats
+    own, other, first_table, second_table, down, window, shrunk, wide, s, whole, halves, flats
 ):
-    span = own.shape[1]
-    side = span // 3 // 64
-    reach = side - 1
-    layers = side + 2 * reach
-    near, far = own[...].astype(F32), other[...].astype(F32)
-    for y in range(layers):
-        start = side * y
-        wide[y, 0:reach, :span] = far[start + 1 : start + side]
-        wide[y, reach : reach + side, :span] = near[start : start + side]
-        wide[y, reach + side : 2 * reach + side, :span] = far[start : start + reach]
-    stage(wide, s, layers, 16, 0, span)
+    across = math.isqrt(own.shape[0])
+    side = window.shape[0] // 2
+    lanes = side * 64
+    span = across * lanes
+    place, core = lax.axis_index("yz"), lax.axis_index("gx")
+    row, column = place // across, place % across
+    layers = 3 * side
+    for k in range(3):
+        i = (row + across // 2 * core + k + across - 1) % across
+        for spot, j in enumerate([across - 1] + list(range(across))):
+            start = spot * lanes
+            size = min(lanes, span + LANES - start)
+            for part, gathered in enumerate((own, other)):
+                block = gathered[i * across + j].astype(F32)
+                for y in range(side):
+                    for tile in range(size // LANES):
+                        first = side * (side * tile + y)
+                        wide[
+                            side * k + y,
+                            8 + side * part : 8 + side * (part + 1),
+                            start + LANES * tile : start + LANES * (tile + 1),
+                        ] = block[first : first + side]
+    wrap_x(wide, layers, 2 * side)
+    stage(wide, s, layers, 16, 7, span + LANES)
     layers -= 2
-    tiles = span // LANES - 1
-    for tile in range(tiles):
+    for tile in range(span // LANES):
         value = rounded_relu(convolve(s, first_table, layers, 16, tile))
-        wide[:layers, 0:16, span_of(tile)] = value.astype(F32).reshape(layers, 16, LANES)
-    stage(wide, s, layers, 16, 0, tiles * LANES)
+        wide[:layers, 8:24, span_of(tile)] = value.astype(F32).reshape(layers, 16, LANES)
+    wide[:layers, :, span : span + LANES] = wide[:layers, :, 0:LANES]
+    wrap_x(wide, layers, 2 * side)
+    stage(wide, s, layers, 16, 7, span + LANES)
     layers -= 2
-    for tile in range(tiles - 1):
-        value = rounded_relu(convolve(s, second_table, layers, 16, tile)).reshape(layers, 16, LANES)
-        whole[:, :, span_of(tile)] = value
-        wide[:layers, 0:16, span_of(tile)] = value.astype(F32)
-    width = window.shape[2]
-    skipped = layers - side - 3
-    wide[:layers, 16 : 16 + layers - 3, :width] = wide[:layers, 3:layers, :width]
-    wide[:layers, 13 + layers : 16 + layers, :width] = wide[:layers, 0:3, :width]
-    window[...] = wide[:layers, 16:32, :width].astype(BF)
-    half = side // 2
-    lefts = [
-        jnp.concatenate(
+    for tile in range(span // LANES):
+        value = rounded_relu(convolve(s, second_table, layers, 16, tile))
+        whole[:, :, span_of(tile)] = value.reshape(layers, 16, LANES)
+    whole[:, :, span : span + 512] = whole[:, :, 0:512]
+    window[...] = whole[
+        1 : 1 + window.shape[0],
+        :,
+        pl.ds(pl.multiple_of(column * lanes, LANES), window.shape[2]),
+    ]
+    for tile in range(shrunk.shape[1] // LANES):
+        left = jnp.concatenate(
             [
                 jnp.concatenate(
                     [
-                        whole[skipped + 2 * y + dy, :, (tile + 1) * DEPTH : (tile + 2) * DEPTH]
-                        for y in range(half)
+                        whole[2 * y + dy, :, tile * DEPTH : (tile + 1) * DEPTH]
+                        for y in range(side)
                     ],
                     axis=0,
                 )
@@ -251,66 +273,33 @@
             ],
             axis=1,
         )
-        for tile in range(2)
-    ]
-    across = downs.shape[0]
-    for quarter in range(across):
-        for tile, left in enumerate(lefts):
-            total = dot(left, downs[quarter])
-            halves[0] = total[:, :LANES]
-            halves[1] = total[:, LANES:]
-            for y in range(half):
-                value = halves[0, pl.ds(16 * y + 3, half, 2), :]
-                value = value + halves[1, pl.ds(16 * y + 4, half, 2), :]
-                row = half * (half * tile + y)
-                flats[row : row + half, :] = value
-        count = half * half
-        fold = (count + 1) // 2
-        last = flats[count : count + 16, :]
-        turn = pltpu.roll(last, 64, 1)
-        flats[count : count + fold, :] = jnp.where(
-            lane_group(fold, 64) == 0, last[:fold], turn[fold : 2 * fold]
-        )
-        result = flats[0 : sent.shape[1], :].astype(BF)
-        for target in range(quarter, sent.shape[0], across):
-            sent[target] = result
-
-
-def bottom_start(gathered, turned, swapped, partial, wide, s, table, flat, flats):
+        total = dot(left, down[...])
+        halves[0] = total[:, :LANES]
+        halves[1] = total[:, LANES:]
+        for y in range(side):
+            value = halves[0, pl.ds(16 * y, side, 2), :]
+            value = value + halves[1, pl.ds(16 * y + 1, side, 2), :]
+            flats[side * y : side * (y + 1), span_of(tile)] = value
+    shrunk[...] = flats[...].astype(BF)
+
+
+def bottom_start(near, far, turned, swapped, partial, wide, s, table, flat, flats):
     span = partial.shape[1]
     cells = span // 64
     side = cells // 2
     core = lax.axis_index("gx")
-    devices = gathered.shape[0] // 2
-    across = math.isqrt(devices)
-    half = cells // across
-    count = half * half
-    fold = (count + 1) // 2
-    low = lane_group(count, 64) == 0
-    for part in range(2):
-        base = (core if part == 0 else 1 - core) * devices
-        for i in range(across):
-            for j in range(0, across, 2):
-                here = gathered[base + across * i + j].astype(F32)
-                after = gathered[base + across * i + j + 1].astype(F32)
-                here_turn, after_turn = pltpu.roll(here, 64, 1), pltpu.roll(after, 64, 1)
-
-                def unfold(one, two):
-                    return jnp.concatenate([one[count : count + fold], two[count : 2 * count - fold]])
-
-                pieces = (
-                    here[:count],
-                    jnp.where(low, unfold(here, here_turn), after_turn[:count]),
-                    jnp.where(low, after_turn[:count], unfold(after_turn, after)),
-                )
-                for turn, piece in enumerate(pieces):
-                    tile = half * (j // 2) + turn
-                    for y in range(half):
-                        wide[
-                            1 + half * i + y,
-                            8 + half * part : 8 + half * (part + 1),
-                            span_of(tile),
-                        ] = piece[half * y : half * (y + 1)]
+    across = cells * 2 // side
+    block = side // 2
+    row = lax.axis_index("yz") // across
+    for part, given in enumerate((near, far)):
+        values = given[...].astype(F32)
+        half = core if part == 0 else 1 - core
+        for y in range(side):
+            layer = (block * row + side * half + y + cells - 2) % cells + 1
+            value = values[side * y : side * (y + 1)]
+            if part == 1:
+                value = jnp.concatenate([value[block:], value[:block]], axis=0)
+            wide[pl.ds(layer, 1), 8 : 8 + side, :span] = value[None]
     wide[1 : cells + 1, 8 : 8 + side, span : span + LANES] = wide[
         1 : cells + 1, 8 : 8 + side, 0:LANES
     ]
@@ -348,10 +337,11 @@
     stage(wide, s, cells + 2, 16, 7, span + LANES)
     for tile in range(span // LANES):
         value = convolve(s, table, cells, 16, tile).reshape(cells, 16, LANES)
-        whole[2 : cells + 2, :, span_of(tile + 2)] = value[:, :8]
+        whole[2 : cells + 2, :, span_of(tile + 1)] = value[:, :8]
     whole[0:2] = whole[cells : cells + 2]
     whole[cells + 2 : cells + 5] = whole[2:5]
-    whole[:, :, 0 : 2 * LANES] = whole[:, :, span : span + 2 * LANES]
+    whole[:, :, 0:LANES] = whole[:, :, span : span + LANES]
+    whole[:, :, span + LANES : span + 512] = whole[:, :, LANES:512]
     block = cells // across
     kept = side // 2
     layers = block + 4
@@ -373,6 +363,7 @@
     near,
     far,
     window,
+    far_window,
     skip,
     lift,
     m1_table,
@@ -424,8 +415,15 @@
                             16 * y : 16 * y + 2 * kept, span_of(half)
                         ]
     count = window.shape[0]
+    is_first = lax.axis_index("gx") == 0
     for tile in range(window.shape[2] // LANES):
-        total = spread[tile, 1 : count + 1, 8:24, :] + window[:, :, span_of(tile)].astype(F32)
+        theirs = far_window[:, :, span_of(tile)].astype(F32)
+        wide[:count, 8 : 8 + count // 2, span_of(tile)] = theirs[:, count // 2 : count]
+        wide[:count, 8 + count // 2 : 8 + count, span_of(tile)] = theirs[:, : count // 2]
+        kept_here = jnp.where(
+            is_first, window[:, :, span_of(tile)].astype(F32), wide[:count, 8:24, span_of(tile)]
+        )
+        total = spread[tile, 1 : count + 1, 8:24, :] + kept_here
         wide[:count, 8:24, span_of(tile)] = total.astype(BF).astype(F32)
     ends = 8 + count
     wide[:, 7:8, :] = wide[:, ends - 1 : ends, :]
@@ -536,7 +534,7 @@
     )
     middle_tabs = call(
         middle_tables,
-        (table, table, jax.ShapeDtypeStruct((across, *down.shape), BF)),
+        (table, table, down),
         [flat],
         encode_middle_first,
         encode_middle_second,
@@ -583,14 +581,14 @@
         fine_encoder,
         (
             jax.ShapeDtypeStruct((ext + 4, ext + 4, (ext + 4) * fine), BF),
-            jax.ShapeDtypeStruct((side * side, side * mid), BF),
+            jax.ShapeDtypeStruct((devices, 112, LANES), BF),
         ),
         [
             pltpu.VMEM((seen, 40, seen * fine), F32),
             pltpu.VMEM((3, seen * 32, seen * fine), BF),
             pltpu.VMEM((3, (seen - 2) * 16, seen * fine), BF),
             pltpu.VMEM((2, side * 16, LANES), F32),
-            pltpu.VMEM((side * side, side * mid), F32),
+            pltpu.VMEM((112, LANES), F32),
         ],
         low,
         cells,
@@ -601,35 +599,30 @@
     small, turned = lax.optimization_barrier((small, turned))
     swap = [(s, around(s, 1)) for s in range(cores)]
     swapped = lax.ppermute(turned, "gx", swap)
-    reach = (side - 1) * side
-    low, high = exchange(small[:reach], small[side:], "yz", along_y)
-    small = jnp.concatenate([low, small, high], axis=0)
-    low, high = exchange(small, small, "yz", along_z)
-    own = jnp.concatenate([low, small, high], axis=1)
+    own = lax.all_to_all(small, "yz", 0, 0)
     other = lax.ppermute(own, "gx", swap)
 
     total = side * across
     half = total // 2
-    layers, span = 3 * side - 2, 3 * side * mid
-    window, sent = call(
+    span = total * mid
+    window, shrunk = call(
         middle,
         (
-            jax.ShapeDtypeStruct((layers - 4, 16, 14 * mid), BF),
-            jax.ShapeDtypeStruct((devices * cores, 16, LANES), BF),
+            jax.ShapeDtypeStruct((2 * side, 16, 14 * mid), BF),
+            jax.ShapeDtypeStruct((side * side, half * mid), BF),
         ),
         [
-            pltpu.VMEM((layers, 32, span), F32),
-            pltpu.VMEM((3, layers * 16, span), BF),
-            pltpu.VMEM((layers - 4, 16, 14 * mid), BF),
-            pltpu.VMEM((2, side * 8, LANES), F32),
-            pltpu.VMEM((32, LANES), F32),
+            pltpu.VMEM((3 * side, 32, span + LANES), F32),
+            pltpu.VMEM((3, 3 * side * 16, span + LANES), BF),
+            pltpu.VMEM((3 * side - 4, 16, span + 512), BF),
+            pltpu.VMEM((2, side * 16, LANES), F32),
+            pltpu.VMEM((side * side, half * mid), F32),
         ],
         own,
         other,
         *middle_tabs,
     )
-    sent, swapped = lax.optimization_barrier((sent, swapped))
-    gathered = lax.all_to_all(sent, ("gx", "yz"), 0, 0)
+    far_shrunk = lax.ppermute(shrunk, "gx", swap)
     partial = call(
         bottom_start,
         jax.ShapeDtypeStruct((half * side, half * mid), BF),
@@ -640,10 +633,13 @@
             flat,
             pltpu.VMEM((half * side, half * mid), F32),
         ],
-        gathered,
+        shrunk,
+        far_shrunk,
         turned,
         swapped,
     )
+    partial, window = lax.optimization_barrier((partial, window))
+    far_window = lax.ppermute(window, "gx", swap)
 
     pieces = [partial] + [
         lax.ppermute(partial, "yz", [(s, s ^ turn) for s in range(devices)])
@@ -655,12 +651,13 @@
         [
             pltpu.VMEM((half + 2, 32, half * mid + LANES), F32),
             pltpu.VMEM((3, (half + 2) * 16, half * mid + LANES), BF),
-            pltpu.VMEM((half + 5, 8, half * mid + 2 * LANES), F32),
+            pltpu.VMEM((half + 5, 8, half * mid + 512), F32),
             pltpu.VMEM((88, LANES), F32),
         ],
         *pieces,
         bottom_tab,
     )
+    sent, far_window = lax.optimization_barrier((sent, far_window))
     near = lax.all_to_all(sent, "yz", 0, 0)
     far = lax.ppermute(near, "gx", swap)
 
@@ -676,6 +673,7 @@
         near,
         far,
         window,
+        far_window,
         skip,
         *decoder_tabs,
     )

time: 88.6 us -> 87.6 us (0.989)
  blocking collectives: 27.1 us -> 37.5 us
  starting transfers between devices: 22.1 us -> 14 us
  waiting for transfers between devices: 17 us -> 11.6 us
  Pallas kernels: 17.7 us -> 19.8 us
    all_to_all x1, blocking collectives: 12 us -> 21.7 us  [gathered_body(): own = lax.all_to_all(small, 'yz', 0, 0)]
    ppermute x10 -> x6, starting transfers between devices: 17.2 us -> 8.74 us  [exchange(): return (lax.ppermute(tail, axis, ahead), lax.ppermute(head, axis, back))]
    ppermute x10 -> x6, waiting for transfers between devices: 12.1 us -> 5.09 us  [exchange(): return (lax.ppermute(tail, axis, ahead), lax.ppermute(head, axis, back))]
    pallas_call x8, Pallas kernels: 17.7 us -> 19.8 us  [call(): pl.pallas_call(kernel, out_shape=jax.tree.map(lambda out: pltpu.VMEM(out....]
    ppermute x0 -> x2, waiting for transfers between devices: none -> 1.11 us  [the longest x1 1.11 us: gathered_body(): far_shrunk = lax.ppermute(shrunk, 'gx', swap)]
  transfers between devices with their start and end apart: 17 -> 15, of which waited for: 13 -> 12; matrix products, arithmetic and copies ran while one was open for 1% -> 1% of each run, Pallas kernels for 11% -> 16%
where the time goes in v4:
time: 87.6 us; the launch traced here: 87.4 us
  blocking collectives  37.5 us (43%)
  Pallas kernels  19.8 us (23%)
  starting transfers between devices  14 us (16%)
  waiting for transfers between devices  11.6 us (13%)
  local copies, waits for them, and re-layouts  4.12 us (5%)
    all_to_all x1, blocking collectives, gathered_body(): own = lax.all_to_all(small, 'yz', 0, 0)  21.7 us
    pallas_call x8, Pallas kernels, call(): pl.pallas_call(kernel, out_shape=jax.tree.map(lambda out: pltpu.VMEM(out....  19.8 us
    all_to_all x1, blocking collectives, gathered_body(): near = lax.all_to_all(sent, 'yz', 0, 0)  15.8 us
    ppermute x6, starting transfers between devices, exchange(): return (lax.ppermute(tail, axis, ahead), lax.ppermute(head, axis, back))  8.74 us
    ppermute x6, waiting for transfers between devices, exchange(): return (lax.ppermute(tail, axis, ahead), lax.ppermute(head, axis, back))  5.09 us
    ppermute x3, starting transfers between devices, gathered_body(): lax.ppermute(partial, 'yz', [(s, s ^ turn) for s in range(devices)])  3.49 us
    ppermute x3, waiting for transfers between devices, gathered_body(): lax.ppermute(partial, 'yz', [(s, s ^ turn) for s in range(devices)])  2.98 us
  transfers between devices with their start and end apart: 15, of which 12 were waited for; matrix products, arithmetic and copies ran while one was open for 1% of the time, Pallas kernels for 16%

profile of v4, /device:TPU:0, one launch (start us, length us, event | category | flops | bytes accessed | tf_op | source)
XLA Modules:
  0.0 87.4 jit_solution(608608694790244737)
XLA Ops:
  0.0 1.2 %copy.18 = bf16[1,32,12,144]{1,3,2,0:T(8,128)(2,1)S(1)} copy(bf16[1,32,12,144]{3,1,2,0:T(8,128)(2,1)} %param.15) | data formatting | bytes 221184 | tf_op args[0]
  1.2 0.1 reshape.14
  1.4 0.0 copy-start.8
  1.4 0.0 copy-start.9
  1.4 0.0 copy-start.13
  1.5 0.2 slice.28
  1.6 3.1 %collective-permute-start = (bf16[4,12,384]{2,1,0:T(8,128)(2,1)S(1)}, bf16[4,12,384]{2,1,0:T(8,128)(2,1)S(1)}, u32[]{:S(2)}, u32[]{:S(2)}) collective-permute-start(bf16[4,12,384]{2,1,0:T(8,128)(2,1)S(1)} %copy.19), channel_id=1, source_target_pairs={{0,4},{1,5},{2,6},{3,7},{4,8},{5,9},{6,10},{7,11},{8,12},{9,13},{1... | collective-permute-start | bytes 110600 | tf_op jit(solution)/shard_map/ppermute | solution.py:487
  4.7 0.2 slice.30
  4.9 2.1 %collective-permute-start.1 = (bf16[4,12,384]{2,1,0:T(8,128)(2,1)S(1)}, bf16[4,12,384]{2,1,0:T(8,128)(2,1)S(1)}, u32[]{:S(2)}, u32[]{:S(2)}) collective-permute-start(bf16[4,12,384]{2,1,0:T(8,128)(2,1)S(1)} %copy.21), channel_id=1, source_target_pairs={{0,12},{1,13},{2,14},{3,15},{4,0},{5,1},{6,2},{7,3},{8,4},{9,5},{1... | collective-permute-start | bytes 110600 | tf_op jit(solution)/shard_map/ppermute | solution.py:487
  7.0 0.4 reshape.18
  7.5 1.5 %collective-permute-done = bf16[4,12,384]{2,1,0:T(8,128)(2,1)S(1)} collective-permute-done((bf16[4,12,384]{2,1,0:T(8,128)(2,1)S(1)}, bf16[4,12,384]{2,1,0:T(8,128)(2,1)S(1)}, u32[]{:S(2)}, u32[]{:S(2)}) %collective-permute-start) | collective-permute-done | bytes 36896 | tf_op jit(solution)/shard_map/ppermute | solution.py:487
  9.0 0.5 collective-permute-done.1
  9.5 1.7 %collective-permute-start.2 = (bf16[20,12,128]{2,1,0:T(8,128)(2,1)S(1)}, bf16[20,12,128]{2,1,0:T(8,128)(2,1)S(1)}, u32[]{:S(2)}, u32[]{:S(2)}) collective-permute-start(bf16[20,12,128]{2,1,0:T(8,128)(2,1)S(1)} %get-tuple-element.55), channel_id=1, source_target_pairs={{0,1},{1,2},{2,3},{3,0},{4,5},{5,6},{6,7},{7,4},{8,9},{9,10},{10,1... | collective-permute-start | bytes 184328 | tf_op jit(solution)/shard_map/ppermute | solution.py:487
  11.2 1.3 %collective-permute-start.3 = (bf16[20,12,128]{2,1,0:T(8,128)(2,1)S(1)}, bf16[20,12,128]{2,1,0:T(8,128)(2,1)S(1)}, u32[]{:S(2)}, u32[]{:S(2)}) collective-permute-start(bf16[20,12,128]{2,1,0:T(8,128)(2,1)S(1)} %get-tuple-element.56), channel_id=1, source_target_pairs={{0,3},{1,0},{2,1},{3,2},{4,7},{5,4},{6,5},{7,6},{8,11},{9,8},{10,9... | collective-permute-start | bytes 184328 | tf_op jit(solution)/shard_map/ppermute | solution.py:487
  12.5 0.0 copy-start.1
  12.5 0.0 copy-start.6
  12.5 0.0 copy-start.7
  12.5 0.8 collective-permute-start.6
  13.4 1.6 %collective-permute-done.2 = bf16[20,12,128]{2,1,0:T(8,128)(2,1)S(1)} collective-permute-done((bf16[20,12,128]{2,1,0:T(8,128)(2,1)S(1)}, bf16[20,12,128]{2,1,0:T(8,128)(2,1)S(1)}, u32[]{:S(2)}, u32[]{:S(2)}) %collective-permute-start.2) | collective-permute-done | bytes 61472 | tf_op jit(solution)/shard_map/ppermute | solution.py:487
  14.9 1.0 %collective-permute-done.3 = bf16[20,12,128]{2,1,0:T(8,128)(2,1)S(1)} collective-permute-done((bf16[20,12,128]{2,1,0:T(8,128)(2,1)S(1)}, bf16[20,12,128]{2,1,0:T(8,128)(2,1)S(1)}, u32[]{:S(2)}, u32[]{:S(2)}) %collective-permute-start.3) | collective-permute-done | bytes 61472 | tf_op jit(solution)/shard_map/ppermute | solution.py:487
  16.0 0.1 pad_maximum_fusion.mid
  16.0 0.1 fusion.1
  16.1 0.1 collective-permute-start.4
  16.2 0.5 collective-permute-start.5
  16.7 0.4 fine_tables.1
  17.1 0.4 collective-permute-done.4.low
  17.5 0.2 collective-permute-done.5.high
  17.6 3.6 %fine_encoder.1 = (bf16[16,16,512]{2,1,0:T(8,128)(2,1)S(1)}, bf16[16,112,128]{2,1,0:T(8,128)(2,1)S(1)}) custom-call(bf16[20,4,640]{2,1,0:T(4,128)(2,1)S(1)} %collective-permute-done.4.low, bf16[20,12,640]{2,1,0:T(8,128)(2,1)S(1)} %pad_maximum_fusion.mid, bf16[20,4,640]{2,1,0:T(4,128)(2,1)S(1)} %collective-permute-done.5.high, ...), custom_call_target="tpu_custom_call" | custom-call | tf_op jit(solution)/shard_map/fine_encoder/pallas_call | solution.py:469
  21.3 0.0 collective-permute-done.6.turned
  21.3 0.0 copy-start.2
  21.3 0.0 copy-start.3
  21.3 0.0 copy-start.4
  21.3 0.0 copy-start.5
  21.3 0.0 copy-start.10
  21.3 0.0 copy-start.11
  21.3 0.0 copy-start.12
  21.4 21.7 %all_to_all.10.own = bf16[16,112,128]{2,1,0:T(8,128)(2,1)S(1)} all-to-all(bf16[16,112,128]{2,1,0:T(8,128)(2,1)S(1)} %get-tuple-element.32), channel_id=1, replica_groups=mesh['gx'=2,'yz'=16] {'yz'}, dimensions={0} | all-to-all | bytes 917504 | tf_op jit(solution)/shard_map/all_to_all | solution.py:602
  43.1 0.0 collective-permute-start.7
  43.1 0.5 collective-permute-start.9
  43.6 0.5 middle_tables.1
  44.1 0.7 collective-permute-done.7.other
  44.9 5.9 %middle.1 = (bf16[12,16,896]{2,1,0:T(8,128)(2,1)S(1)}, bf16[36,768]{1,0:T(8,128)(2,1)S(1)}) custom-call(bf16[16,112,128]{2,1,0:T(8,128)(2,1)S(1)} %all_to_all.10.own, bf16[16,112,128]{2,1,0:T(8,128)(2,1)S(1)} %collective-permute-done.7.other, bf16[768,384]{1,0:T(8,128)(2,1)S(1)} %get-tuple-element.33.first_table, ...), custom_call_target="tpu_custom_call" | custom-call | tf_op jit(solution)/shard_map/middle/pallas_call | solution.py:469
  50.8 0.2 collective-permute-start.8
  51.0 0.0 collective-permute-done.9.swapped
  51.0 1.1 %collective-permute-done.8.far = bf16[36,768]{1,0:T(8,128)(2,1)S(1)} collective-permute-done((bf16[36,768]{1,0:T(8,128)(2,1)S(1)}, bf16[36,768]{1,0:T(8,128)(2,1)S(1)}, u32[]{:S(2)}, u32[]{:S(2)}) %collective-permute-start.8) | collective-permute-done | bytes 55328 | tf_op jit(solution)/shard_map/ppermute | solution.py:625
  52.1 1.5 %bottom_start.1.refs_0_ = bf16[72,768]{1,0:T(8,128)(2,1)S(1)} custom-call(bf16[36,768]{1,0:T(8,128)(2,1)S(1)} %get-tuple-element.36.near, bf16[36,768]{1,0:T(8,128)(2,1)S(1)} %collective-permute-done.8.far, bf16[32,1728]{1,0:T(8,128)(2,1)S(1)} %collective-permute-done.6.turned, bf16[32,1728]{1,0:T(8,128)(2,1)S(1)} %collective-permute-done.9.swapped), custom_call_target="tpu_custom_call" | custom-call | tf_op jit(solution)/shard_map/bottom_start/pallas_call | solution.py:469
  53.6 0.2 collective-permute-start.13
  53.9 0.6 collective-permute-start.10
  54.4 0.9 collective-permute-start.11
  55.3 2.1 %collective-permute-start.12 = (bf16[72,768]{1,0:T(8,128)(2,1)S(1)}, bf16[72,768]{1,0:T(8,128)(2,1)S(1)}, u32[]{:S(2)}, u32[]{:S(2)}) collective-permute-start(bf16[72,768]{1,0:T(8,128)(2,1)S(1)} %bottom_start.1.refs_0_), channel_id=1, source_target_pairs={{0,3},{1,2},{2,1},{3,0},{4,7},{5,6},{6,5},{7,4},{8,11},{9,10},{10,... | collective-permute-start | bytes 331784 | tf_op jit(solution)/shard_map/ppermute | solution.py:645
  57.4 1.5 %decoder_tables.1 = (bf16[768,384]{1,0:T(8,128)(2,1)S(1)}, bf16[4,1024,256]{2,1,0:T(8,128)(2,1)S(1)}, bf16[768,384]{1,0:T(8,128)(2,1)S(1)}, bf16[768,384]{1,0:T(...) custom-call(bf16[64,1728]{1,0:T(8,128)(2,1)S(1)} %copy-done.3, ...), custom_call_target="tpu_custom_call" | custom-call | tf_op jit(solution)/shard_map/decoder_tables/pallas_call | solution.py:469
  58.9 0.9 %collective-permute-done.10.refs_1_ = bf16[72,768]{1,0:T(8,128)(2,1)S(1)} collective-permute-done((bf16[72,768]{1,0:T(8,128)(2,1)S(1)}, bf16[72,768]{1,0:T(8,128)(2,1)S(1)}, u32[]{:S(2)}, u32[]{:S(2)}) %collective-permute-start.10) | collective-permute-done | bytes 110624 | tf_op jit(solution)/shard_map/ppermute | solution.py:645
  59.8 0.3 collective-permute-done.11.refs_2_
  60.1 1.8 %collective-permute-done.12.refs_3_ = bf16[72,768]{1,0:T(8,128)(2,1)S(1)} collective-permute-done((bf16[72,768]{1,0:T(8,128)(2,1)S(1)}, bf16[72,768]{1,0:T(8,128)(2,1)S(1)}, u32[]{:S(2)}, u32[]{:S(2)}) %collective-permute-start.12) | collective-permute-done | bytes 110624 | tf_op jit(solution)/shard_map/ppermute | solution.py:645
  61.9 1.6 %bottom.3 = bf16[16,88,128]{2,1,0:T(8,128)(2,1)S(1)} custom-call(bf16[72,768]{1,0:T(8,128)(2,1)S(1)} %bottom_start.1.refs_0_, bf16[72,768]{1,0:T(8,128)(2,1)S(1)} %collective-permute-done.10.refs_1_, bf16[72,768]{1,0:T(8,128)(2,1)S(1)} %collective-permute-done.11.refs_2_, bf16[72,768]{1,0:T(8,128)(2,1)S(1)} %collective-permute-done.12.refs_3_, ...), custom_call_target="tpu_custom_call" | custom-call | tf_op jit(solution)/shard_map/bottom/pallas_call | solution.py:469
  63.4 0.0 collective-permute-done.13.far_window
  63.4 15.8 %all_to_all.11.near = bf16[16,88,128]{2,1,0:T(8,128)(2,1)S(1)} all-to-all(bf16[16,88,128]{2,1,0:T(8,128)(2,1)S(1)} %bottom.3), channel_id=1, replica_groups=mesh['gx'=2,'yz'=16] {'yz'}, dimensions={0} | all-to-all | bytes 720896 | tf_op jit(solution)/shard_map/all_to_all | solution.py:661
  79.2 0.0 collective-permute-start.14
  79.2 1.7 %collective-permute-done.14.far = bf16[16,88,128]{2,1,0:T(8,128)(2,1)S(1)} collective-permute-done((bf16[16,88,128]{2,1,0:T(8,128)(2,1)S(1)}, bf16[16,88,128]{2,1,0:T(8,128)(2,1)S(1)}, u32[]{:S(2)}, u32[]{:S(2)}) %collective-permute-start.14) | collective-permute-done | bytes 360480 | tf_op jit(solution)/shard_map/ppermute | solution.py:662
  80.9 4.8 %decoder.1 = bf16[12,16,384]{2,1,0:T(8,128)(2,1)S(1)} custom-call(bf16[16,88,128]{2,1,0:T(8,128)(2,1)S(1)} %all_to_all.11.near, bf16[16,88,128]{2,1,0:T(8,128)(2,1)S(1)} %collective-permute-done.14.far, bf16[12,16,896]{2,1,0:T(8,128)(2,1)S(1)} %get-tuple-element.41.window, bf16[12,16,896]{2,1,0:T(8,128)(2,1)S(1)} %collective-permute-done.13.far_window, ...), custom_call_target="tpu_custom_call" | custom-call | tf_op jit(solution)/shard_map/decoder/pallas_call | solution.py:469
  85.6 0.4 reshape.16
  86.1 0.1 copy.27
  86.2 0.2 reshape.17
  86.5 0.9 %copy.23 = bf16[1,32,12,144]{3,1,2,0:T(8,128)(2,1)} copy(bf16[1,32,12,144]{1,3,2,0:T(8,128)(2,1)S(1)} %reshape.17) | data formatting | bytes 221184 | tf_op jit(solution)/shard_map/reshape | solution.py:681
  (23 shorter events, 0.2 us)
Async XLA Ops:
  0.0 12.5 %copy-start = (bf16[64,1728]{1,0:T(8,128)(2,1)S(1)}, bf16[64,1728]{1,0:T(8,128)(2,1)}, u32[]{:S(2)}) copy-start(bf16[64,1728]{1,0:T(8,128)(2,1)} %param.22) | copy-start | bytes 663556
  1.4 15.3 %copy-start.8 = (bf16[32,864]{1,0:T(8,128)(2,1)S(1)}, bf16[32,864]{1,0:T(8,128)(2,1)}, u32[]{:S(2)}) copy-start(bf16[32,864]{1,0:T(8,128)(2,1)} %first.2) | copy-start | bytes 165892
  1.4 15.3 %copy-start.9 = (bf16[32,864]{1,0:T(8,128)(2,1)S(1)}, bf16[32,864]{1,0:T(8,128)(2,1)}, u32[]{:S(2)}) copy-start(bf16[32,864]{1,0:T(8,128)(2,1)} %second.2) | copy-start | bytes 165892
  1.4 15.3 %copy-start.13 = (bf16[64,256]{1,0:T(8,128)(2,1)S(1)}, bf16[64,256]{1,0:T(8,128)(2,1)}, u32[]{:S(2)}) copy-start(bf16[64,256]{1,0:T(8,128)(2,1)} %reduce.2) | copy-start | bytes 98308
  1.6 7.3 %collective-permute-start = (bf16[4,12,384]{2,1,0:T(8,128)(2,1)S(1)}, bf16[4,12,384]{2,1,0:T(8,128)(2,1)S(1)}, u32[]{:S(2)}, u32[]{:S(2)}) collective-permute-start(bf16[4,12,384]{2,1,0:T(8,128)(2,1)S(1)} %copy.19), channel_id=1, source_target_pairs={{0,4},{1,5},{2,6},{3,7},{4,8},{5,9},{6,10},{7,11},{8,12},{9,13},{1... | collective-permute-start | bytes 110600 | tf_op jit(solution)/shard_map/ppermute | solution.py:487
  4.9 4.5 %collective-permute-start.1 = (bf16[4,12,384]{2,1,0:T(8,128)(2,1)S(1)}, bf16[4,12,384]{2,1,0:T(8,128)(2,1)S(1)}, u32[]{:S(2)}, u32[]{:S(2)}) collective-permute-start(bf16[4,12,384]{2,1,0:T(8,128)(2,1)S(1)} %copy.21), channel_id=1, source_target_pairs={{0,12},{1,13},{2,14},{3,15},{4,0},{5,1},{6,2},{7,3},{8,4},{9,5},{1... | collective-permute-start | bytes 110600 | tf_op jit(solution)/shard_map/ppermute | solution.py:487
  9.5 5.4 %collective-permute-start.2 = (bf16[20,12,128]{2,1,0:T(8,128)(2,1)S(1)}, bf16[20,12,128]{2,1,0:T(8,128)(2,1)S(1)}, u32[]{:S(2)}, u32[]{:S(2)}) collective-permute-start(bf16[20,12,128]{2,1,0:T(8,128)(2,1)S(1)} %get-tuple-element.55), channel_id=1, source_target_pairs={{0,1},{1,2},{2,3},{3,0},{4,5},{5,6},{6,7},{7,4},{8,9},{9,10},{10,1... | collective-permute-start | bytes 184328 | tf_op jit(solution)/shard_map/ppermute | solution.py:487
  11.2 4.8 %collective-permute-start.3 = (bf16[20,12,128]{2,1,0:T(8,128)(2,1)S(1)}, bf16[20,12,128]{2,1,0:T(8,128)(2,1)S(1)}, u32[]{:S(2)}, u32[]{:S(2)}) collective-permute-start(bf16[20,12,128]{2,1,0:T(8,128)(2,1)S(1)} %get-tuple-element.56), channel_id=1, source_target_pairs={{0,3},{1,0},{2,1},{3,2},{4,7},{5,4},{6,5},{7,6},{8,11},{9,8},{10,9... | collective-permute-start | bytes 184328 | tf_op jit(solution)/shard_map/ppermute | solution.py:487
  12.5 31.1 %copy-start.1 = (bf16[256,512]{1,0:T(8,128)(2,1)S(1)}, bf16[256,512]{1,0:T(8,128)(2,1)}, u32[]{:S(2)}) copy-start(bf16[256,512]{1,0:T(8,128)(2,1)} %reduce.3) | copy-start | bytes 786436
  12.5 31.1 %copy-start.6 = (bf16[64,1728]{1,0:T(8,128)(2,1)S(1)}, bf16[64,1728]{1,0:T(8,128)(2,1)}, u32[]{:S(2)}) copy-start(bf16[64,1728]{1,0:T(8,128)(2,1)} %first.3) | copy-start | bytes 663556
  12.5 31.1 %copy-start.7 = (bf16[64,1728]{1,0:T(8,128)(2,1)S(1)}, bf16[64,1728]{1,0:T(8,128)(2,1)}, u32[]{:S(2)}) copy-start(bf16[64,1728]{1,0:T(8,128)(2,1)} %second.3) | copy-start | bytes 663556
  12.5 8.7 %collective-permute-start.6 = (bf16[32,1728]{1,0:T(8,128)(2,1)S(1)}, bf16[32,1728]{1,0:T(8,128)(2,1)S(1)}, u32[]{:S(2)}, u32[]{:S(2)}) collective-permute-start(bf16[32,1728]{1,0:T(8,128)(2,1)S(1)} %constant_dynamic-slice_fusion), channel_id=1, source_target_pairs={{0,0},{1,4},{2,8},{3,12},{4,1},{5,5},{6,9},{7,13},{8,2},{9,6},{10,... | collective-permute-start | bytes 331784 | tf_op jit(solution)/shard_map/ppermute | solution.py:567
  16.1 1.4 %collective-permute-start.4 = (bf16[20,4,640]{2,1,0:T(4,128)(2,1)S(1)}, bf16[20,4,640]{2,1,0:T(4,128)(2,1)S(1)}, u32[]{:S(2)}, u32[]{:S(2)}) collective-permute-start(bf16[20,4,640]{2,1,0:T(4,128)(2,1)S(1)} %get-tuple-element.54), channel_id=1, source_target_pairs={{0,16},{16,0},{1,17},{17,1},{2,18},{18,2},{3,19},{19,3},{4,20},{20... | collective-permute-start | bytes 307208 | tf_op jit(solution)/shard_map/ppermute | solution.py:487
  16.2 1.4 %collective-permute-start.5 = (bf16[20,4,640]{2,1,0:T(4,128)(2,1)S(1)}, bf16[20,4,640]{2,1,0:T(4,128)(2,1)S(1)}, u32[]{:S(2)}, u32[]{:S(2)}) collective-permute-start(bf16[20,4,640]{2,1,0:T(4,128)(2,1)S(1)} %get-tuple-element.53), channel_id=1, source_target_pairs={{0,16},{16,0},{1,17},{17,1},{2,18},{18,2},{3,19},{19,3},{4,20},{20... | collective-permute-start | bytes 307208 | tf_op jit(solution)/shard_map/ppermute | solution.py:487
  21.3 36.1 %copy-start.2 = (bf16[256,512]{1,0:T(8,128)(2,1)S(1)}, bf16[256,512]{1,0:T(8,128)(2,1)}, u32[]{:S(2)}) copy-start(bf16[256,512]{1,0:T(8,128)(2,1)} %up.1) | copy-start | bytes 786436
  21.3 36.1 %copy-start.3 = (bf16[64,1728]{1,0:T(8,128)(2,1)S(1)}, bf16[64,1728]{1,0:T(8,128)(2,1)}, u32[]{:S(2)}) copy-start(bf16[64,1728]{1,0:T(8,128)(2,1)} %bottom.2) | copy-start | bytes 663556
  21.3 36.1 %copy-start.4 = (bf16[64,1728]{1,0:T(8,128)(2,1)S(1)}, bf16[64,1728]{1,0:T(8,128)(2,1)}, u32[]{:S(2)}) copy-start(bf16[64,1728]{1,0:T(8,128)(2,1)} %m1.1) | copy-start | bytes 663556
  21.3 36.1 %copy-start.5 = (bf16[64,1728]{1,0:T(8,128)(2,1)S(1)}, bf16[64,1728]{1,0:T(8,128)(2,1)}, u32[]{:S(2)}) copy-start(bf16[64,1728]{1,0:T(8,128)(2,1)} %m2.1) | copy-start | bytes 663556
  21.3 36.1 %copy-start.10 = (bf16[32,864]{1,0:T(8,128)(2,1)S(1)}, bf16[32,864]{1,0:T(8,128)(2,1)}, u32[]{:S(2)}) copy-start(bf16[32,864]{1,0:T(8,128)(2,1)} %f1.1) | copy-start | bytes 165892
  21.3 36.1 %copy-start.11 = (bf16[32,864]{1,0:T(8,128)(2,1)S(1)}, bf16[32,864]{1,0:T(8,128)(2,1)}, u32[]{:S(2)}) copy-start(bf16[32,864]{1,0:T(8,128)(2,1)} %f2.1) | copy-start | bytes 165892
  21.3 36.0 %copy-start.12 = (bf16[64,256]{1,0:T(8,128)(2,1)S(1)}, bf16[64,256]{1,0:T(8,128)(2,1)}, u32[]{:S(2)}) copy-start(bf16[64,256]{1,0:T(8,128)(2,1)} %up_fine.1) | copy-start | bytes 98308
  43.1 1.8 %collective-permute-start.7 = (bf16[16,112,128]{2,1,0:T(8,128)(2,1)S(1)}, bf16[16,112,128]{2,1,0:T(8,128)(2,1)S(1)}, u32[]{:S(2)}, u32[]{:S(2)}) collective-permute-start(bf16[16,112,128]{2,1,0:T(8,128)(2,1)S(1)} %all_to_all.10.own), channel_id=1, source_target_pairs={{0,16},{16,0},{1,17},{17,1},{2,18},{18,2},{3,19},{19,3},{4,20},{20... | collective-permute-start | bytes 1376264 | tf_op jit(solution)/shard_map/ppermute | solution.py:603
  43.1 8.0 %collective-permute-start.9 = (bf16[32,1728]{1,0:T(8,128)(2,1)S(1)}, bf16[32,1728]{1,0:T(8,128)(2,1)S(1)}, u32[]{:S(2)}, u32[]{:S(2)}) collective-permute-start(bf16[32,1728]{1,0:T(8,128)(2,1)S(1)} %collective-permute-done.6.turned), channel_id=1, source_target_pairs={{0,16},{16,0},{1,17},{17,1},{2,18},{18,2},{3,19},{19,3},{4,20},{20... | collective-permute-start | bytes 331784 | tf_op jit(solution)/shard_map/ppermute | solution.py:601
  50.8 1.3 %collective-permute-start.8 = (bf16[36,768]{1,0:T(8,128)(2,1)S(1)}, bf16[36,768]{1,0:T(8,128)(2,1)S(1)}, u32[]{:S(2)}, u32[]{:S(2)}) collective-permute-start(bf16[36,768]{1,0:T(8,128)(2,1)S(1)} %get-tuple-element.36.near), channel_id=1, source_target_pairs={{0,16},{16,0},{1,17},{17,1},{2,18},{18,2},{3,19},{19,3},{4,20},{20... | collective-permute-start | bytes 165896 | tf_op jit(solution)/shard_map/ppermute | solution.py:625
  53.6 9.8 %collective-permute-start.13 = (bf16[12,16,896]{2,1,0:T(8,128)(2,1)S(1)}, bf16[12,16,896]{2,1,0:T(8,128)(2,1)S(1)}, u32[]{:S(2)}, u32[]{:S(2)}) collective-permute-start(bf16[12,16,896]{2,1,0:T(8,128)(2,1)S(1)} %get-tuple-element.41.window), channel_id=1, source_target_pairs={{0,16},{16,0},{1,17},{17,1},{2,18},{18,2},{3,19},{19,3},{4,20},{20... | collective-permute-start | bytes 1032200 | tf_op jit(solution)/shard_map/ppermute | solution.py:642
  53.9 5.9 %collective-permute-start.10 = (bf16[72,768]{1,0:T(8,128)(2,1)S(1)}, bf16[72,768]{1,0:T(8,128)(2,1)S(1)}, u32[]{:S(2)}, u32[]{:S(2)}) collective-permute-start(bf16[72,768]{1,0:T(8,128)(2,1)S(1)} %bottom_start.1.refs_0_), channel_id=1, source_target_pairs={{0,1},{1,0},{2,3},{3,2},{4,5},{5,4},{6,7},{7,6},{8,9},{9,8},{10,11... | collective-permute-start | bytes 331784 | tf_op jit(solution)/shard_map/ppermute | solution.py:645
  54.4 5.6 %collective-permute-start.11 = (bf16[72,768]{1,0:T(8,128)(2,1)S(1)}, bf16[72,768]{1,0:T(8,128)(2,1)S(1)}, u32[]{:S(2)}, u32[]{:S(2)}) collective-permute-start(bf16[72,768]{1,0:T(8,128)(2,1)S(1)} %bottom_start.1.refs_0_), channel_id=1, source_target_pairs={{0,2},{1,3},{2,0},{3,1},{4,6},{5,7},{6,4},{7,5},{8,10},{9,11},{10,... | collective-permute-start | bytes 331784 | tf_op jit(solution)/shard_map/ppermute | solution.py:645
  55.3 6.6 %collective-permute-start.12 = (bf16[72,768]{1,0:T(8,128)(2,1)S(1)}, bf16[72,768]{1,0:T(8,128)(2,1)S(1)}, u32[]{:S(2)}, u32[]{:S(2)}) collective-permute-start(bf16[72,768]{1,0:T(8,128)(2,1)S(1)} %bottom_start.1.refs_0_), channel_id=1, source_target_pairs={{0,3},{1,2},{2,1},{3,0},{4,7},{5,6},{6,5},{7,4},{8,11},{9,10},{10,... | collective-permute-start | bytes 331784 | tf_op jit(solution)/shard_map/ppermute | solution.py:645
  79.2 1.7 %collective-permute-start.14 = (bf16[16,88,128]{2,1,0:T(8,128)(2,1)S(1)}, bf16[16,88,128]{2,1,0:T(8,128)(2,1)S(1)}, u32[]{:S(2)}, u32[]{:S(2)}) collective-permute-start(bf16[16,88,128]{2,1,0:T(8,128)(2,1)S(1)} %all_to_all.11.near), channel_id=1, source_target_pairs={{0,16},{16,0},{1,17},{17,1},{2,18},{18,2},{3,19},{19,3},{4,20},{20... | collective-permute-start | bytes 1081352 | tf_op jit(solution)/shard_map/ppermute | solution.py:662

commit v5 on v4

--- a/solution.py
+++ b/solution.py
@@ -95,6 +95,10 @@
     pair = dot(left[: height + rows], right[:, : 2 * LANES])
     last = dot(left[2 * rows :], right[:, 2 * LANES :])
     return pair[:height, :LANES] + pair[rows:, LANES:] + last
+
+
+def relu(value):
+    return jnp.maximum(value, 0.0)
 
 
 def rounded_relu(value):
@@ -168,8 +172,8 @@
     tiles = width // LANES
     for tile in range(tiles):
         depth = DEPTH if tile + 1 < tiles else LANES
-        value = rounded_relu(convolve(s1, first_table, inner, 32, tile, depth))
-        wide[:inner, :32, span_of(tile)] = value.astype(F32).reshape(inner, 32, LANES)
+        value = relu(convolve(s1, first_table, inner, 32, tile, depth))
+        wide[:inner, :32, span_of(tile)] = value.reshape(inner, 32, LANES)
     stage(wide, s2, inner, 16, 0, width)
     kept = inner - 2
     for tile in range(tiles - 1):
@@ -224,7 +228,7 @@
     span = across * lanes
     place, core = lax.axis_index("yz"), lax.axis_index("gx")
     row, column = place // across, place % across
-    layers = 3 * side
+    layers = 3 * side - 1
     for k in range(3):
         i = (row + across // 2 * core + k + across - 1) % across
         for spot, j in enumerate([across - 1] + list(range(across))):
@@ -232,7 +236,7 @@
             size = min(lanes, span + LANES - start)
             for part, gathered in enumerate((own, other)):
                 block = gathered[i * across + j].astype(F32)
-                for y in range(side):
+                for y in range(min(side, layers - side * k)):
                     for tile in range(size // LANES):
                         first = side * (side * tile + y)
                         wide[
@@ -244,8 +248,8 @@
     stage(wide, s, layers, 16, 7, span + LANES)
     layers -= 2
     for tile in range(span // LANES):
-        value = rounded_relu(convolve(s, first_table, layers, 16, tile))
-        wide[:layers, 8:24, span_of(tile)] = value.astype(F32).reshape(layers, 16, LANES)
+        value = relu(convolve(s, first_table, layers, 16, tile))
+        wide[:layers, 8:24, span_of(tile)] = value.reshape(layers, 16, LANES)
     wide[:layers, :, span : span + LANES] = wide[:layers, :, 0:LANES]
     wrap_x(wide, layers, 2 * side)
     stage(wide, s, layers, 16, 7, span + LANES)
@@ -327,7 +331,7 @@
     total = 0.0
     for piece in pieces:
         total = total + piece[...].astype(F32)
-    total = jnp.maximum(total, 0.0).astype(BF).astype(F32)
+    total = relu(total)
     for y in range(cells):
         wide[1 + y, 8 : 8 + side, :span] = total[side * y : side * (y + 1)]
     wide[1 : cells + 1, 8 : 8 + side, span : span + LANES] = wide[
@@ -424,15 +428,15 @@
             is_first, window[:, :, span_of(tile)].astype(F32), wide[:count, 8:24, span_of(tile)]
         )
         total = spread[tile, 1 : count + 1, 8:24, :] + kept_here
-        wide[:count, 8:24, span_of(tile)] = total.astype(BF).astype(F32)
+        wide[:count, 8:24, span_of(tile)] = total
     ends = 8 + count
     wide[:, 7:8, :] = wide[:, ends - 1 : ends, :]
     wide[:, ends : ends + 1, :] = wide[:, 8:9, :]
     stage(wide, s, count, 16, 7, window.shape[2])
     count = count - 2
     for tile in range(6):
-        value = rounded_relu(convolve(s, m1_table, count, 16, tile))
-        wide[:count, 8:24, span_of(tile)] = value.astype(F32).reshape(count, 16, LANES)
+        value = relu(convolve(s, m1_table, count, 16, tile))
+        wide[:count, 8:24, span_of(tile)] = value.reshape(count, 16, LANES)
     wide[:, 7:8, :] = wide[:, ends - 1 : ends, :]
     wide[:, ends : ends + 1, :] = wide[:, 8:9, :]
     stage(wide, s, count, 16, 7, 6 * LANES)
@@ -452,12 +456,12 @@
     count = 2 * count
     for tile in range(skip.shape[2] // LANES):
         total = spread[tile, :count, 0:16, :] + skip[:, :, span_of(tile)].astype(F32)
-        wide[:count, 0:16, span_of(tile)] = total.astype(BF).astype(F32)
+        wide[:count, 0:16, span_of(tile)] = total
     stage(wide, s, count, 16, 0, 4 * LANES)
     count = count - 2
     for tile in range(4):
-        value = rounded_relu(convolve(s, f1_table, count, 16, tile, DEPTH if tile < 3 else LANES))
-        wide[:count, 0:16, span_of(tile)] = value.astype(F32).reshape(count, 16, LANES)
+        value = relu(convolve(s, f1_table, count, 16, tile, DEPTH if tile < 3 else LANES))
+        wide[:count, 0:16, span_of(tile)] = value.reshape(count, 16, LANES)
     stage(wide, s, count, 16, 0, 4 * LANES)
     count = count - 2
     for tile in range(3):
@@ -614,7 +618,7 @@
         [
             pltpu.VMEM((3 * side, 32, span + LANES), F32),
             pltpu.VMEM((3, 3 * side * 16, span + LANES), BF),
-            pltpu.VMEM((3 * side - 4, 16, span + 512), BF),
+            pltpu.VMEM((3 * side - 5, 16, span + 512), BF),
             pltpu.VMEM((2, side * 16, LANES), F32),
             pltpu.VMEM((side * side, half * mid), F32),
         ],

time: 87.6 us -> 87.2 us (level)
  transfers between devices with their start and end apart: 15 -> 15, of which waited for: 12 -> 12; matrix products, arithmetic and copies ran while one was open for 1% -> 1% of each run, Pallas kernels for 16% -> 15%
where the time goes in v5:
time: 87.2 us; the launch traced here: 87 us
  blocking collectives  37.5 us (43%)
  Pallas kernels  19.4 us (22%)
  starting transfers between devices  14 us (16%)
  waiting for transfers between devices  11.6 us (13%)
  local copies, waits for them, and re-layouts  4.13 us (5%)
    all_to_all x1, blocking collectives, gathered_body(): own = lax.all_to_all(small, 'yz', 0, 0)  21.7 us
    pallas_call x8, Pallas kernels, call(): pl.pallas_call(kernel, out_shape=jax.tree.map(lambda out: pltpu.VMEM(out....  19.4 us
    all_to_all x1, blocking collectives, gathered_body(): near = lax.all_to_all(sent, 'yz', 0, 0)  15.8 us
    ppermute x6, starting transfers between devices, exchange(): return (lax.ppermute(tail, axis, ahead), lax.ppermute(head, axis, back))  8.74 us
    ppermute x6, waiting for transfers between devices, exchange(): return (lax.ppermute(tail, axis, ahead), lax.ppermute(head, axis, back))  5.09 us
    ppermute x3, starting transfers between devices, gathered_body(): lax.ppermute(partial, 'yz', [(s, s ^ turn) for s in range(devices)])  3.49 us
    ppermute x3, waiting for transfers between devices, gathered_body(): lax.ppermute(partial, 'yz', [(s, s ^ turn) for s in range(devices)])  2.98 us
  transfers between devices with their start and end apart: 15, of which 12 were waited for; matrix products, arithmetic and copies ran while one was open for 1% of the time, Pallas kernels for 15%

profile of v5, /device:TPU:0, one launch (start us, length us, event | category | flops | bytes accessed | tf_op | source)
XLA Modules:
  0.0 87.0 jit_solution(3658162583983379523)
XLA Ops:
  0.0 1.2 %copy.18 = bf16[1,32,12,144]{1,3,2,0:T(8,128)(2,1)S(1)} copy(bf16[1,32,12,144]{3,1,2,0:T(8,128)(2,1)} %param.15) | data formatting | bytes 221184 | tf_op args[0]
  1.2 0.1 reshape.14
  1.4 0.0 copy-start.8
  1.4 0.0 copy-start.9
  1.4 0.0 copy-start.13
  1.5 0.2 slice.28
  1.6 3.1 %collective-permute-start = (bf16[4,12,384]{2,1,0:T(8,128)(2,1)S(1)}, bf16[4,12,384]{2,1,0:T(8,128)(2,1)S(1)}, u32[]{:S(2)}, u32[]{:S(2)}) collective-permute-start(bf16[4,12,384]{2,1,0:T(8,128)(2,1)S(1)} %copy.19), channel_id=1, source_target_pairs={{0,4},{1,5},{2,6},{3,7},{4,8},{5,9},{6,10},{7,11},{8,12},{9,13},{1... | collective-permute-start | bytes 110600 | tf_op jit(solution)/shard_map/ppermute | solution.py:491
  4.7 0.2 slice.30
  4.9 2.1 %collective-permute-start.1 = (bf16[4,12,384]{2,1,0:T(8,128)(2,1)S(1)}, bf16[4,12,384]{2,1,0:T(8,128)(2,1)S(1)}, u32[]{:S(2)}, u32[]{:S(2)}) collective-permute-start(bf16[4,12,384]{2,1,0:T(8,128)(2,1)S(1)} %copy.21), channel_id=1, source_target_pairs={{0,12},{1,13},{2,14},{3,15},{4,0},{5,1},{6,2},{7,3},{8,4},{9,5},{1... | collective-permute-start | bytes 110600 | tf_op jit(solution)/shard_map/ppermute | solution.py:491
  7.0 0.4 reshape.18
  7.5 1.5 %collective-permute-done = bf16[4,12,384]{2,1,0:T(8,128)(2,1)S(1)} collective-permute-done((bf16[4,12,384]{2,1,0:T(8,128)(2,1)S(1)}, bf16[4,12,384]{2,1,0:T(8,128)(2,1)S(1)}, u32[]{:S(2)}, u32[]{:S(2)}) %collective-permute-start) | collective-permute-done | bytes 36896 | tf_op jit(solution)/shard_map/ppermute | solution.py:491
  9.0 0.5 collective-permute-done.1
  9.5 1.7 %collective-permute-start.2 = (bf16[20,12,128]{2,1,0:T(8,128)(2,1)S(1)}, bf16[20,12,128]{2,1,0:T(8,128)(2,1)S(1)}, u32[]{:S(2)}, u32[]{:S(2)}) collective-permute-start(bf16[20,12,128]{2,1,0:T(8,128)(2,1)S(1)} %get-tuple-element.55), channel_id=1, source_target_pairs={{0,1},{1,2},{2,3},{3,0},{4,5},{5,6},{6,7},{7,4},{8,9},{9,10},{10,1... | collective-permute-start | bytes 184328 | tf_op jit(solution)/shard_map/ppermute | solution.py:491
  11.2 1.3 %collective-permute-start.3 = (bf16[20,12,128]{2,1,0:T(8,128)(2,1)S(1)}, bf16[20,12,128]{2,1,0:T(8,128)(2,1)S(1)}, u32[]{:S(2)}, u32[]{:S(2)}) collective-permute-start(bf16[20,12,128]{2,1,0:T(8,128)(2,1)S(1)} %get-tuple-element.56), channel_id=1, source_target_pairs={{0,3},{1,0},{2,1},{3,2},{4,7},{5,4},{6,5},{7,6},{8,11},{9,8},{10,9... | collective-permute-start | bytes 184328 | tf_op jit(solution)/shard_map/ppermute | solution.py:491
  12.5 0.0 copy-start.1
  12.5 0.0 copy-start.6
  12.5 0.0 copy-start.7
  12.5 0.8 collective-permute-start.6
  13.4 1.6 %collective-permute-done.2 = bf16[20,12,128]{2,1,0:T(8,128)(2,1)S(1)} collective-permute-done((bf16[20,12,128]{2,1,0:T(8,128)(2,1)S(1)}, bf16[20,12,128]{2,1,0:T(8,128)(2,1)S(1)}, u32[]{:S(2)}, u32[]{:S(2)}) %collective-permute-start.2) | collective-permute-done | bytes 61472 | tf_op jit(solution)/shard_map/ppermute | solution.py:491
  14.9 1.0 %collective-permute-done.3 = bf16[20,12,128]{2,1,0:T(8,128)(2,1)S(1)} collective-permute-done((bf16[20,12,128]{2,1,0:T(8,128)(2,1)S(1)}, bf16[20,12,128]{2,1,0:T(8,128)(2,1)S(1)}, u32[]{:S(2)}, u32[]{:S(2)}) %collective-permute-start.3) | collective-permute-done | bytes 61472 | tf_op jit(solution)/shard_map/ppermute | solution.py:491
  16.0 0.1 pad_maximum_fusion.mid
  16.0 0.1 fusion.1
  16.1 0.1 collective-permute-start.4
  16.2 0.5 collective-permute-start.5
  16.7 0.4 fine_tables.1
  17.1 0.4 collective-permute-done.4.low
  17.5 0.2 collective-permute-done.5.high
  17.6 3.7 %fine_encoder.1 = (bf16[16,16,512]{2,1,0:T(8,128)(2,1)S(1)}, bf16[16,112,128]{2,1,0:T(8,128)(2,1)S(1)}) custom-call(bf16[20,4,640]{2,1,0:T(4,128)(2,1)S(1)} %collective-permute-done.4.low, bf16[20,12,640]{2,1,0:T(8,128)(2,1)S(1)} %pad_maximum_fusion.mid, bf16[20,4,640]{2,1,0:T(4,128)(2,1)S(1)} %collective-permute-done.5.high, ...), custom_call_target="tpu_custom_call" | custom-call | tf_op jit(solution)/shard_map/fine_encoder/pallas_call | solution.py:473
  21.3 0.0 collective-permute-done.6.turned
  21.3 0.0 copy-start.2
  21.3 0.0 copy-start.3
  21.3 0.0 copy-start.4
  21.3 0.0 copy-start.5
  21.3 0.0 copy-start.10
  21.3 0.0 copy-start.11
  21.4 0.0 copy-start.12
  21.4 21.7 %all_to_all.10.own = bf16[16,112,128]{2,1,0:T(8,128)(2,1)S(1)} all-to-all(bf16[16,112,128]{2,1,0:T(8,128)(2,1)S(1)} %get-tuple-element.32), channel_id=1, replica_groups=mesh['gx'=2,'yz'=16] {'yz'}, dimensions={0} | all-to-all | bytes 917504 | tf_op jit(solution)/shard_map/all_to_all | solution.py:606
  43.1 0.0 collective-permute-start.7
  43.1 0.5 collective-permute-start.9
  43.6 0.5 middle_tables.1
  44.2 0.7 collective-permute-done.7.other
  44.9 5.6 %middle.1 = (bf16[12,16,896]{2,1,0:T(8,128)(2,1)S(1)}, bf16[36,768]{1,0:T(8,128)(2,1)S(1)}) custom-call(bf16[16,112,128]{2,1,0:T(8,128)(2,1)S(1)} %all_to_all.10.own, bf16[16,112,128]{2,1,0:T(8,128)(2,1)S(1)} %collective-permute-done.7.other, bf16[768,384]{1,0:T(8,128)(2,1)S(1)} %get-tuple-element.33.first_table, ...), custom_call_target="tpu_custom_call" | custom-call | tf_op jit(solution)/shard_map/middle/pallas_call | solution.py:473
  50.5 0.2 collective-permute-start.8
  50.7 0.0 collective-permute-done.9.swapped
  50.7 1.1 %collective-permute-done.8.far = bf16[36,768]{1,0:T(8,128)(2,1)S(1)} collective-permute-done((bf16[36,768]{1,0:T(8,128)(2,1)S(1)}, bf16[36,768]{1,0:T(8,128)(2,1)S(1)}, u32[]{:S(2)}, u32[]{:S(2)}) %collective-permute-start.8) | collective-permute-done | bytes 55328 | tf_op jit(solution)/shard_map/ppermute | solution.py:629
  51.8 1.5 %bottom_start.1.refs_0_ = bf16[72,768]{1,0:T(8,128)(2,1)S(1)} custom-call(bf16[36,768]{1,0:T(8,128)(2,1)S(1)} %get-tuple-element.36.near, bf16[36,768]{1,0:T(8,128)(2,1)S(1)} %collective-permute-done.8.far, bf16[32,1728]{1,0:T(8,128)(2,1)S(1)} %collective-permute-done.6.turned, bf16[32,1728]{1,0:T(8,128)(2,1)S(1)} %collective-permute-done.9.swapped), custom_call_target="tpu_custom_call" | custom-call | tf_op jit(solution)/shard_map/bottom_start/pallas_call | solution.py:473
  53.3 0.2 collective-permute-start.13
  53.5 0.6 collective-permute-start.10
  54.1 0.9 %collective-permute-start.11 = (bf16[72,768]{1,0:T(8,128)(2,1)S(1)}, bf16[72,768]{1,0:T(8,128)(2,1)S(1)}, u32[]{:S(2)}, u32[]{:S(2)}) collective-permute-start(bf16[72,768]{1,0:T(8,128)(2,1)S(1)} %bottom_start.1.refs_0_), channel_id=1, source_target_pairs={{0,2},{1,3},{2,0},{3,1},{4,6},{5,7},{6,4},{7,5},{8,10},{9,11},{10,... | collective-permute-start | bytes 331784 | tf_op jit(solution)/shard_map/ppermute | solution.py:649
  54.9 2.1 %collective-permute-start.12 = (bf16[72,768]{1,0:T(8,128)(2,1)S(1)}, bf16[72,768]{1,0:T(8,128)(2,1)S(1)}, u32[]{:S(2)}, u32[]{:S(2)}) collective-permute-start(bf16[72,768]{1,0:T(8,128)(2,1)S(1)} %bottom_start.1.refs_0_), channel_id=1, source_target_pairs={{0,3},{1,2},{2,1},{3,0},{4,7},{5,6},{6,5},{7,4},{8,11},{9,10},{10,... | collective-permute-start | bytes 331784 | tf_op jit(solution)/shard_map/ppermute | solution.py:649
  57.0 1.5 %decoder_tables.1 = (bf16[768,384]{1,0:T(8,128)(2,1)S(1)}, bf16[4,1024,256]{2,1,0:T(8,128)(2,1)S(1)}, bf16[768,384]{1,0:T(8,128)(2,1)S(1)}, bf16[768,384]{1,0:T(...) custom-call(bf16[64,1728]{1,0:T(8,128)(2,1)S(1)} %copy-done.3, ...), custom_call_target="tpu_custom_call" | custom-call | tf_op jit(solution)/shard_map/decoder_tables/pallas_call | solution.py:473
  58.5 0.9 %collective-permute-done.10.refs_1_ = bf16[72,768]{1,0:T(8,128)(2,1)S(1)} collective-permute-done((bf16[72,768]{1,0:T(8,128)(2,1)S(1)}, bf16[72,768]{1,0:T(8,128)(2,1)S(1)}, u32[]{:S(2)}, u32[]{:S(2)}) %collective-permute-start.10) | collective-permute-done | bytes 110624 | tf_op jit(solution)/shard_map/ppermute | solution.py:649
  59.4 0.3 collective-permute-done.11.refs_2_
  59.7 1.8 %collective-permute-done.12.refs_3_ = bf16[72,768]{1,0:T(8,128)(2,1)S(1)} collective-permute-done((bf16[72,768]{1,0:T(8,128)(2,1)S(1)}, bf16[72,768]{1,0:T(8,128)(2,1)S(1)}, u32[]{:S(2)}, u32[]{:S(2)}) %collective-permute-start.12) | collective-permute-done | bytes 110624 | tf_op jit(solution)/shard_map/ppermute | solution.py:649
  61.5 1.5 %bottom.3 = bf16[16,88,128]{2,1,0:T(8,128)(2,1)S(1)} custom-call(bf16[72,768]{1,0:T(8,128)(2,1)S(1)} %bottom_start.1.refs_0_, bf16[72,768]{1,0:T(8,128)(2,1)S(1)} %collective-permute-done.10.refs_1_, bf16[72,768]{1,0:T(8,128)(2,1)S(1)} %collective-permute-done.11.refs_2_, bf16[72,768]{1,0:T(8,128)(2,1)S(1)} %collective-permute-done.12.refs_3_, ...), custom_call_target="tpu_custom_call" | custom-call | tf_op jit(solution)/shard_map/bottom/pallas_call | solution.py:473
  63.0 0.0 collective-permute-done.13.far_window
  63.1 15.8 %all_to_all.11.near = bf16[16,88,128]{2,1,0:T(8,128)(2,1)S(1)} all-to-all(bf16[16,88,128]{2,1,0:T(8,128)(2,1)S(1)} %bottom.3), channel_id=1, replica_groups=mesh['gx'=2,'yz'=16] {'yz'}, dimensions={0} | all-to-all | bytes 720896 | tf_op jit(solution)/shard_map/all_to_all | solution.py:665
  78.8 0.0 collective-permute-start.14
  78.8 1.7 %collective-permute-done.14.far = bf16[16,88,128]{2,1,0:T(8,128)(2,1)S(1)} collective-permute-done((bf16[16,88,128]{2,1,0:T(8,128)(2,1)S(1)}, bf16[16,88,128]{2,1,0:T(8,128)(2,1)S(1)}, u32[]{:S(2)}, u32[]{:S(2)}) %collective-permute-start.14) | collective-permute-done | bytes 360480 | tf_op jit(solution)/shard_map/ppermute | solution.py:666
  80.5 4.7 %decoder.1 = bf16[12,16,384]{2,1,0:T(8,128)(2,1)S(1)} custom-call(bf16[16,88,128]{2,1,0:T(8,128)(2,1)S(1)} %all_to_all.11.near, bf16[16,88,128]{2,1,0:T(8,128)(2,1)S(1)} %collective-permute-done.14.far, bf16[12,16,896]{2,1,0:T(8,128)(2,1)S(1)} %get-tuple-element.41.window, bf16[12,16,896]{2,1,0:T(8,128)(2,1)S(1)} %collective-permute-done.13.far_window, ...), custom_call_target="tpu_custom_call" | custom-call | tf_op jit(solution)/shard_map/decoder/pallas_call | solution.py:473
  85.2 0.4 reshape.16
  85.7 0.1 copy.27
  85.8 0.2 reshape.17
  86.1 0.9 %copy.23 = bf16[1,32,12,144]{3,1,2,0:T(8,128)(2,1)} copy(bf16[1,32,12,144]{1,3,2,0:T(8,128)(2,1)S(1)} %reshape.17) | data formatting | bytes 221184 | tf_op jit(solution)/shard_map/reshape | solution.py:685
  (23 shorter events, 0.2 us)
Async XLA Ops:
  0.0 12.5 %copy-start = (bf16[64,1728]{1,0:T(8,128)(2,1)S(1)}, bf16[64,1728]{1,0:T(8,128)(2,1)}, u32[]{:S(2)}) copy-start(bf16[64,1728]{1,0:T(8,128)(2,1)} %param.22) | copy-start | bytes 663556
  1.4 15.3 %copy-start.8 = (bf16[32,864]{1,0:T(8,128)(2,1)S(1)}, bf16[32,864]{1,0:T(8,128)(2,1)}, u32[]{:S(2)}) copy-start(bf16[32,864]{1,0:T(8,128)(2,1)} %first.2) | copy-start | bytes 165892
  1.4 15.3 %copy-start.9 = (bf16[32,864]{1,0:T(8,128)(2,1)S(1)}, bf16[32,864]{1,0:T(8,128)(2,1)}, u32[]{:S(2)}) copy-start(bf16[32,864]{1,0:T(8,128)(2,1)} %second.2) | copy-start | bytes 165892
  1.4 15.3 %copy-start.13 = (bf16[64,256]{1,0:T(8,128)(2,1)S(1)}, bf16[64,256]{1,0:T(8,128)(2,1)}, u32[]{:S(2)}) copy-start(bf16[64,256]{1,0:T(8,128)(2,1)} %reduce.2) | copy-start | bytes 98308
  1.6 7.3 %collective-permute-start = (bf16[4,12,384]{2,1,0:T(8,128)(2,1)S(1)}, bf16[4,12,384]{2,1,0:T(8,128)(2,1)S(1)}, u32[]{:S(2)}, u32[]{:S(2)}) collective-permute-start(bf16[4,12,384]{2,1,0:T(8,128)(2,1)S(1)} %copy.19), channel_id=1, source_target_pairs={{0,4},{1,5},{2,6},{3,7},{4,8},{5,9},{6,10},{7,11},{8,12},{9,13},{1... | collective-permute-start | bytes 110600 | tf_op jit(solution)/shard_map/ppermute | solution.py:491
  4.9 4.5 %collective-permute-start.1 = (bf16[4,12,384]{2,1,0:T(8,128)(2,1)S(1)}, bf16[4,12,384]{2,1,0:T(8,128)(2,1)S(1)}, u32[]{:S(2)}, u32[]{:S(2)}) collective-permute-start(bf16[4,12,384]{2,1,0:T(8,128)(2,1)S(1)} %copy.21), channel_id=1, source_target_pairs={{0,12},{1,13},{2,14},{3,15},{4,0},{5,1},{6,2},{7,3},{8,4},{9,5},{1... | collective-permute-start | bytes 110600 | tf_op jit(solution)/shard_map/ppermute | solution.py:491
  9.5 5.4 %collective-permute-start.2 = (bf16[20,12,128]{2,1,0:T(8,128)(2,1)S(1)}, bf16[20,12,128]{2,1,0:T(8,128)(2,1)S(1)}, u32[]{:S(2)}, u32[]{:S(2)}) collective-permute-start(bf16[20,12,128]{2,1,0:T(8,128)(2,1)S(1)} %get-tuple-element.55), channel_id=1, source_target_pairs={{0,1},{1,2},{2,3},{3,0},{4,5},{5,6},{6,7},{7,4},{8,9},{9,10},{10,1... | collective-permute-start | bytes 184328 | tf_op jit(solution)/shard_map/ppermute | solution.py:491
  11.2 4.8 %collective-permute-start.3 = (bf16[20,12,128]{2,1,0:T(8,128)(2,1)S(1)}, bf16[20,12,128]{2,1,0:T(8,128)(2,1)S(1)}, u32[]{:S(2)}, u32[]{:S(2)}) collective-permute-start(bf16[20,12,128]{2,1,0:T(8,128)(2,1)S(1)} %get-tuple-element.56), channel_id=1, source_target_pairs={{0,3},{1,0},{2,1},{3,2},{4,7},{5,4},{6,5},{7,6},{8,11},{9,8},{10,9... | collective-permute-start | bytes 184328 | tf_op jit(solution)/shard_map/ppermute | solution.py:491
  12.5 31.1 %copy-start.1 = (bf16[256,512]{1,0:T(8,128)(2,1)S(1)}, bf16[256,512]{1,0:T(8,128)(2,1)}, u32[]{:S(2)}) copy-start(bf16[256,512]{1,0:T(8,128)(2,1)} %reduce.3) | copy-start | bytes 786436
  12.5 31.1 %copy-start.6 = (bf16[64,1728]{1,0:T(8,128)(2,1)S(1)}, bf16[64,1728]{1,0:T(8,128)(2,1)}, u32[]{:S(2)}) copy-start(bf16[64,1728]{1,0:T(8,128)(2,1)} %first.3) | copy-start | bytes 663556
  12.5 31.1 %copy-start.7 = (bf16[64,1728]{1,0:T(8,128)(2,1)S(1)}, bf16[64,1728]{1,0:T(8,128)(2,1)}, u32[]{:S(2)}) copy-start(bf16[64,1728]{1,0:T(8,128)(2,1)} %second.3) | copy-start | bytes 663556
  12.5 8.7 %collective-permute-start.6 = (bf16[32,1728]{1,0:T(8,128)(2,1)S(1)}, bf16[32,1728]{1,0:T(8,128)(2,1)S(1)}, u32[]{:S(2)}, u32[]{:S(2)}) collective-permute-start(bf16[32,1728]{1,0:T(8,128)(2,1)S(1)} %constant_dynamic-slice_fusion), channel_id=1, source_target_pairs={{0,0},{1,4},{2,8},{3,12},{4,1},{5,5},{6,9},{7,13},{8,2},{9,6},{10,... | collective-permute-start | bytes 331784 | tf_op jit(solution)/shard_map/ppermute | solution.py:571
  16.1 1.4 %collective-permute-start.4 = (bf16[20,4,640]{2,1,0:T(4,128)(2,1)S(1)}, bf16[20,4,640]{2,1,0:T(4,128)(2,1)S(1)}, u32[]{:S(2)}, u32[]{:S(2)}) collective-permute-start(bf16[20,4,640]{2,1,0:T(4,128)(2,1)S(1)} %get-tuple-element.54), channel_id=1, source_target_pairs={{0,16},{16,0},{1,17},{17,1},{2,18},{18,2},{3,19},{19,3},{4,20},{20... | collective-permute-start | bytes 307208 | tf_op jit(solution)/shard_map/ppermute | solution.py:491
  16.2 1.4 %collective-permute-start.5 = (bf16[20,4,640]{2,1,0:T(4,128)(2,1)S(1)}, bf16[20,4,640]{2,1,0:T(4,128)(2,1)S(1)}, u32[]{:S(2)}, u32[]{:S(2)}) collective-permute-start(bf16[20,4,640]{2,1,0:T(4,128)(2,1)S(1)} %get-tuple-element.53), channel_id=1, source_target_pairs={{0,16},{16,0},{1,17},{17,1},{2,18},{18,2},{3,19},{19,3},{4,20},{20... | collective-permute-start | bytes 307208 | tf_op jit(solution)/shard_map/ppermute | solution.py:491
  21.3 35.7 %copy-start.2 = (bf16[256,512]{1,0:T(8,128)(2,1)S(1)}, bf16[256,512]{1,0:T(8,128)(2,1)}, u32[]{:S(2)}) copy-start(bf16[256,512]{1,0:T(8,128)(2,1)} %up.1) | copy-start | bytes 786436
  21.3 35.7 %copy-start.3 = (bf16[64,1728]{1,0:T(8,128)(2,1)S(1)}, bf16[64,1728]{1,0:T(8,128)(2,1)}, u32[]{:S(2)}) copy-start(bf16[64,1728]{1,0:T(8,128)(2,1)} %bottom.2) | copy-start | bytes 663556
  21.3 35.7 %copy-start.4 = (bf16[64,1728]{1,0:T(8,128)(2,1)S(1)}, bf16[64,1728]{1,0:T(8,128)(2,1)}, u32[]{:S(2)}) copy-start(bf16[64,1728]{1,0:T(8,128)(2,1)} %m1.1) | copy-start | bytes 663556
  21.3 35.7 %copy-start.5 = (bf16[64,1728]{1,0:T(8,128)(2,1)S(1)}, bf16[64,1728]{1,0:T(8,128)(2,1)}, u32[]{:S(2)}) copy-start(bf16[64,1728]{1,0:T(8,128)(2,1)} %m2.1) | copy-start | bytes 663556
  21.3 35.7 %copy-start.10 = (bf16[32,864]{1,0:T(8,128)(2,1)S(1)}, bf16[32,864]{1,0:T(8,128)(2,1)}, u32[]{:S(2)}) copy-start(bf16[32,864]{1,0:T(8,128)(2,1)} %f1.1) | copy-start | bytes 165892
  21.3 35.7 %copy-start.11 = (bf16[32,864]{1,0:T(8,128)(2,1)S(1)}, bf16[32,864]{1,0:T(8,128)(2,1)}, u32[]{:S(2)}) copy-start(bf16[32,864]{1,0:T(8,128)(2,1)} %f2.1) | copy-start | bytes 165892
  21.4 35.7 %copy-start.12 = (bf16[64,256]{1,0:T(8,128)(2,1)S(1)}, bf16[64,256]{1,0:T(8,128)(2,1)}, u32[]{:S(2)}) copy-start(bf16[64,256]{1,0:T(8,128)(2,1)} %up_fine.1) | copy-start | bytes 98308
  43.1 1.8 %collective-permute-start.7 = (bf16[16,112,128]{2,1,0:T(8,128)(2,1)S(1)}, bf16[16,112,128]{2,1,0:T(8,128)(2,1)S(1)}, u32[]{:S(2)}, u32[]{:S(2)}) collective-permute-start(bf16[16,112,128]{2,1,0:T(8,128)(2,1)S(1)} %all_to_all.10.own), channel_id=1, source_target_pairs={{0,16},{16,0},{1,17},{17,1},{2,18},{18,2},{3,19},{19,3},{4,20},{20... | collective-permute-start | bytes 1376264 | tf_op jit(solution)/shard_map/ppermute | solution.py:607
  43.1 7.6 %collective-permute-start.9 = (bf16[32,1728]{1,0:T(8,128)(2,1)S(1)}, bf16[32,1728]{1,0:T(8,128)(2,1)S(1)}, u32[]{:S(2)}, u32[]{:S(2)}) collective-permute-start(bf16[32,1728]{1,0:T(8,128)(2,1)S(1)} %collective-permute-done.6.turned), channel_id=1, source_target_pairs={{0,16},{16,0},{1,17},{17,1},{2,18},{18,2},{3,19},{19,3},{4,20},{20... | collective-permute-start | bytes 331784 | tf_op jit(solution)/shard_map/ppermute | solution.py:605
  50.5 1.3 %collective-permute-start.8 = (bf16[36,768]{1,0:T(8,128)(2,1)S(1)}, bf16[36,768]{1,0:T(8,128)(2,1)S(1)}, u32[]{:S(2)}, u32[]{:S(2)}) collective-permute-start(bf16[36,768]{1,0:T(8,128)(2,1)S(1)} %get-tuple-element.36.near), channel_id=1, source_target_pairs={{0,16},{16,0},{1,17},{17,1},{2,18},{18,2},{3,19},{19,3},{4,20},{20... | collective-permute-start | bytes 165896 | tf_op jit(solution)/shard_map/ppermute | solution.py:629
  53.3 9.8 %collective-permute-start.13 = (bf16[12,16,896]{2,1,0:T(8,128)(2,1)S(1)}, bf16[12,16,896]{2,1,0:T(8,128)(2,1)S(1)}, u32[]{:S(2)}, u32[]{:S(2)}) collective-permute-start(bf16[12,16,896]{2,1,0:T(8,128)(2,1)S(1)} %get-tuple-element.41.window), channel_id=1, source_target_pairs={{0,16},{16,0},{1,17},{17,1},{2,18},{18,2},{3,19},{19,3},{4,20},{20... | collective-permute-start | bytes 1032200 | tf_op jit(solution)/shard_map/ppermute | solution.py:646
  53.5 5.9 %collective-permute-start.10 = (bf16[72,768]{1,0:T(8,128)(2,1)S(1)}, bf16[72,768]{1,0:T(8,128)(2,1)S(1)}, u32[]{:S(2)}, u32[]{:S(2)}) collective-permute-start(bf16[72,768]{1,0:T(8,128)(2,1)S(1)} %bottom_start.1.refs_0_), channel_id=1, source_target_pairs={{0,1},{1,0},{2,3},{3,2},{4,5},{5,4},{6,7},{7,6},{8,9},{9,8},{10,11... | collective-permute-start | bytes 331784 | tf_op jit(solution)/shard_map/ppermute | solution.py:649
  54.1 5.6 %collective-permute-start.11 = (bf16[72,768]{1,0:T(8,128)(2,1)S(1)}, bf16[72,768]{1,0:T(8,128)(2,1)S(1)}, u32[]{:S(2)}, u32[]{:S(2)}) collective-permute-start(bf16[72,768]{1,0:T(8,128)(2,1)S(1)} %bottom_start.1.refs_0_), channel_id=1, source_target_pairs={{0,2},{1,3},{2,0},{3,1},{4,6},{5,7},{6,4},{7,5},{8,10},{9,11},{10,... | collective-permute-start | bytes 331784 | tf_op jit(solution)/shard_map/ppermute | solution.py:649
  54.9 6.5 %collective-permute-start.12 = (bf16[72,768]{1,0:T(8,128)(2,1)S(1)}, bf16[72,768]{1,0:T(8,128)(2,1)S(1)}, u32[]{:S(2)}, u32[]{:S(2)}) collective-permute-start(bf16[72,768]{1,0:T(8,128)(2,1)S(1)} %bottom_start.1.refs_0_), channel_id=1, source_target_pairs={{0,3},{1,2},{2,1},{3,0},{4,7},{5,6},{6,5},{7,4},{8,11},{9,10},{10,... | collective-permute-start | bytes 331784 | tf_op jit(solution)/shard_map/ppermute | solution.py:649
  78.8 1.7 %collective-permute-start.14 = (bf16[16,88,128]{2,1,0:T(8,128)(2,1)S(1)}, bf16[16,88,128]{2,1,0:T(8,128)(2,1)S(1)}, u32[]{:S(2)}, u32[]{:S(2)}) collective-permute-start(bf16[16,88,128]{2,1,0:T(8,128)(2,1)S(1)} %all_to_all.11.near), channel_id=1, source_target_pairs={{0,16},{16,0},{1,17},{17,1},{2,18},{18,2},{3,19},{19,3},{4,20},{20... | collective-permute-start | bytes 1081352 | tf_op jit(solution)/shard_map/ppermute | solution.py:666
